TPU v7x, 256 devices: a whole 4x4x8 slice. The times are simulated.
256 devices in a mesh: wide: 16 (over z_hi, x), narrow: 16 (over z_lo, y, core).
Axes of the slice: x: 4, y: 4, z: 8 (z_hi: 4, z_lo: 2; z = z_hi * 2 + z_lo), core: 2. Of those that a mesh axis runs over, the one named last changes fastest.
Arguments:
- node: bfloat16 [256, 256, 256], P('narrow'), may hold values from -6 to 6
- right_side: bfloat16 [256, 256, 256], P('narrow'), may hold values from -16 to 16
- leg_ops: bfloat16 [3, 12, 256, 256], replicated, may hold values from -0.375 to 0.375
- op_index: int32 [64, 3], P('wide'), may hold values from 0 to 11, as said below
- offsets: int32 [64], P('wide'), may hold values from 0 to 7
Outputs:
- new_node: float32 [256, 256, 256], P('narrow')
Inputs may be any that keep to these rules, and one draw needn't show every extreme that they name: `op_index`: no two triples name the same pair of leg b and leg c operators; every operator of each leg is named by some triple.
All inputs are finite; a program needn't handle non-finite values.
Results may differ from a plain program's by a relative error of at most 0.0019.
Values may be sent and summed in bfloat16 or wider, within the bound.
No kernel may reach another device: no remote copies, remote signals or barrier semaphores. Data moves between devices by JAX's collectives and lax.ppermute only.
A program may use at most 64 MiB of HBM per device.

v0:
```python
import functools
import math

import jax
import jax.numpy as jnp
from jax import lax
from jax.experimental import pallas as pl
from jax.experimental.pallas import tpu as pltpu
from jax.sharding import PartitionSpec as P

Z_HI, X_SIZE, Z_LO, Y_SIZE, CORES = 4, 4, 2, 4, 2
NT = (((1,), (1,)), ((), ()))
NN = (((1,), (0,)), ((), ()))


def grant(mib):
    return pltpu.CompilerParams(vmem_limit_bytes=mib << 20)


def pairs_of(move):
    out = []
    for z_hi in range(Z_HI):
        for x in range(X_SIZE):
            for z_lo in range(Z_LO):
                for y in range(Y_SIZE):
                    for core in range(CORES):
                        a, b, c, d, e = move(z_hi, x, z_lo, y, core)
                        there = (a % Z_HI) * X_SIZE + b % X_SIZE
                        block = ((c % Z_LO) * Y_SIZE + d % Y_SIZE) * CORES + e % CORES
                        here = (z_hi * X_SIZE + x) * 16 + (z_lo * Y_SIZE + y) * CORES + core
                        out.append((here, there * 16 + block))
    return out


def send(value, dz_hi=0, dx=0, dz_lo=0, dy=0, dcore=0):
    def move(z_hi, x, z_lo, y, core):
        return z_hi + dz_hi, x + dx, z_lo + dz_lo, y + dy, core + dcore

    return lax.ppermute(value, ("wide", "narrow"), pairs_of(move))


def swap_wide(value, bit):
    pairs = [(w, w ^ bit) for w in range(16)]
    return lax.ppermute(value, "wide", pairs)


def leg_c(node_ref, ops, scratch):
    rows = ops.shape[0]
    for a in range(16):
        block = lax.dot_general(ops, node_ref[a], NT, preferred_element_type=jnp.float32)
        for c in range(2):
            scratch[c, pl.ds(a, rows, stride=16), :] = block[:, c * 128 : (c + 1) * 128]


def put_first(scratch, out_ref):
    for k in range(12):
        for c in range(2):
            value = scratch[c, k * 128 : (k + 1) * 128].astype(jnp.bfloat16)
            out_ref[k, 0, :, c * 128 : (c + 1) * 128] = value


def prep_kernel(node_ref, leg_a_ref, legs_ref, first_ref, cols_ref, ops_ref, tiles, wide_tiles, scratch, sem):
    wide, narrow = lax.axis_index("wide"), lax.axis_index("narrow")
    core = lax.rem(narrow, 2)
    fetch = pltpu.make_async_copy(legs_ref.at[2, :, pl.ds(pl.multiple_of(wide * 16, 16), 16), :], tiles, sem)
    fetch.start()
    lane = lax.broadcasted_iota(jnp.int32, (256, 128), 1) % 32
    source = (narrow - core) * 16 + jnp.where(lane < 16, core * 16 + lane, (1 - core) * 16 + lane - 16)
    row = lax.broadcasted_iota(jnp.int32, (256, 128), 0)
    pick = jnp.where(row == source, 1.0, 0.0).astype(jnp.bfloat16)
    for i in range(12):
        block = lax.dot_general(leg_a_ref[0, i], pick, NN, preferred_element_type=jnp.float32)
        block = block.astype(jnp.bfloat16)
        cols_ref[i, :256] = block
        cols_ref[i, 256:] = block
    fetch.wait()
    wide_tiles[...] = tiles[...].astype(jnp.float32)
    half = [wide_tiles[k, pl.ds(pl.multiple_of(core * 8, 8), 8), :] for k in range(12)]
    ops = jnp.concatenate(half, axis=0).astype(jnp.bfloat16)
    ops_ref[...] = ops
    leg_c(node_ref, ops, scratch)
    put_first(scratch, first_ref)


def prep(node, leg_ops):
    return pl.pallas_call(
        prep_kernel,
        out_shape=[
            jax.ShapeDtypeStruct((12, 2, 128, 256), jnp.bfloat16),
            jax.ShapeDtypeStruct((12, 512, 128), jnp.bfloat16),
            jax.ShapeDtypeStruct((96, 256), jnp.bfloat16),
        ],
        grid=(1,),
        in_specs=[
            pl.BlockSpec((16, 256, 256), lambda g: (0, 0, 0)),
            pl.BlockSpec((1, 12, 256, 256), lambda g: (0, 0, 0, 0)),
            pl.BlockSpec(memory_space=pl.ANY),
        ],
        out_specs=[
            pl.BlockSpec((12, 1, 128, 256), lambda g: (0, 0, 0, 0)),
            pl.BlockSpec((12, 512, 128), lambda g: (0, 0, 0)),
            pl.BlockSpec((96, 256), lambda g: (0, 0)),
        ],
        scratch_shapes=[
            pltpu.VMEM((12, 16, 256), jnp.bfloat16),
            pltpu.VMEM((12, 16, 256), jnp.float32),
            pltpu.VMEM((2, 1536, 128), jnp.float32),
            pltpu.SemaphoreType.DMA(()),
        ],
        compiler_params=grant(17),
        cost_estimate=pl.CostEstimate(flops=2 * 3072 * 256 * 300, bytes_accessed=6 << 20, transcendentals=0),
        name="prep",
    )(node, leg_ops, leg_ops)


def sibling_kernel(node_ref, ops_ref, first_ref, out_ref, scratch):
    del first_ref
    leg_c(node_ref, ops_ref[...], scratch)
    put_first(scratch, out_ref)


def add_sibling(node, ops, first):
    return pl.pallas_call(
        sibling_kernel,
        out_shape=jax.ShapeDtypeStruct((12, 2, 128, 256), jnp.bfloat16),
        grid=(1,),
        in_specs=[
            pl.BlockSpec((16, 256, 256), lambda g: (0, 0, 0)),
            pl.BlockSpec((96, 256), lambda g: (0, 0)),
            pl.BlockSpec(memory_space=pl.ANY),
        ],
        out_specs=pl.BlockSpec((12, 1, 128, 256), lambda g: (0, 1, 0, 0)),
        scratch_shapes=[pltpu.VMEM((2, 1536, 128), jnp.float32)],
        input_output_aliases={2: 0},
        compiler_params=grant(10),
        cost_estimate=pl.CostEstimate(flops=2 * 1536 * 65536, bytes_accessed=3 << 20, transcendentals=0),
        name="sibling",
    )(node, ops, first)


def table_kernel(index_ref, offset_ref, out_ref):
    shape = (16, 128)
    row, lane = lax.broadcasted_iota(jnp.int32, shape, 0), lax.broadcasted_iota(jnp.int32, shape, 1)
    value = jnp.zeros(shape, jnp.int32)
    for t in range(4):
        for m in range(4):
            entry = offset_ref[t] if m == 3 else index_ref[t, m]
            value = jnp.where(lane == t * 4 + m, entry, value)
    out_ref[...] = jnp.where(row == lax.axis_index("wide"), value, 0)


def own_rows(op_index, offsets):
    smem = pl.BlockSpec(memory_space=pltpu.SMEM)
    return pl.pallas_call(
        table_kernel,
        out_shape=jax.ShapeDtypeStruct((16, 128), jnp.int32),
        in_specs=[smem, smem],
        compiler_params=grant(1),
        name="own_rows",
    )(op_index, offsets)


def main_kernel(table, first_ref, ops_ref, cols_ref, keep_ref, m1_ref, m2_ref, m3_ref, second, a_abs, a_rel):
    narrow = lax.axis_index("narrow")
    lane = lax.broadcasted_iota(jnp.int32, (16, 128), 1) // 32

    def fill(g, carry):
        starts = []
        for s in range(4):
            start = pl.multiple_of(256 - 32 * table[g, s * 4 + 3], 32)
            starts.append((table[g, s * 4], start))
        for blk in range(16):
            value = None
            for s, (i, start) in enumerate(starts):
                part = cols_ref[i, pl.ds(start + 16 * blk, 16), :]
                value = part if value is None else jnp.where(lane == s, part, value)
            a_abs[g, pl.ds(16 * blk, 16), :] = value
        return carry

    lax.fori_loop(0, 16, fill, 0)
    core, z_lo = lax.rem(narrow, 2), narrow // 8
    y = lax.rem(narrow // 2, 4)
    for blk in range(16):
        dy, dz, dc = blk // 4, (blk // 2) % 2, blk % 2
        block = lax.rem(z_lo + dz, 2) * 8 + lax.rem(y + dy, 4) * 2 + lax.rem(core + dc, 2)
        source = pl.multiple_of(block * 16, 16)
        for g in range(16):
            a_rel[16 * blk : 16 * blk + 16, g * 128 : (g + 1) * 128] = a_abs[g, pl.ds(source, 16), :]

    def step(g, carry):
        for s in range(4):
            j, k = table[g, s * 4 + 1], table[g, s * 4 + 2]
            lhs = first_ref[k].reshape(256, 256)
            value = lax.dot_general(lhs, ops_ref[0, j], NT, preferred_element_type=jnp.float32)
            value = value.astype(jnp.bfloat16)
            for half in range(2):
                for q in range(8):
                    where = pl.multiple_of(g * 128 + s * 32 + half * 16, 16)
                    source = half * 128 + q * 16
                    second[q, pl.ds(where, 16), :] = value[source : source + 16]
        return carry

    lax.fori_loop(0, 16, step, 0)
    for q in range(8):
        value = lax.dot_general(a_rel[...], second[q], NN, preferred_element_type=jnp.float32)
        keep_ref[q] = value[:64]
        m1_ref[q] = value[64:128].astype(jnp.bfloat16)
        m2_ref[q] = value[128:192].astype(jnp.bfloat16)
        m3_ref[q] = value[192:].astype(jnp.bfloat16)


def main_of(table, first, leg_ops, cols):
    whole3 = lambda g, s: (0, 0, 0)
    return pl.pallas_call(
        main_kernel,
        out_shape=[jax.ShapeDtypeStruct((8, 64, 256), jnp.float32)]
        + [jax.ShapeDtypeStruct((8, 64, 256), jnp.bfloat16)] * 3,
        grid_spec=pltpu.PrefetchScalarGridSpec(
            num_scalar_prefetch=1,
            grid=(1,),
            in_specs=[
                pl.BlockSpec((12, 2, 128, 256), lambda g, s: (0, 0, 0, 0)),
                pl.BlockSpec((1, 12, 256, 256), lambda g, s: (1, 0, 0, 0)),
                pl.BlockSpec((12, 512, 128), whole3),
            ],
            out_specs=[pl.BlockSpec((8, 64, 256), whole3)] * 4,
            scratch_shapes=[
                pltpu.VMEM((8, 2048, 256), jnp.bfloat16),
                pltpu.VMEM((16, 256, 128), jnp.bfloat16),
                pltpu.VMEM((256, 2048), jnp.bfloat16),
            ],
        ),
        compiler_params=grant(28),
        cost_estimate=pl.CostEstimate(flops=128 * 2 * 256**3, bytes_accessed=8 << 20, transcendentals=0),
        name="two_legs",
    )(table, first, leg_ops, cols)


def y_kernel(keep_ref, r1_ref, r2_ref, r3_ref, keep_out, m01_ref, m10_ref, m11_ref):
    f32 = jnp.float32
    for q in range(8):
        value = keep_ref[q] + r1_ref[q].astype(f32) + r2_ref[q].astype(f32) + r3_ref[q].astype(f32)
        keep_out[q] = value[:16]
        m01_ref[q] = value[16:32].astype(jnp.bfloat16)
        m10_ref[q] = value[32:48].astype(jnp.bfloat16)
        m11_ref[q] = value[48:].astype(jnp.bfloat16)


def y_sum(keep, r1, r2, r3):
    return pl.pallas_call(
        y_kernel,
        out_shape=[jax.ShapeDtypeStruct((8, 16, 256), jnp.float32)]
        + [jax.ShapeDtypeStruct((8, 16, 256), jnp.bfloat16)] * 3,
        compiler_params=grant(6),
        name="sum_y",
    )(keep, r1, r2, r3)


def z_kernel(keep_ref, r01_ref, r10_ref, r11_ref, out_ref, scratch):
    f32 = jnp.float32
    core = lax.rem(lax.axis_index("narrow"), 2)
    for q in range(8):
        mine = keep_ref[q] + r10_ref[q].astype(f32)
        other = r01_ref[q].astype(f32) + r11_ref[q].astype(f32)
        low = jnp.where(core == 0, mine, other)
        high = jnp.where(core == 0, other, mine)
        for c in range(2):
            scratch[c, pl.ds(q, 16, stride=16), :] = low[:, c * 128 : (c + 1) * 128]
            scratch[c, pl.ds(8 + q, 16, stride=16), :] = high[:, c * 128 : (c + 1) * 128]
    for c in range(2):
        out_ref[:, c * 128 : (c + 1) * 128] = scratch[c].astype(jnp.bfloat16)


def z_sum(keep, r01, r10, r11):
    vmem = pl.BlockSpec(memory_space=pltpu.VMEM)
    return pl.pallas_call(
        z_kernel,
        out_shape=jax.ShapeDtypeStruct((256, 256), jnp.bfloat16),
        in_specs=[vmem] * 4,
        out_specs=vmem,
        scratch_shapes=[pltpu.VMEM((2, 256, 128), jnp.float32)],
        compiler_params=grant(3),
        name="sum_z",
    )(keep, r01, r10, r11)


def last_kernel(tau, own_ref, left_ref, right_ref, fl_ref, fr_ref, node_ref, side_ref, out_ref, sigma):
    f32 = jnp.float32
    wide = lax.axis_index("wide")
    z_hi, x = wide // 4, lax.rem(wide, 4)
    row = lax.broadcasted_iota(jnp.int32, (256, 256), 0)
    column = lax.broadcasted_iota(jnp.int32, (256, 256), 1)
    eye = jnp.where(row == column, 1.0, 0.0).astype(jnp.bfloat16)
    for r in range(ROWS):
        for dz in range(4):
            two = fl_ref[dz] if dz < 2 else fr_ref[dz - 2]
            for dx, value in ((0, own_ref[dz]), (1, left_ref[dz]), (3, right_ref[dz]), (2, two)):
                w = lax.rem(z_hi - dz + 4, 4) * 4 + lax.rem(x - dx + 4, 4)
                place = pl.ds(pl.multiple_of(w * 16, 16), 16)
                sigma[r, place, :] = value[r * 16 : (r + 1) * 16]
    for r in range(ROWS):
        turned = lax.dot_general(eye, sigma[r], NT, preferred_element_type=f32)
        out_ref[r] = node_ref[r].astype(f32) + tau * (side_ref[r].astype(f32) - turned)


ROWS = 4


def last_of(tau, own, left, right, fl, fr, node, side):
    def piece(n):
        return pl.BlockSpec((n, ROWS * 16, 256), lambda r: (0, r, 0))

    row = pl.BlockSpec((ROWS, 256, 256), lambda r: (r, 0, 0))
    return pl.pallas_call(
        functools.partial(last_kernel, tau),
        out_shape=jax.ShapeDtypeStruct((16, 256, 256), jnp.float32),
        grid=(16 // ROWS,),
        in_specs=[piece(4), piece(4), piece(4), piece(2), piece(2), row, row],
        out_specs=row,
        scratch_shapes=[pltpu.VMEM((ROWS, 256, 256), jnp.bfloat16)],
        compiler_params=grant(16),
        name="update",
    )(own, left, right, fl, fr, node, side)


def per_device(node, right_side, leg_ops, op_index, offsets):
    tau = 0.5 / math.sqrt(op_index.shape[0] * lax.axis_size("wide"))
    table = own_rows(op_index, offsets)
    for step in range(4):
        table = table + swap_wide(table, 1 << step)
    sibling = send(node, dcore=1)
    first, cols, ops_c = prep(node, leg_ops)
    first = add_sibling(sibling, ops_c, first)
    keep, m1, m2, m3 = main_of(table, first, leg_ops, cols)
    r1, r3, r2 = send(m1, dy=1), send(m3, dy=3), send(m2, dy=2)
    keep, m01, m10, m11 = y_sum(keep, r1, r2, r3)
    r10, r11, r01 = send(m10, dz_lo=1), send(m11, dz_lo=1, dcore=1), send(m01, dcore=1)
    piece = z_sum(keep, r01, r10, r11)
    got = [piece] + [send(piece, dz_hi=d) for d in (1, 2, 3)]
    got = jnp.stack(got)
    left, right = send(got, dx=1), send(got, dx=3)
    fl, fr = send(left[:2], dx=1), send(right[2:], dx=3)
    return last_of(tau, got, left, right, fl, fr, node, right_side)


def solution(mesh):
    in_specs = (P("narrow", None, None), P("narrow", None, None), P(), P("wide", None), P("wide"))
    out_specs = P("narrow", None, None)
    return jax.shard_map(
        per_device, mesh=mesh, in_specs=in_specs, out_specs=out_specs, check_vma=False
    )
```

profile of v0, /device:TPU:32, one launch (start us, length us, event | category | flops | bytes accessed | tf_op | source)
XLA Modules:
  0.0 107.8 jit_solution(13604956857665191579)
XLA Ops:
  0.0 0.7 copy-done.5
  1.9 1.6 %collective-permute-start = (s32[16,128]{1,0:T(8,128)S(1)}, s32[16,128]{1,0:T(8,128)S(1)}, u32[]{:S(2)}, u32[]{:S(2)}) collective-permute-start(s32[16,128]{1,0:T(8,128)S(1)} %own_rows.1), channel_id=1, source_target_pairs={{0,16},{16,0},{32,48},{48,32},{64,80},{80,64},{96,112},{112,96},{1... | collective-permute-start | bytes 24584 | tf_op jit(solution)/shard_map/ppermute | solution.py:44
  3.5 2.2 %collective-permute-done = s32[16,128]{1,0:T(8,128)S(1)} collective-permute-done((s32[16,128]{1,0:T(8,128)S(1)}, s32[16,128]{1,0:T(8,128)S(1)}, u32[]{:S(2)}, u32[]{:S(2)}) %collective-permute-start) | collective-permute-done | bytes 8224 | tf_op jit(solution)/shard_map/ppermute | solution.py:44
  5.7 3.0 %collective-permute-start.1 = (s32[16,128]{1,0:T(8,128)S(1)}, s32[16,128]{1,0:T(8,128)S(1)}, u32[]{:S(2)}, u32[]{:S(2)}) collective-permute-start(s32[16,128]{1,0:T(8,128)S(1)} %add.12), channel_id=1, source_target_pairs={{0,32},{16,48},{32,0},{48,16},{64,96},{80,112},{96,64},{112,80},{1... | collective-permute-start | bytes 24584 | tf_op jit(solution)/shard_map/ppermute | solution.py:44
  8.7 2.1 %collective-permute-done.1 = s32[16,128]{1,0:T(8,128)S(1)} collective-permute-done((s32[16,128]{1,0:T(8,128)S(1)}, s32[16,128]{1,0:T(8,128)S(1)}, u32[]{:S(2)}, u32[]{:S(2)}) %collective-permute-start.1) | collective-permute-done | bytes 8224 | tf_op jit(solution)/shard_map/ppermute | solution.py:44
  10.8 3.3 %collective-permute-start.2 = (s32[16,128]{1,0:T(8,128)S(1)}, s32[16,128]{1,0:T(8,128)S(1)}, u32[]{:S(2)}, u32[]{:S(2)}) collective-permute-start(s32[16,128]{1,0:T(8,128)S(1)} %add.13), channel_id=1, source_target_pairs={{0,64},{16,80},{32,96},{48,112},{64,0},{80,16},{96,32},{112,48},{1... | collective-permute-start | bytes 24584 | tf_op jit(solution)/shard_map/ppermute | solution.py:44
  14.1 1.6 %collective-permute-done.2 = s32[16,128]{1,0:T(8,128)S(1)} collective-permute-done((s32[16,128]{1,0:T(8,128)S(1)}, s32[16,128]{1,0:T(8,128)S(1)}, u32[]{:S(2)}, u32[]{:S(2)}) %collective-permute-start.2) | collective-permute-done | bytes 8224 | tf_op jit(solution)/shard_map/ppermute | solution.py:44
  15.7 5.9 %collective-permute-start.3 = (s32[16,128]{1,0:T(8,128)S(1)}, s32[16,128]{1,0:T(8,128)S(1)}, u32[]{:S(2)}, u32[]{:S(2)}) collective-permute-start(s32[16,128]{1,0:T(8,128)S(1)} %add.14), channel_id=1, source_target_pairs={{0,128},{16,144},{32,160},{48,176},{64,192},{80,208},{96,224},{112... | collective-permute-start | bytes 24584 | tf_op jit(solution)/shard_map/ppermute | solution.py:44
  21.7 2.3 %copy-done = bf16[3,12,256,256]{3,2,1,0:T(8,128)(2,1)S(1)} copy-done((bf16[3,12,256,256]{3,2,1,0:T(8,128)(2,1)S(1)}, bf16[3,12,256,256]{3,2,1,0:T(8,128)(2,1)}, u32[]{:S(2)}) %copy-start) | copy-done | bytes 4718616
  24.0 1.6 %copy-done.2 = bf16[16,256,256]{2,1,0:T(8,128)(2,1)S(1)} copy-done((bf16[16,256,256]{2,1,0:T(8,128)(2,1)S(1)}, bf16[16,256,256]{2,1,0:T(8,128)(2,1)}, u32[]{:S(2)}) %copy-start.2) | copy-done | bytes 2097176
  25.6 1.7 %prep.1 = (bf16[12,2,128,256]{3,2,1,0:T(8,128)(2,1)S(1)}, bf16[12,512,128]{2,1,0:T(8,128)(2,1)S(1)}, bf16[96,256]{1,0:T(8,128)(2,1)S(1)}) custom-call(bf16[16,256,256]{2,1,0:T(8,128)(2,1)S(1)} %copy-done.2, bf16[3,12,256,256]{3,2,1,0:T(8,128)(2,1)S(1)} %copy-done, bf16[3,12,256,256]{3,2,1,0:T(8,128)(2,1)S(1)} %copy-done), custom_call_target="tpu_custom_call" | custom-call | flops 471859200 | bytes 6291456 | tf_op jit(solution)/shard_map/prep/pallas_call | solution.py:86
  27.4 1.1 %sibling.1.first_ref = bf16[12,2,128,256]{3,2,1,0:T(8,128)(2,1)S(1)} custom-call(bf16[16,256,256]{2,1,0:T(8,128)(2,1)S(1)} %collective-permute-done.4.node_ref, bf16[96,256]{1,0:T(8,128)(2,1)S(1)} %get-tuple-element.16.ops_ref, bf16[12,2,128,256]{3,2,1,0:T(8,128)(2,1)S(1)} %get-tuple-element.17.first_ref), custom_call_target="tpu_custom_call", output_to_operand_aliasing={{}: (2, {})} | custom-call | flops 201326592 | bytes 3145728 | tf_op jit(solution)/shard_map/sibling/pallas_call | solution.py:123
  28.5 1.2 %copy-done.1 = bf16[3,12,256,256]{3,2,1,0:T(8,128)(2,1)S(1)} copy-done((bf16[3,12,256,256]{3,2,1,0:T(8,128)(2,1)S(1)}, bf16[3,12,256,256]{3,2,1,0:T(8,128)(2,1)}, u32[]{:S(2)}) %copy-start.1) | copy-done | bytes 4718616
  29.7 10.3 %two_legs.1 = (f32[8,64,256]{2,1,0:T(8,128)S(1)}, bf16[8,64,256]{2,1,0:T(8,128)(2,1)S(1)}, bf16[8,64,256]{2,1,0:T(8,128)(2,1)S(1)}, bf16[8,64,256]{2,1,0:T(8,128)(2,1)S(1)}) custom-call(s32[16,128]{1,0:T(8,128)S(1)} %add.15.table, bf16[12,2,128,256]{3,2,1,0:T(8,128)(2,1)S(1)} %sibling.1.first_ref, bf16[3,12,256,256]{3,2,1,0:T(8,128)(2,1)S(1)} %copy-done.1, ...), custom_call_target="tpu_custom_call" | custom-call | flops 4294967296 | bytes 8388608 | tf_op jit(solution)/shard_map/two_legs/pallas_call | solution.py:214
  40.0 1.6 %collective-permute-start.5 = (bf16[8,64,256]{2,1,0:T(8,128)(2,1)S(1)}, bf16[8,64,256]{2,1,0:T(8,128)(2,1)S(1)}, u32[]{:S(2)}, u32[]{:S(2)}) collective-permute-start(bf16[8,64,256]{2,1,0:T(8,128)(2,1)S(1)} %get-tuple-element.20), channel_id=1, source_target_pairs={{0,2},{1,3},{2,4},{3,5},{4,6},{5,7},{6,0},{7,1},{8,10},{9,11},{10,... | collective-permute-start | bytes 786440 | tf_op jit(solution)/shard_map/ppermute | solution.py:39
  41.6 2.9 %collective-permute-start.6 = (bf16[8,64,256]{2,1,0:T(8,128)(2,1)S(1)}, bf16[8,64,256]{2,1,0:T(8,128)(2,1)S(1)}, u32[]{:S(2)}, u32[]{:S(2)}) collective-permute-start(bf16[8,64,256]{2,1,0:T(8,128)(2,1)S(1)} %get-tuple-element.21), channel_id=1, source_target_pairs={{0,4},{1,5},{2,6},{3,7},{4,0},{5,1},{6,2},{7,3},{8,12},{9,13},{10,... | collective-permute-start | bytes 786440 | tf_op jit(solution)/shard_map/ppermute | solution.py:39
  44.5 1.3 %collective-permute-start.7 = (bf16[8,64,256]{2,1,0:T(8,128)(2,1)S(1)}, bf16[8,64,256]{2,1,0:T(8,128)(2,1)S(1)}, u32[]{:S(2)}, u32[]{:S(2)}) collective-permute-start(bf16[8,64,256]{2,1,0:T(8,128)(2,1)S(1)} %get-tuple-element.22), channel_id=1, source_target_pairs={{0,6},{1,7},{2,0},{3,1},{4,2},{5,3},{6,4},{7,5},{8,14},{9,15},{10,... | collective-permute-start | bytes 786440 | tf_op jit(solution)/shard_map/ppermute | solution.py:39
  45.9 4.4 %collective-permute-done.5.r1_ref = bf16[8,64,256]{2,1,0:T(8,128)(2,1)S(1)} collective-permute-done((bf16[8,64,256]{2,1,0:T(8,128)(2,1)S(1)}, bf16[8,64,256]{2,1,0:T(8,128)(2,1)S(1)}, u32[]{:S(2)}, u32[]{:S(2)}) %collective-permute-start.5) | collective-permute-done | bytes 262176 | tf_op jit(solution)/shard_map/ppermute | solution.py:39
  50.3 2.8 %collective-permute-done.6.r2_ref = bf16[8,64,256]{2,1,0:T(8,128)(2,1)S(1)} collective-permute-done((bf16[8,64,256]{2,1,0:T(8,128)(2,1)S(1)}, bf16[8,64,256]{2,1,0:T(8,128)(2,1)S(1)}, u32[]{:S(2)}, u32[]{:S(2)}) %collective-permute-start.6) | collective-permute-done | bytes 262176 | tf_op jit(solution)/shard_map/ppermute | solution.py:39
  53.3 1.1 %collective-permute-start.9 = (bf16[8,16,256]{2,1,0:T(8,128)(2,1)S(1)}, bf16[8,16,256]{2,1,0:T(8,128)(2,1)S(1)}, u32[]{:S(2)}, u32[]{:S(2)}) collective-permute-start(bf16[8,16,256]{2,1,0:T(8,128)(2,1)S(1)} %get-tuple-element.25), channel_id=1, source_target_pairs={{0,8},{1,9},{2,10},{3,11},{4,12},{5,13},{6,14},{7,15},{8,0},{9,1},... | collective-permute-start | bytes 196616 | tf_op jit(solution)/shard_map/ppermute | solution.py:39
  54.4 0.7 collective-permute-start.10
  55.2 3.0 %collective-permute-done.9.r10_ref = bf16[8,16,256]{2,1,0:T(8,128)(2,1)S(1)} collective-permute-done((bf16[8,16,256]{2,1,0:T(8,128)(2,1)S(1)}, bf16[8,16,256]{2,1,0:T(8,128)(2,1)S(1)}, u32[]{:S(2)}, u32[]{:S(2)}) %collective-permute-start.9) | collective-permute-done | bytes 65568 | tf_op jit(solution)/shard_map/ppermute | solution.py:39
  59.4 4.6 %collective-permute-start.12 = (bf16[256,256]{1,0:T(8,128)(2,1)S(1)}, bf16[256,256]{1,0:T(8,128)(2,1)S(1)}, u32[]{:S(2)}, u32[]{:S(2)}) collective-permute-start(bf16[256,256]{1,0:T(8,128)(2,1)S(1)} %sum_z.1), channel_id=1, source_target_pairs={{0,128},{1,129},{2,130},{3,131},{4,132},{5,133},{6,134},{7,135},{8... | collective-permute-start | bytes 393224 | tf_op jit(solution)/shard_map/ppermute | solution.py:39
  64.1 4.5 %collective-permute-done.13 = bf16[256,256]{1,0:T(8,128)(2,1)S(1)} collective-permute-done((bf16[256,256]{1,0:T(8,128)(2,1)S(1)}, bf16[256,256]{1,0:T(8,128)(2,1)S(1)}, u32[]{:S(2)}, u32[]{:S(2)}) %collective-permute-start.13) | collective-permute-done | bytes 131104 | tf_op jit(solution)/shard_map/ppermute | solution.py:39
  68.6 6.9 %collective-permute-done.12 = bf16[256,256]{1,0:T(8,128)(2,1)S(1)} collective-permute-done((bf16[256,256]{1,0:T(8,128)(2,1)S(1)}, bf16[256,256]{1,0:T(8,128)(2,1)S(1)}, u32[]{:S(2)}, u32[]{:S(2)}) %collective-permute-start.12) | collective-permute-done | bytes 131104 | tf_op jit(solution)/shard_map/ppermute | solution.py:39
  75.6 2.2 %collective-permute-done.11 = bf16[256,256]{1,0:T(8,128)(2,1)S(1)} collective-permute-done((bf16[256,256]{1,0:T(8,128)(2,1)S(1)}, bf16[256,256]{1,0:T(8,128)(2,1)S(1)}, u32[]{:S(2)}, u32[]{:S(2)}) %collective-permute-start.11) | collective-permute-done | bytes 131104 | tf_op jit(solution)/shard_map/ppermute | solution.py:39
  77.8 2.8 %collective-permute-start.15 = (bf16[4,256,256]{2,1,0:T(8,128)(2,1)S(1)}, bf16[4,256,256]{2,1,0:T(8,128)(2,1)S(1)}, u32[]{:S(2)}, u32[]{:S(2)}) collective-permute-start(bf16[4,256,256]{2,1,0:T(8,128)(2,1)S(1)} %pad_maximum_fusion.own_ref), channel_id=1, source_target_pairs={{0,48},{1,49},{2,50},{3,51},{4,52},{5,53},{6,54},{7,55},{8,56},{9,... | collective-permute-start | bytes 1572872 | tf_op jit(solution)/shard_map/ppermute | solution.py:39
  80.7 11.4 %collective-permute-done.15.right_ref = bf16[4,256,256]{2,1,0:T(8,128)(2,1)S(1)} collective-permute-done((bf16[4,256,256]{2,1,0:T(8,128)(2,1)S(1)}, bf16[4,256,256]{2,1,0:T(8,128)(2,1)S(1)}, u32[]{:S(2)}, u32[]{:S(2)}) %collective-permute-start.15) | collective-permute-done | bytes 524320 | tf_op jit(solution)/shard_map/ppermute | solution.py:39
  92.1 3.8 %collective-permute-start.17 = (bf16[2,256,256]{2,1,0:T(8,128)(2,1)S(1)}, bf16[2,256,256]{2,1,0:T(8,128)(2,1)S(1)}, u32[]{:S(2)}, u32[]{:S(2)}) collective-permute-start(bf16[2,256,256]{2,1,0:T(8,128)(2,1)S(1)} %slice.9), channel_id=1, source_target_pairs={{0,48},{1,49},{2,50},{3,51},{4,52},{5,53},{6,54},{7,55},{8,56},{9,... | collective-permute-start | bytes 786440 | tf_op jit(solution)/shard_map/ppermute | solution.py:39
  95.9 4.8 %collective-permute-done.17.fr_ref = bf16[2,256,256]{2,1,0:T(8,128)(2,1)S(1)} collective-permute-done((bf16[2,256,256]{2,1,0:T(8,128)(2,1)S(1)}, bf16[2,256,256]{2,1,0:T(8,128)(2,1)S(1)}, u32[]{:S(2)}, u32[]{:S(2)}) %collective-permute-start.17) | collective-permute-done | bytes 262176 | tf_op jit(solution)/shard_map/ppermute | solution.py:39
  100.7 3.5 %collective-permute-done.16.fl_ref = bf16[2,256,256]{2,1,0:T(8,128)(2,1)S(1)} collective-permute-done((bf16[2,256,256]{2,1,0:T(8,128)(2,1)S(1)}, bf16[2,256,256]{2,1,0:T(8,128)(2,1)S(1)}, u32[]{:S(2)}, u32[]{:S(2)}) %collective-permute-start.16) | collective-permute-done | bytes 262176 | tf_op jit(solution)/shard_map/ppermute | solution.py:39
  104.2 3.5 %update.1 = f32[16,256,256]{2,1,0:T(8,128)} custom-call(bf16[4,256,256]{2,1,0:T(8,128)(2,1)S(1)} %pad_maximum_fusion.own_ref, bf16[4,256,256]{2,1,0:T(8,128)(2,1)S(1)} %collective-permute-done.14.left_ref, bf16[4,256,256]{2,1,0:T(8,128)(2,1)S(1)} %collective-permute-done.15.right_ref, bf16[2,256,256]{2,1,0:T(8,128)(2,1)S(1)} %collective-permute-done.16.fl_ref, ...), custom_call_target="tpu_custom_call" | custom-call | tf_op jit(solution)/shard_map/update/pallas_call | solution.py:314
  (32 shorter events, 2.9 us)
Async XLA Ops:
  0.0 27.3 %collective-permute-start.4 = (bf16[16,256,256]{2,1,0:T(8,128)(2,1)}, bf16[16,256,256]{2,1,0:T(8,128)(2,1)S(1)}, u32[]{:S(2)}, u32[]{:S(2)}) collective-permute-start(bf16[16,256,256]{2,1,0:T(8,128)(2,1)} %node_ref.3), channel_id=1, source_target_pairs={{0,1},{1,0},{2,3},{3,2},{4,5},{5,4},{6,7},{7,6},{8,9},{9,8},{10,11... | collective-permute-start | bytes 6291464 | tf_op jit(solution)/shard_map/ppermute | solution.py:39
  0.0 0.7 copy-start.5
  0.7 0.7 copy-start.6
  1.9 3.7 %collective-permute-start = (s32[16,128]{1,0:T(8,128)S(1)}, s32[16,128]{1,0:T(8,128)S(1)}, u32[]{:S(2)}, u32[]{:S(2)}) collective-permute-start(s32[16,128]{1,0:T(8,128)S(1)} %own_rows.1), channel_id=1, source_target_pairs={{0,16},{16,0},{32,48},{48,32},{64,80},{80,64},{96,112},{112,96},{1... | collective-permute-start | bytes 24584 | tf_op jit(solution)/shard_map/ppermute | solution.py:44
  5.7 5.2 %collective-permute-start.1 = (s32[16,128]{1,0:T(8,128)S(1)}, s32[16,128]{1,0:T(8,128)S(1)}, u32[]{:S(2)}, u32[]{:S(2)}) collective-permute-start(s32[16,128]{1,0:T(8,128)S(1)} %add.12), channel_id=1, source_target_pairs={{0,32},{16,48},{32,0},{48,16},{64,96},{80,112},{96,64},{112,80},{1... | collective-permute-start | bytes 24584 | tf_op jit(solution)/shard_map/ppermute | solution.py:44
  10.8 4.9 %collective-permute-start.2 = (s32[16,128]{1,0:T(8,128)S(1)}, s32[16,128]{1,0:T(8,128)S(1)}, u32[]{:S(2)}, u32[]{:S(2)}) collective-permute-start(s32[16,128]{1,0:T(8,128)S(1)} %add.13), channel_id=1, source_target_pairs={{0,64},{16,80},{32,96},{48,112},{64,0},{80,16},{96,32},{112,48},{1... | collective-permute-start | bytes 24584 | tf_op jit(solution)/shard_map/ppermute | solution.py:44
  15.7 11.6 %collective-permute-start.3 = (s32[16,128]{1,0:T(8,128)S(1)}, s32[16,128]{1,0:T(8,128)S(1)}, u32[]{:S(2)}, u32[]{:S(2)}) collective-permute-start(s32[16,128]{1,0:T(8,128)S(1)} %add.14), channel_id=1, source_target_pairs={{0,128},{16,144},{32,160},{48,176},{64,192},{80,208},{96,224},{112... | collective-permute-start | bytes 24584 | tf_op jit(solution)/shard_map/ppermute | solution.py:44
  21.7 2.3 %copy-start = (bf16[3,12,256,256]{3,2,1,0:T(8,128)(2,1)S(1)}, bf16[3,12,256,256]{3,2,1,0:T(8,128)(2,1)}, u32[]{:S(2)}) copy-start(bf16[3,12,256,256]{3,2,1,0:T(8,128)(2,1)} %ops_ref.1) | copy-start | bytes 14155780
  24.0 1.6 %copy-start.2 = (bf16[16,256,256]{2,1,0:T(8,128)(2,1)S(1)}, bf16[16,256,256]{2,1,0:T(8,128)(2,1)}, u32[]{:S(2)}) copy-start(bf16[16,256,256]{2,1,0:T(8,128)(2,1)} %node_ref.3) | copy-start | bytes 6291460
  27.3 2.3 %copy-start.1 = (bf16[3,12,256,256]{3,2,1,0:T(8,128)(2,1)S(1)}, bf16[3,12,256,256]{3,2,1,0:T(8,128)(2,1)}, u32[]{:S(2)}) copy-start(bf16[3,12,256,256]{3,2,1,0:T(8,128)(2,1)} %ops_ref.1) | copy-start | bytes 14155780
  29.7 74.6 %copy-start.4 = (bf16[16,256,256]{2,1,0:T(8,128)(2,1)S(1)}, bf16[16,256,256]{2,1,0:T(8,128)(2,1)}, u32[]{:S(2)}) copy-start(bf16[16,256,256]{2,1,0:T(8,128)(2,1)} %side_ref.1) | copy-start | bytes 6291460
  40.0 64.3 %copy-start.3 = (bf16[16,256,256]{2,1,0:T(8,128)(2,1)S(1)}, bf16[16,256,256]{2,1,0:T(8,128)(2,1)}, u32[]{:S(2)}) copy-start(bf16[16,256,256]{2,1,0:T(8,128)(2,1)} %node_ref.3) | copy-start | bytes 6291460
  40.0 10.3 %collective-permute-start.5 = (bf16[8,64,256]{2,1,0:T(8,128)(2,1)S(1)}, bf16[8,64,256]{2,1,0:T(8,128)(2,1)S(1)}, u32[]{:S(2)}, u32[]{:S(2)}) collective-permute-start(bf16[8,64,256]{2,1,0:T(8,128)(2,1)S(1)} %get-tuple-element.20), channel_id=1, source_target_pairs={{0,2},{1,3},{2,4},{3,5},{4,6},{5,7},{6,0},{7,1},{8,10},{9,11},{10,... | collective-permute-start | bytes 786440 | tf_op jit(solution)/shard_map/ppermute | solution.py:39
  41.6 11.5 %collective-permute-start.6 = (bf16[8,64,256]{2,1,0:T(8,128)(2,1)S(1)}, bf16[8,64,256]{2,1,0:T(8,128)(2,1)S(1)}, u32[]{:S(2)}, u32[]{:S(2)}) collective-permute-start(bf16[8,64,256]{2,1,0:T(8,128)(2,1)S(1)} %get-tuple-element.21), channel_id=1, source_target_pairs={{0,4},{1,5},{2,6},{3,7},{4,0},{5,1},{6,2},{7,3},{8,12},{9,13},{10,... | collective-permute-start | bytes 786440 | tf_op jit(solution)/shard_map/ppermute | solution.py:39
  44.5 8.6 %collective-permute-start.7 = (bf16[8,64,256]{2,1,0:T(8,128)(2,1)S(1)}, bf16[8,64,256]{2,1,0:T(8,128)(2,1)S(1)}, u32[]{:S(2)}, u32[]{:S(2)}) collective-permute-start(bf16[8,64,256]{2,1,0:T(8,128)(2,1)S(1)} %get-tuple-element.22), channel_id=1, source_target_pairs={{0,6},{1,7},{2,0},{3,1},{4,2},{5,3},{6,4},{7,5},{8,14},{9,15},{10,... | collective-permute-start | bytes 786440 | tf_op jit(solution)/shard_map/ppermute | solution.py:39
  53.2 2.0 %collective-permute-start.8 = (bf16[8,16,256]{2,1,0:T(8,128)(2,1)S(1)}, bf16[8,16,256]{2,1,0:T(8,128)(2,1)S(1)}, u32[]{:S(2)}, u32[]{:S(2)}) collective-permute-start(bf16[8,16,256]{2,1,0:T(8,128)(2,1)S(1)} %get-tuple-element.24), channel_id=1, source_target_pairs={{0,1},{1,0},{2,3},{3,2},{4,5},{5,4},{6,7},{7,6},{8,9},{9,8},{10,11... | collective-permute-start | bytes 196616 | tf_op jit(solution)/shard_map/ppermute | solution.py:39
  53.3 4.9 %collective-permute-start.9 = (bf16[8,16,256]{2,1,0:T(8,128)(2,1)S(1)}, bf16[8,16,256]{2,1,0:T(8,128)(2,1)S(1)}, u32[]{:S(2)}, u32[]{:S(2)}) collective-permute-start(bf16[8,16,256]{2,1,0:T(8,128)(2,1)S(1)} %get-tuple-element.25), channel_id=1, source_target_pairs={{0,8},{1,9},{2,10},{3,11},{4,12},{5,13},{6,14},{7,15},{8,0},{9,1},... | collective-permute-start | bytes 196616 | tf_op jit(solution)/shard_map/ppermute | solution.py:39
  54.4 4.4 %collective-permute-start.10 = (bf16[8,16,256]{2,1,0:T(8,128)(2,1)S(1)}, bf16[8,16,256]{2,1,0:T(8,128)(2,1)S(1)}, u32[]{:S(2)}, u32[]{:S(2)}) collective-permute-start(bf16[8,16,256]{2,1,0:T(8,128)(2,1)S(1)} %get-tuple-element.26), channel_id=1, source_target_pairs={{0,9},{1,8},{2,11},{3,10},{4,13},{5,12},{6,15},{7,14},{8,1},{9,0},... | collective-permute-start | bytes 196616 | tf_op jit(solution)/shard_map/ppermute | solution.py:39
  59.0 9.7 %collective-permute-start.13 = (bf16[256,256]{1,0:T(8,128)(2,1)S(1)}, bf16[256,256]{1,0:T(8,128)(2,1)S(1)}, u32[]{:S(2)}, u32[]{:S(2)}) collective-permute-start(bf16[256,256]{1,0:T(8,128)(2,1)S(1)} %sum_z.1), channel_id=1, source_target_pairs={{0,192},{1,193},{2,194},{3,195},{4,196},{5,197},{6,198},{7,199},{8... | collective-permute-start | bytes 393224 | tf_op jit(solution)/shard_map/ppermute | solution.py:39
  59.4 16.1 %collective-permute-start.12 = (bf16[256,256]{1,0:T(8,128)(2,1)S(1)}, bf16[256,256]{1,0:T(8,128)(2,1)S(1)}, u32[]{:S(2)}, u32[]{:S(2)}) collective-permute-start(bf16[256,256]{1,0:T(8,128)(2,1)S(1)} %sum_z.1), channel_id=1, source_target_pairs={{0,128},{1,129},{2,130},{3,131},{4,132},{5,133},{6,134},{7,135},{8... | collective-permute-start | bytes 393224 | tf_op jit(solution)/shard_map/ppermute | solution.py:39
  64.1 13.7 %collective-permute-start.11 = (bf16[256,256]{1,0:T(8,128)(2,1)S(1)}, bf16[256,256]{1,0:T(8,128)(2,1)S(1)}, u32[]{:S(2)}, u32[]{:S(2)}) collective-permute-start(bf16[256,256]{1,0:T(8,128)(2,1)S(1)} %sum_z.1), channel_id=1, source_target_pairs={{0,64},{1,65},{2,66},{3,67},{4,68},{5,69},{6,70},{7,71},{8,72},{9,... | collective-permute-start | bytes 393224 | tf_op jit(solution)/shard_map/ppermute | solution.py:39
  77.8 14.2 %collective-permute-start.15 = (bf16[4,256,256]{2,1,0:T(8,128)(2,1)S(1)}, bf16[4,256,256]{2,1,0:T(8,128)(2,1)S(1)}, u32[]{:S(2)}, u32[]{:S(2)}) collective-permute-start(bf16[4,256,256]{2,1,0:T(8,128)(2,1)S(1)} %pad_maximum_fusion.own_ref), channel_id=1, source_target_pairs={{0,48},{1,49},{2,50},{3,51},{4,52},{5,53},{6,54},{7,55},{8,56},{9,... | collective-permute-start | bytes 1572872 | tf_op jit(solution)/shard_map/ppermute | solution.py:39
  80.7 15.2 %collective-permute-start.14 = (bf16[4,256,256]{2,1,0:T(8,128)(2,1)S(1)}, bf16[4,256,256]{2,1,0:T(8,128)(2,1)S(1)}, u32[]{:S(2)}, u32[]{:S(2)}) collective-permute-start(bf16[4,256,256]{2,1,0:T(8,128)(2,1)S(1)} %pad_maximum_fusion.own_ref), channel_id=1, source_target_pairs={{0,16},{1,17},{2,18},{3,19},{4,20},{5,21},{6,22},{7,23},{8,24},{9,... | collective-permute-start | bytes 1572872 | tf_op jit(solution)/shard_map/ppermute | solution.py:39
  92.1 8.7 %collective-permute-start.17 = (bf16[2,256,256]{2,1,0:T(8,128)(2,1)S(1)}, bf16[2,256,256]{2,1,0:T(8,128)(2,1)S(1)}, u32[]{:S(2)}, u32[]{:S(2)}) collective-permute-start(bf16[2,256,256]{2,1,0:T(8,128)(2,1)S(1)} %slice.9), channel_id=1, source_target_pairs={{0,48},{1,49},{2,50},{3,51},{4,52},{5,53},{6,54},{7,55},{8,56},{9,... | collective-permute-start | bytes 786440 | tf_op jit(solution)/shard_map/ppermute | solution.py:39
  95.9 8.4 %collective-permute-start.16 = (bf16[2,256,256]{2,1,0:T(8,128)(2,1)S(1)}, bf16[2,256,256]{2,1,0:T(8,128)(2,1)S(1)}, u32[]{:S(2)}, u32[]{:S(2)}) collective-permute-start(bf16[2,256,256]{2,1,0:T(8,128)(2,1)S(1)} %slice.8), channel_id=1, source_target_pairs={{0,16},{1,17},{2,18},{3,19},{4,20},{5,21},{6,22},{7,23},{8,24},{9,... | collective-permute-start | bytes 786440 | tf_op jit(solution)/shard_map/ppermute | solution.py:39
where the time goes:
time: 108 us
  waiting for transfers between devices  50.1 us (46%)
  starting transfers between devices  33.5 us (31%)
  Pallas kernels  17.4 us (16%)
  local copies, waits for them, and re-layouts  6.54 us (6%)
    ppermute x14, waiting for transfers between devices, send(): return lax.ppermute(value, ('wide', 'narrow'), pairs_of(move))  44.2 us
    ppermute x14, starting transfers between devices, send(): return lax.ppermute(value, ('wide', 'narrow'), pairs_of(move))  19.6 us
    ppermute x4, starting transfers between devices, swap_wide(): return lax.ppermute(value, 'wide', pairs)  13.8 us
    pallas_call x1, Pallas kernels, main_of(): pl.pallas_call(main_kernel, out_shape=[jax.ShapeDtypeStruct((8, 64, 256),...  10.3 us
    unnamed x14, local copies, waits for them, and re-layouts  6.5 us
    ppermute x4, waiting for transfers between devices, swap_wide(): return lax.ppermute(value, 'wide', pairs)  5.93 us
    pallas_call x1, Pallas kernels, last_of(): pl.pallas_call(functools.partial(last_kernel, tau), out_shape=jax.ShapeDt...  3.53 us
  transfers between devices with their start and end apart: 18, of which 13 were waited for; matrix products, arithmetic and copies ran while one was open for 0% of the time, Pallas kernels for 2%

commit v1 on v0

--- a/solution.py
+++ b/solution.py
@@ -11,6 +11,10 @@
 Z_HI, X_SIZE, Z_LO, Y_SIZE, CORES = 4, 4, 2, 4, 2
 NT = (((1,), (1,)), ((), ()))
 NN = (((1,), (0,)), ((), ()))
+
+
+def in_hbm(value):
+    return pltpu.with_memory_space_constraint(value, pltpu.HBM)
 
 
 def grant(mib):
@@ -39,11 +43,6 @@
     return lax.ppermute(value, ("wide", "narrow"), pairs_of(move))
 
 
-def swap_wide(value, bit):
-    pairs = [(w, w ^ bit) for w in range(16)]
-    return lax.ppermute(value, "wide", pairs)
-
-
 def leg_c(node_ref, ops, scratch):
     rows = ops.shape[0]
     for a in range(16):
@@ -59,25 +58,32 @@
             out_ref[k, 0, :, c * 128 : (c + 1) * 128] = value
 
 
-def prep_kernel(node_ref, leg_a_ref, legs_ref, first_ref, cols_ref, ops_ref, tiles, wide_tiles, scratch, sem):
+def prep_kernel(node_hbm, legs_hbm, first_ref, cols_ref, ops_ref, node_ref, leg_a, tiles, wide_tiles, scratch, sems):
     wide, narrow = lax.axis_index("wide"), lax.axis_index("narrow")
     core = lax.rem(narrow, 2)
-    fetch = pltpu.make_async_copy(legs_ref.at[2, :, pl.ds(pl.multiple_of(wide * 16, 16), 16), :], tiles, sem)
-    fetch.start()
+    columns = pl.ds(pl.multiple_of(wide * 16, 16), 16)
+    fetch_a = pltpu.make_async_copy(legs_hbm.at[0], leg_a, sems.at[0])
+    fetch_c = pltpu.make_async_copy(legs_hbm.at[2, :, columns, :], tiles, sems.at[1])
+    fetch_node = pltpu.make_async_copy(node_hbm, node_ref, sems.at[2])
+    fetch_a.start()
+    fetch_c.start()
+    fetch_node.start()
     lane = lax.broadcasted_iota(jnp.int32, (256, 128), 1) % 32
     source = (narrow - core) * 16 + jnp.where(lane < 16, core * 16 + lane, (1 - core) * 16 + lane - 16)
     row = lax.broadcasted_iota(jnp.int32, (256, 128), 0)
     pick = jnp.where(row == source, 1.0, 0.0).astype(jnp.bfloat16)
+    fetch_a.wait()
     for i in range(12):
-        block = lax.dot_general(leg_a_ref[0, i], pick, NN, preferred_element_type=jnp.float32)
+        block = lax.dot_general(leg_a[i], pick, NN, preferred_element_type=jnp.float32)
         block = block.astype(jnp.bfloat16)
         cols_ref[i, :256] = block
         cols_ref[i, 256:] = block
-    fetch.wait()
+    fetch_c.wait()
     wide_tiles[...] = tiles[...].astype(jnp.float32)
     half = [wide_tiles[k, pl.ds(pl.multiple_of(core * 8, 8), 8), :] for k in range(12)]
     ops = jnp.concatenate(half, axis=0).astype(jnp.bfloat16)
     ops_ref[...] = ops
+    fetch_node.wait()
     leg_c(node_ref, ops, scratch)
     put_first(scratch, first_ref)
 
@@ -91,26 +97,24 @@
             jax.ShapeDtypeStruct((96, 256), jnp.bfloat16),
         ],
         grid=(1,),
-        in_specs=[
-            pl.BlockSpec((16, 256, 256), lambda g: (0, 0, 0)),
-            pl.BlockSpec((1, 12, 256, 256), lambda g: (0, 0, 0, 0)),
-            pl.BlockSpec(memory_space=pl.ANY),
-        ],
+        in_specs=[pl.BlockSpec(memory_space=pltpu.HBM)] * 2,
         out_specs=[
             pl.BlockSpec((12, 1, 128, 256), lambda g: (0, 0, 0, 0)),
             pl.BlockSpec((12, 512, 128), lambda g: (0, 0, 0)),
             pl.BlockSpec((96, 256), lambda g: (0, 0)),
         ],
         scratch_shapes=[
+            pltpu.VMEM((16, 256, 256), jnp.bfloat16),
+            pltpu.VMEM((12, 256, 256), jnp.bfloat16),
             pltpu.VMEM((12, 16, 256), jnp.bfloat16),
             pltpu.VMEM((12, 16, 256), jnp.float32),
             pltpu.VMEM((2, 1536, 128), jnp.float32),
-            pltpu.SemaphoreType.DMA(()),
+            pltpu.SemaphoreType.DMA((3,)),
         ],
-        compiler_params=grant(17),
+        compiler_params=grant(14),
         cost_estimate=pl.CostEstimate(flops=2 * 3072 * 256 * 300, bytes_accessed=6 << 20, transcendentals=0),
         name="prep",
-    )(node, leg_ops, leg_ops)
+    )(in_hbm(node), in_hbm(leg_ops))
 
 
 def sibling_kernel(node_ref, ops_ref, first_ref, out_ref, scratch):
@@ -157,10 +161,12 @@
         in_specs=[smem, smem],
         compiler_params=grant(1),
         name="own_rows",
-    )(op_index, offsets)
-
-
-def main_kernel(table, first_ref, ops_ref, cols_ref, keep_ref, m1_ref, m2_ref, m3_ref, second, a_abs, a_rel):
+    )(in_hbm(op_index), in_hbm(offsets))
+
+
+def main_kernel(table, first_ref, legs_hbm, cols_ref, keep_ref, m1_ref, m2_ref, m3_ref, leg_b, second, a_abs, a_rel, sem):
+    fetch = pltpu.make_async_copy(legs_hbm.at[1], leg_b, sem)
+    fetch.start()
     narrow = lax.axis_index("narrow")
     lane = lax.broadcasted_iota(jnp.int32, (16, 128), 1) // 32
 
@@ -187,11 +193,13 @@
         for g in range(16):
             a_rel[16 * blk : 16 * blk + 16, g * 128 : (g + 1) * 128] = a_abs[g, pl.ds(source, 16), :]
 
+    fetch.wait()
+
     def step(g, carry):
         for s in range(4):
             j, k = table[g, s * 4 + 1], table[g, s * 4 + 2]
             lhs = first_ref[k].reshape(256, 256)
-            value = lax.dot_general(lhs, ops_ref[0, j], NT, preferred_element_type=jnp.float32)
+            value = lax.dot_general(lhs, leg_b[j], NT, preferred_element_type=jnp.float32)
             value = value.astype(jnp.bfloat16)
             for half in range(2):
                 for q in range(8):
@@ -220,20 +228,22 @@
             grid=(1,),
             in_specs=[
                 pl.BlockSpec((12, 2, 128, 256), lambda g, s: (0, 0, 0, 0)),
-                pl.BlockSpec((1, 12, 256, 256), lambda g, s: (1, 0, 0, 0)),
+                pl.BlockSpec(memory_space=pltpu.HBM),
                 pl.BlockSpec((12, 512, 128), whole3),
             ],
             out_specs=[pl.BlockSpec((8, 64, 256), whole3)] * 4,
             scratch_shapes=[
+                pltpu.VMEM((12, 256, 256), jnp.bfloat16),
                 pltpu.VMEM((8, 2048, 256), jnp.bfloat16),
                 pltpu.VMEM((16, 256, 128), jnp.bfloat16),
                 pltpu.VMEM((256, 2048), jnp.bfloat16),
+                pltpu.SemaphoreType.DMA(()),
             ],
         ),
         compiler_params=grant(28),
         cost_estimate=pl.CostEstimate(flops=128 * 2 * 256**3, bytes_accessed=8 << 20, transcendentals=0),
         name="two_legs",
-    )(table, first, leg_ops, cols)
+    )(table, first, in_hbm(leg_ops), cols)
 
 
 def y_kernel(keep_ref, r1_ref, r2_ref, r3_ref, keep_out, m01_ref, m10_ref, m11_ref):
@@ -284,20 +294,22 @@
     )(keep, r01, r10, r11)
 
 
-def last_kernel(tau, own_ref, left_ref, right_ref, fl_ref, fr_ref, node_ref, side_ref, out_ref, sigma):
+def last_kernel(tau, n0, n2, l0, l2, r0, r2, fl, fr, f2, node_ref, side_ref, out_ref, sigma):
     f32 = jnp.float32
     wide = lax.axis_index("wide")
     z_hi, x = wide // 4, lax.rem(wide, 4)
     row = lax.broadcasted_iota(jnp.int32, (256, 256), 0)
     column = lax.broadcasted_iota(jnp.int32, (256, 256), 1)
     eye = jnp.where(row == column, 1.0, 0.0).astype(jnp.bfloat16)
+    pieces = []
+    for dx, near, far in ((0, n0, n2), (1, l0, l2), (3, r0, r2)):
+        pieces += [(dx, 0, near, 0), (dx, 1, near, 1), (dx, 3, near, 2), (dx, 2, far, 0)]
+    pieces += [(2, 0, fl, 0), (2, 1, fl, 1), (2, 3, fr, 0), (2, 2, f2, 0)]
     for r in range(ROWS):
-        for dz in range(4):
-            two = fl_ref[dz] if dz < 2 else fr_ref[dz - 2]
-            for dx, value in ((0, own_ref[dz]), (1, left_ref[dz]), (3, right_ref[dz]), (2, two)):
-                w = lax.rem(z_hi - dz + 4, 4) * 4 + lax.rem(x - dx + 4, 4)
-                place = pl.ds(pl.multiple_of(w * 16, 16), 16)
-                sigma[r, place, :] = value[r * 16 : (r + 1) * 16]
+        for dx, dz, ref, slot in pieces:
+            w = lax.rem(z_hi - dz + 4, 4) * 4 + lax.rem(x - dx + 4, 4)
+            place = pl.ds(pl.multiple_of(w * 16, 16), 16)
+            sigma[r, place, :] = ref[slot, r * 16 : (r + 1) * 16]
     for r in range(ROWS):
         turned = lax.dot_general(eye, sigma[r], NT, preferred_element_type=f32)
         out_ref[r] = node_ref[r].astype(f32) + tau * (side_ref[r].astype(f32) - turned)
@@ -306,7 +318,7 @@
 ROWS = 4
 
 
-def last_of(tau, own, left, right, fl, fr, node, side):
+def last_of(tau, pieces, node, side):
     def piece(n):
         return pl.BlockSpec((n, ROWS * 16, 256), lambda r: (0, r, 0))
 
@@ -315,19 +327,19 @@
         functools.partial(last_kernel, tau),
         out_shape=jax.ShapeDtypeStruct((16, 256, 256), jnp.float32),
         grid=(16 // ROWS,),
-        in_specs=[piece(4), piece(4), piece(4), piece(2), piece(2), row, row],
+        in_specs=[piece(p.shape[0]) for p in pieces] + [row, row],
         out_specs=row,
         scratch_shapes=[pltpu.VMEM((ROWS, 256, 256), jnp.bfloat16)],
         compiler_params=grant(16),
         name="update",
-    )(own, left, right, fl, fr, node, side)
+    )(*pieces, node, side)
 
 
 def per_device(node, right_side, leg_ops, op_index, offsets):
     tau = 0.5 / math.sqrt(op_index.shape[0] * lax.axis_size("wide"))
     table = own_rows(op_index, offsets)
-    for step in range(4):
-        table = table + swap_wide(table, 1 << step)
+    for axis in ("x", "z_hi"):
+        table = table + sum(send(table, **{f"d{axis}": d}) for d in (1, 3, 2))
     sibling = send(node, dcore=1)
     first, cols, ops_c = prep(node, leg_ops)
     first = add_sibling(sibling, ops_c, first)
@@ -336,11 +348,15 @@
     keep, m01, m10, m11 = y_sum(keep, r1, r2, r3)
     r10, r11, r01 = send(m10, dz_lo=1), send(m11, dz_lo=1, dcore=1), send(m01, dcore=1)
     piece = z_sum(keep, r01, r10, r11)
-    got = [piece] + [send(piece, dz_hi=d) for d in (1, 2, 3)]
-    got = jnp.stack(got)
-    left, right = send(got, dx=1), send(got, dx=3)
-    fl, fr = send(left[:2], dx=1), send(right[2:], dx=3)
-    return last_of(tau, got, left, right, fl, fr, node, right_side)
+    piece = piece[None]
+    z1, z3 = send(piece, dz_hi=1), send(piece, dz_hi=3)
+    near = jnp.concatenate([piece, z1, z3])
+    l0, r0 = send(near, dx=1), send(near, dx=3)
+    fa, fb = send(z1[:, :128], dz_hi=1), send(z3[:, 128:], dz_hi=3)
+    far = jnp.concatenate([fa, fb], axis=1)
+    l2, r2, f2 = send(far, dx=1), send(far, dx=3), send(far, dx=2)
+    fl, fr = send(l0[:2], dx=1), send(r0[2:], dx=3)
+    return last_of(tau, (near, far, l0, l2, r0, r2, fl, fr, f2), node, right_side)
 
 
 def solution(mesh):

time: 108 us -> 95.7 us (0.89)
  waiting for transfers between devices: 50.1 us -> 36.8 us
  local copies, waits for them, and re-layouts: 6.54 us -> 0.06 us
  starting transfers between devices: 33.5 us -> 39.4 us
  Pallas kernels: 17.4 us -> 19.1 us
    ppermute x14 -> x24, starting transfers between devices: 19.6 us -> 39.4 us  [send(): return lax.ppermute(value, ('wide', 'narrow'), pairs_of(move))]
    ppermute x4 -> x0, starting transfers between devices: 13.8 us -> none  [swap_wide(): return lax.ppermute(value, 'wide', pairs)]
    ppermute x14 -> x24, waiting for transfers between devices: 44.2 us -> 36.8 us  [send(): return lax.ppermute(value, ('wide', 'narrow'), pairs_of(move))]
    unnamed x14 -> x5, local copies, waits for them, and re-layouts: 6.5 us -> 0.02 us
    ppermute x4 -> x0, waiting for transfers between devices: 5.93 us -> none  [swap_wide(): return lax.ppermute(value, 'wide', pairs)]
    pallas_call x1, Pallas kernels: 1.69 us -> 3.23 us  [prep(): pl.pallas_call(prep_kernel, out_shape=[jax.ShapeDtypeStruct((12, 2, 128,...]
  transfers between devices with their start and end apart: 18 -> 24, of which waited for: 13 -> 14; matrix products, arithmetic and copies ran while one was open for 0% -> 0% of each run, Pallas kernels for 2% -> 4%
where the time goes in v1:
time: 95.7 us; the launch traced here: 95.6 us
  starting transfers between devices  39.4 us (41%)
  waiting for transfers between devices  36.8 us (38%)
  Pallas kernels  19.1 us (20%)
    ppermute x24, starting transfers between devices, send(): return lax.ppermute(value, ('wide', 'narrow'), pairs_of(move))  39.4 us
    ppermute x24, waiting for transfers between devices, send(): return lax.ppermute(value, ('wide', 'narrow'), pairs_of(move))  36.8 us
    pallas_call x1, Pallas kernels, main_of(): pl.pallas_call(main_kernel, out_shape=[jax.ShapeDtypeStruct((8, 64, 256),...  10.3 us
    pallas_call x1, Pallas kernels, last_of(): pl.pallas_call(functools.partial(last_kernel, tau), out_shape=jax.ShapeDt...  3.52 us
    pallas_call x1, Pallas kernels, prep(): pl.pallas_call(prep_kernel, out_shape=[jax.ShapeDtypeStruct((12, 2, 128,...  3.23 us
  transfers between devices with their start and end apart: 24, of which 14 were waited for; matrix products, arithmetic and copies ran while one was open for 0% of the time, Pallas kernels for 4%

profile of v1, /device:TPU:32, one launch (start us, length us, event | category | flops | bytes accessed | tf_op | source)
XLA Modules:
  0.0 95.6 jit_solution(7671790862801279009)
XLA Ops:
  0.7 3.1 %collective-permute-start.2 = (s32[16,128]{1,0:T(8,128)S(1)}, s32[16,128]{1,0:T(8,128)S(1)}, u32[]{:S(2)}, u32[]{:S(2)}) collective-permute-start(s32[16,128]{1,0:T(8,128)S(1)} %own_rows.1), channel_id=1, source_target_pairs={{0,32},{1,33},{2,34},{3,35},{4,36},{5,37},{6,38},{7,39},{8,40},{9,... | collective-permute-start | bytes 24584 | tf_op jit(solution)/shard_map/ppermute | solution.py:43
  3.8 1.1 %collective-permute-start.1 = (s32[16,128]{1,0:T(8,128)S(1)}, s32[16,128]{1,0:T(8,128)S(1)}, u32[]{:S(2)}, u32[]{:S(2)}) collective-permute-start(s32[16,128]{1,0:T(8,128)S(1)} %own_rows.1), channel_id=1, source_target_pairs={{0,48},{1,49},{2,50},{3,51},{4,52},{5,53},{6,54},{7,55},{8,56},{9,... | collective-permute-start | bytes 24584 | tf_op jit(solution)/shard_map/ppermute | solution.py:43
  5.0 0.9 collective-permute-start
  6.0 1.5 %collective-permute-done.1 = s32[16,128]{1,0:T(8,128)S(1)} collective-permute-done((s32[16,128]{1,0:T(8,128)S(1)}, s32[16,128]{1,0:T(8,128)S(1)}, u32[]{:S(2)}, u32[]{:S(2)}) %collective-permute-start.1) | collective-permute-done | bytes 8224 | tf_op jit(solution)/shard_map/ppermute | solution.py:43
  7.5 2.4 %collective-permute-done = s32[16,128]{1,0:T(8,128)S(1)} collective-permute-done((s32[16,128]{1,0:T(8,128)S(1)}, s32[16,128]{1,0:T(8,128)S(1)}, u32[]{:S(2)}, u32[]{:S(2)}) %collective-permute-start) | collective-permute-done | bytes 8224 | tf_op jit(solution)/shard_map/ppermute | solution.py:43
  9.8 6.3 %collective-permute-start.5 = (s32[16,128]{1,0:T(8,128)S(1)}, s32[16,128]{1,0:T(8,128)S(1)}, u32[]{:S(2)}, u32[]{:S(2)}) collective-permute-start(s32[16,128]{1,0:T(8,128)S(1)} %add_add_fusion.1), channel_id=1, source_target_pairs={{0,128},{1,129},{2,130},{3,131},{4,132},{5,133},{6,134},{7,135},{8... | collective-permute-start | bytes 24584 | tf_op jit(solution)/shard_map/ppermute | solution.py:43
  16.7 2.4 %collective-permute-start.3 = (s32[16,128]{1,0:T(8,128)S(1)}, s32[16,128]{1,0:T(8,128)S(1)}, u32[]{:S(2)}, u32[]{:S(2)}) collective-permute-start(s32[16,128]{1,0:T(8,128)S(1)} %add_add_fusion.1), channel_id=1, source_target_pairs={{0,64},{1,65},{2,66},{3,67},{4,68},{5,69},{6,70},{7,71},{8,72},{9,... | collective-permute-start | bytes 24584 | tf_op jit(solution)/shard_map/ppermute | solution.py:43
  19.1 3.2 %prep.1 = (bf16[12,2,128,256]{3,2,1,0:T(8,128)(2,1)S(1)}, bf16[12,512,128]{2,1,0:T(8,128)(2,1)S(1)}, bf16[96,256]{1,0:T(8,128)(2,1)S(1)}) custom-call(bf16[16,256,256]{2,1,0:T(8,128)(2,1)} %node_ref.1, bf16[3,12,256,256]{3,2,1,0:T(8,128)(2,1)} %legs_hbm.3), custom_call_target="tpu_custom_call" | custom-call | flops 471859200 | bytes 6291456 | tf_op jit(solution)/shard_map/prep/pallas_call | solution.py:92
  22.5 1.1 %sibling.1.first_ref = bf16[12,2,128,256]{3,2,1,0:T(8,128)(2,1)S(1)} custom-call(bf16[16,256,256]{2,1,0:T(8,128)(2,1)S(1)} %collective-permute-done.6.node_ref, bf16[96,256]{1,0:T(8,128)(2,1)S(1)} %get-tuple-element.16.ops_ref, bf16[12,2,128,256]{3,2,1,0:T(8,128)(2,1)S(1)} %get-tuple-element.17.first_ref), custom_call_target="tpu_custom_call", output_to_operand_aliasing={{}: (2, {})} | custom-call | flops 201326592 | bytes 3145728 | tf_op jit(solution)/shard_map/sibling/pallas_call | solution.py:127
  23.6 10.3 %two_legs.1 = (f32[8,64,256]{2,1,0:T(8,128)S(1)}, bf16[8,64,256]{2,1,0:T(8,128)(2,1)S(1)}, bf16[8,64,256]{2,1,0:T(8,128)(2,1)S(1)}, bf16[8,64,256]{2,1,0:T(8,128)(2,1)S(1)}) custom-call(s32[16,128]{1,0:T(8,128)S(1)} %add_add_fusion.table, bf16[12,2,128,256]{3,2,1,0:T(8,128)(2,1)S(1)} %sibling.1.first_ref, bf16[3,12,256,256]{3,2,1,0:T(8,128)(2,1)} %legs_hbm.3, ...), custom_call_target="tpu_custom_call" | custom-call | flops 4294967296 | bytes 8388608 | tf_op jit(solution)/shard_map/two_legs/pallas_call | solution.py:222
  33.9 1.7 %collective-permute-start.7 = (bf16[8,64,256]{2,1,0:T(8,128)(2,1)S(1)}, bf16[8,64,256]{2,1,0:T(8,128)(2,1)S(1)}, u32[]{:S(2)}, u32[]{:S(2)}) collective-permute-start(bf16[8,64,256]{2,1,0:T(8,128)(2,1)S(1)} %get-tuple-element.20), channel_id=1, source_target_pairs={{0,2},{1,3},{2,4},{3,5},{4,6},{5,7},{6,0},{7,1},{8,10},{9,11},{10,... | collective-permute-start | bytes 786440 | tf_op jit(solution)/shard_map/ppermute | solution.py:43
  35.5 2.9 %collective-permute-start.8 = (bf16[8,64,256]{2,1,0:T(8,128)(2,1)S(1)}, bf16[8,64,256]{2,1,0:T(8,128)(2,1)S(1)}, u32[]{:S(2)}, u32[]{:S(2)}) collective-permute-start(bf16[8,64,256]{2,1,0:T(8,128)(2,1)S(1)} %get-tuple-element.21), channel_id=1, source_target_pairs={{0,4},{1,5},{2,6},{3,7},{4,0},{5,1},{6,2},{7,3},{8,12},{9,13},{10,... | collective-permute-start | bytes 786440 | tf_op jit(solution)/shard_map/ppermute | solution.py:43
  38.4 1.3 %collective-permute-start.9 = (bf16[8,64,256]{2,1,0:T(8,128)(2,1)S(1)}, bf16[8,64,256]{2,1,0:T(8,128)(2,1)S(1)}, u32[]{:S(2)}, u32[]{:S(2)}) collective-permute-start(bf16[8,64,256]{2,1,0:T(8,128)(2,1)S(1)} %get-tuple-element.22), channel_id=1, source_target_pairs={{0,6},{1,7},{2,0},{3,1},{4,2},{5,3},{6,4},{7,5},{8,14},{9,15},{10,... | collective-permute-start | bytes 786440 | tf_op jit(solution)/shard_map/ppermute | solution.py:43
  39.8 3.9 %collective-permute-done.7.r1_ref = bf16[8,64,256]{2,1,0:T(8,128)(2,1)S(1)} collective-permute-done((bf16[8,64,256]{2,1,0:T(8,128)(2,1)S(1)}, bf16[8,64,256]{2,1,0:T(8,128)(2,1)S(1)}, u32[]{:S(2)}, u32[]{:S(2)}) %collective-permute-start.7) | collective-permute-done | bytes 262176 | tf_op jit(solution)/shard_map/ppermute | solution.py:43
  43.7 4.4 %collective-permute-done.8.r2_ref = bf16[8,64,256]{2,1,0:T(8,128)(2,1)S(1)} collective-permute-done((bf16[8,64,256]{2,1,0:T(8,128)(2,1)S(1)}, bf16[8,64,256]{2,1,0:T(8,128)(2,1)S(1)}, u32[]{:S(2)}, u32[]{:S(2)}) %collective-permute-start.8) | collective-permute-done | bytes 262176 | tf_op jit(solution)/shard_map/ppermute | solution.py:43
  48.3 1.3 %collective-permute-start.11 = (bf16[8,16,256]{2,1,0:T(8,128)(2,1)S(1)}, bf16[8,16,256]{2,1,0:T(8,128)(2,1)S(1)}, u32[]{:S(2)}, u32[]{:S(2)}) collective-permute-start(bf16[8,16,256]{2,1,0:T(8,128)(2,1)S(1)} %get-tuple-element.25), channel_id=1, source_target_pairs={{0,8},{1,9},{2,10},{3,11},{4,12},{5,13},{6,14},{7,15},{8,0},{9,1},... | collective-permute-start | bytes 196616 | tf_op jit(solution)/shard_map/ppermute | solution.py:43
  50.2 2.9 %collective-permute-done.11.r10_ref = bf16[8,16,256]{2,1,0:T(8,128)(2,1)S(1)} collective-permute-done((bf16[8,16,256]{2,1,0:T(8,128)(2,1)S(1)}, bf16[8,16,256]{2,1,0:T(8,128)(2,1)S(1)}, u32[]{:S(2)}, u32[]{:S(2)}) %collective-permute-start.11) | collective-permute-done | bytes 65568 | tf_op jit(solution)/shard_map/ppermute | solution.py:43
  53.1 0.9 collective-permute-done.12.r11_ref
  54.1 1.6 %collective-permute-start.14 = (bf16[1,256,256]{2,1,0:T(8,128)(2,1)S(1)}, bf16[1,256,256]{2,1,0:T(8,128)(2,1)S(1)}, u32[]{:S(2)}, u32[]{:S(2)}) collective-permute-start(bf16[1,256,256]{2,1,0:T(8,128)(2,1)S(1)} %bitcast.1), channel_id=1, source_target_pairs={{0,192},{1,193},{2,194},{3,195},{4,196},{5,197},{6,198},{7,199},{8... | collective-permute-start | bytes 393224 | tf_op jit(solution)/shard_map/ppermute | solution.py:43
  55.7 1.4 %collective-permute-start.13 = (bf16[1,256,256]{2,1,0:T(8,128)(2,1)S(1)}, bf16[1,256,256]{2,1,0:T(8,128)(2,1)S(1)}, u32[]{:S(2)}, u32[]{:S(2)}) collective-permute-start(bf16[1,256,256]{2,1,0:T(8,128)(2,1)S(1)} %bitcast.2), channel_id=1, source_target_pairs={{0,64},{1,65},{2,66},{3,67},{4,68},{5,69},{6,70},{7,71},{8,72},{9,... | collective-permute-start | bytes 393224 | tf_op jit(solution)/shard_map/ppermute | solution.py:43
  57.1 3.6 %collective-permute-done.14 = bf16[1,256,256]{2,1,0:T(8,128)(2,1)S(1)} collective-permute-done((bf16[1,256,256]{2,1,0:T(8,128)(2,1)S(1)}, bf16[1,256,256]{2,1,0:T(8,128)(2,1)S(1)}, u32[]{:S(2)}, u32[]{:S(2)}) %collective-permute-start.14) | collective-permute-done | bytes 131104 | tf_op jit(solution)/shard_map/ppermute | solution.py:43
  60.8 5.3 %collective-permute-done.13 = bf16[1,256,256]{2,1,0:T(8,128)(2,1)S(1)} collective-permute-done((bf16[1,256,256]{2,1,0:T(8,128)(2,1)S(1)}, bf16[1,256,256]{2,1,0:T(8,128)(2,1)S(1)}, u32[]{:S(2)}, u32[]{:S(2)}) %collective-permute-start.13) | collective-permute-done | bytes 131104 | tf_op jit(solution)/shard_map/ppermute | solution.py:43
  66.2 3.2 %collective-permute-start.19 = (bf16[3,256,256]{2,1,0:T(8,128)(2,1)S(1)}, bf16[3,256,256]{2,1,0:T(8,128)(2,1)S(1)}, u32[]{:S(2)}, u32[]{:S(2)}) collective-permute-start(bf16[3,256,256]{2,1,0:T(8,128)(2,1)S(1)} %pad_maximum_fusion.n0), channel_id=1, source_target_pairs={{0,48},{1,49},{2,50},{3,51},{4,52},{5,53},{6,54},{7,55},{8,56},{9,... | collective-permute-start | bytes 1179656 | tf_op jit(solution)/shard_map/ppermute | solution.py:43
  69.6 4.0 %collective-permute-start.16 = (bf16[1,128,256]{2,1,0:T(8,128)(2,1)S(1)}, bf16[1,128,256]{2,1,0:T(8,128)(2,1)S(1)}, u32[]{:S(2)}, u32[]{:S(2)}) collective-permute-start(bf16[1,128,256]{2,1,0:T(8,128)(2,1)S(1)} %slice.17), channel_id=1, source_target_pairs={{0,192},{1,193},{2,194},{3,195},{4,196},{5,197},{6,198},{7,199},{8... | collective-permute-start | bytes 196616 | tf_op jit(solution)/shard_map/ppermute | solution.py:43
  73.6 4.5 %collective-permute-done.17.l0 = bf16[3,256,256]{2,1,0:T(8,128)(2,1)S(1)} collective-permute-done((bf16[3,256,256]{2,1,0:T(8,128)(2,1)S(1)}, bf16[3,256,256]{2,1,0:T(8,128)(2,1)S(1)}, u32[]{:S(2)}, u32[]{:S(2)}) %collective-permute-start.17) | collective-permute-done | bytes 393248 | tf_op jit(solution)/shard_map/ppermute | solution.py:43
  78.3 1.1 %collective-permute-start.23 = (bf16[1,256,256]{2,1,0:T(8,128)(2,1)S(1)}, bf16[1,256,256]{2,1,0:T(8,128)(2,1)S(1)}, u32[]{:S(2)}, u32[]{:S(2)}) collective-permute-start(bf16[1,256,256]{2,1,0:T(8,128)(2,1)S(1)} %constant_dynamic-update-slice_fusion.n2), channel_id=1, source_target_pairs={{0,32},{1,33},{2,34},{3,35},{4,36},{5,37},{6,38},{7,39},{8,40},{9,... | collective-permute-start | bytes 393224 | tf_op jit(solution)/shard_map/ppermute | solution.py:43
  79.3 2.3 %collective-permute-start.20 = (bf16[1,256,256]{2,1,0:T(8,128)(2,1)S(1)}, bf16[1,256,256]{2,1,0:T(8,128)(2,1)S(1)}, u32[]{:S(2)}, u32[]{:S(2)}) collective-permute-start(bf16[1,256,256]{2,1,0:T(8,128)(2,1)S(1)} %constant_dynamic-update-slice_fusion.n2), channel_id=1, source_target_pairs={{0,48},{1,49},{2,50},{3,51},{4,52},{5,53},{6,54},{7,55},{8,56},{9,... | collective-permute-start | bytes 393224 | tf_op jit(solution)/shard_map/ppermute | solution.py:43
  81.7 0.8 collective-permute-start.18
  82.5 2.5 %collective-permute-start.22 = (bf16[1,256,256]{2,1,0:T(8,128)(2,1)S(1)}, bf16[1,256,256]{2,1,0:T(8,128)(2,1)S(1)}, u32[]{:S(2)}, u32[]{:S(2)}) collective-permute-start(bf16[1,256,256]{2,1,0:T(8,128)(2,1)S(1)} %slice.19), channel_id=1, source_target_pairs={{0,48},{1,49},{2,50},{3,51},{4,52},{5,53},{6,54},{7,55},{8,56},{9,... | collective-permute-start | bytes 393224 | tf_op jit(solution)/shard_map/ppermute | solution.py:43
  85.0 3.5 %collective-permute-done.23.f2 = bf16[1,256,256]{2,1,0:T(8,128)(2,1)S(1)} collective-permute-done((bf16[1,256,256]{2,1,0:T(8,128)(2,1)S(1)}, bf16[1,256,256]{2,1,0:T(8,128)(2,1)S(1)}, u32[]{:S(2)}, u32[]{:S(2)}) %collective-permute-start.23) | collective-permute-done | bytes 131104 | tf_op jit(solution)/shard_map/ppermute | solution.py:43
  88.6 3.5 %collective-permute-done.18.l2 = bf16[1,256,256]{2,1,0:T(8,128)(2,1)S(1)} collective-permute-done((bf16[1,256,256]{2,1,0:T(8,128)(2,1)S(1)}, bf16[1,256,256]{2,1,0:T(8,128)(2,1)S(1)}, u32[]{:S(2)}, u32[]{:S(2)}) %collective-permute-start.18) | collective-permute-done | bytes 131104 | tf_op jit(solution)/shard_map/ppermute | solution.py:43
  92.1 3.5 %update.1 = f32[16,256,256]{2,1,0:T(8,128)} custom-call(bf16[3,256,256]{2,1,0:T(8,128)(2,1)S(1)} %pad_maximum_fusion.n0, bf16[1,256,256]{2,1,0:T(8,128)(2,1)S(1)} %constant_dynamic-update-slice_fusion.n2, bf16[3,256,256]{2,1,0:T(8,128)(2,1)S(1)} %collective-permute-done.17.l0, bf16[1,256,256]{2,1,0:T(8,128)(2,1)S(1)} %collective-permute-done.18.l2, ...), custom_call_target="tpu_custom_call" | custom-call | tf_op jit(solution)/shard_map/update/pallas_call | solution.py:326
  (36 shorter events, 2.9 us)
Async XLA Ops:
  0.0 22.5 %collective-permute-start.6 = (bf16[16,256,256]{2,1,0:T(8,128)(2,1)}, bf16[16,256,256]{2,1,0:T(8,128)(2,1)S(1)}, u32[]{:S(2)}, u32[]{:S(2)}) collective-permute-start(bf16[16,256,256]{2,1,0:T(8,128)(2,1)} %node_ref.1), channel_id=1, source_target_pairs={{0,1},{1,0},{2,3},{3,2},{4,5},{5,4},{6,7},{7,6},{8,9},{9,8},{10,11... | collective-permute-start | bytes 6291464 | tf_op jit(solution)/shard_map/ppermute | solution.py:43
  0.7 5.2 %collective-permute-start.2 = (s32[16,128]{1,0:T(8,128)S(1)}, s32[16,128]{1,0:T(8,128)S(1)}, u32[]{:S(2)}, u32[]{:S(2)}) collective-permute-start(s32[16,128]{1,0:T(8,128)S(1)} %own_rows.1), channel_id=1, source_target_pairs={{0,32},{1,33},{2,34},{3,35},{4,36},{5,37},{6,38},{7,39},{8,40},{9,... | collective-permute-start | bytes 24584 | tf_op jit(solution)/shard_map/ppermute | solution.py:43
  3.8 3.7 %collective-permute-start.1 = (s32[16,128]{1,0:T(8,128)S(1)}, s32[16,128]{1,0:T(8,128)S(1)}, u32[]{:S(2)}, u32[]{:S(2)}) collective-permute-start(s32[16,128]{1,0:T(8,128)S(1)} %own_rows.1), channel_id=1, source_target_pairs={{0,48},{1,49},{2,50},{3,51},{4,52},{5,53},{6,54},{7,55},{8,56},{9,... | collective-permute-start | bytes 24584 | tf_op jit(solution)/shard_map/ppermute | solution.py:43
  5.0 4.9 %collective-permute-start = (s32[16,128]{1,0:T(8,128)S(1)}, s32[16,128]{1,0:T(8,128)S(1)}, u32[]{:S(2)}, u32[]{:S(2)}) collective-permute-start(s32[16,128]{1,0:T(8,128)S(1)} %own_rows.1), channel_id=1, source_target_pairs={{0,16},{1,17},{2,18},{3,19},{4,20},{5,21},{6,22},{7,23},{8,24},{9,... | collective-permute-start | bytes 24584 | tf_op jit(solution)/shard_map/ppermute | solution.py:43
  9.8 12.5 %collective-permute-start.5 = (s32[16,128]{1,0:T(8,128)S(1)}, s32[16,128]{1,0:T(8,128)S(1)}, u32[]{:S(2)}, u32[]{:S(2)}) collective-permute-start(s32[16,128]{1,0:T(8,128)S(1)} %add_add_fusion.1), channel_id=1, source_target_pairs={{0,128},{1,129},{2,130},{3,131},{4,132},{5,133},{6,134},{7,135},{8... | collective-permute-start | bytes 24584 | tf_op jit(solution)/shard_map/ppermute | solution.py:43
  16.1 6.2 %collective-permute-start.4 = (s32[16,128]{1,0:T(8,128)S(1)}, s32[16,128]{1,0:T(8,128)S(1)}, u32[]{:S(2)}, u32[]{:S(2)}) collective-permute-start(s32[16,128]{1,0:T(8,128)S(1)} %add_add_fusion.1), channel_id=1, source_target_pairs={{0,192},{1,193},{2,194},{3,195},{4,196},{5,197},{6,198},{7,199},{8... | collective-permute-start | bytes 24584 | tf_op jit(solution)/shard_map/ppermute | solution.py:43
  16.7 5.8 %collective-permute-start.3 = (s32[16,128]{1,0:T(8,128)S(1)}, s32[16,128]{1,0:T(8,128)S(1)}, u32[]{:S(2)}, u32[]{:S(2)}) collective-permute-start(s32[16,128]{1,0:T(8,128)S(1)} %add_add_fusion.1), channel_id=1, source_target_pairs={{0,64},{1,65},{2,66},{3,67},{4,68},{5,69},{6,70},{7,71},{8,72},{9,... | collective-permute-start | bytes 24584 | tf_op jit(solution)/shard_map/ppermute | solution.py:43
  23.6 68.5 %copy-start.1 = (bf16[16,256,256]{2,1,0:T(8,128)(2,1)S(1)}, bf16[16,256,256]{2,1,0:T(8,128)(2,1)}, u32[]{:S(2)}) copy-start(bf16[16,256,256]{2,1,0:T(8,128)(2,1)} %side_ref.1) | copy-start | bytes 6291460
  33.9 58.2 %copy-start = (bf16[16,256,256]{2,1,0:T(8,128)(2,1)S(1)}, bf16[16,256,256]{2,1,0:T(8,128)(2,1)}, u32[]{:S(2)}) copy-start(bf16[16,256,256]{2,1,0:T(8,128)(2,1)} %node_ref.1) | copy-start | bytes 6291460
  33.9 9.8 %collective-permute-start.7 = (bf16[8,64,256]{2,1,0:T(8,128)(2,1)S(1)}, bf16[8,64,256]{2,1,0:T(8,128)(2,1)S(1)}, u32[]{:S(2)}, u32[]{:S(2)}) collective-permute-start(bf16[8,64,256]{2,1,0:T(8,128)(2,1)S(1)} %get-tuple-element.20), channel_id=1, source_target_pairs={{0,2},{1,3},{2,4},{3,5},{4,6},{5,7},{6,0},{7,1},{8,10},{9,11},{10,... | collective-permute-start | bytes 786440 | tf_op jit(solution)/shard_map/ppermute | solution.py:43
  35.5 12.6 %collective-permute-start.8 = (bf16[8,64,256]{2,1,0:T(8,128)(2,1)S(1)}, bf16[8,64,256]{2,1,0:T(8,128)(2,1)S(1)}, u32[]{:S(2)}, u32[]{:S(2)}) collective-permute-start(bf16[8,64,256]{2,1,0:T(8,128)(2,1)S(1)} %get-tuple-element.21), channel_id=1, source_target_pairs={{0,4},{1,5},{2,6},{3,7},{4,0},{5,1},{6,2},{7,3},{8,12},{9,13},{10,... | collective-permute-start | bytes 786440 | tf_op jit(solution)/shard_map/ppermute | solution.py:43
  38.4 9.7 %collective-permute-start.9 = (bf16[8,64,256]{2,1,0:T(8,128)(2,1)S(1)}, bf16[8,64,256]{2,1,0:T(8,128)(2,1)S(1)}, u32[]{:S(2)}, u32[]{:S(2)}) collective-permute-start(bf16[8,64,256]{2,1,0:T(8,128)(2,1)S(1)} %get-tuple-element.22), channel_id=1, source_target_pairs={{0,6},{1,7},{2,0},{3,1},{4,2},{5,3},{6,4},{7,5},{8,14},{9,15},{10,... | collective-permute-start | bytes 786440 | tf_op jit(solution)/shard_map/ppermute | solution.py:43
  48.2 2.0 %collective-permute-start.10 = (bf16[8,16,256]{2,1,0:T(8,128)(2,1)S(1)}, bf16[8,16,256]{2,1,0:T(8,128)(2,1)S(1)}, u32[]{:S(2)}, u32[]{:S(2)}) collective-permute-start(bf16[8,16,256]{2,1,0:T(8,128)(2,1)S(1)} %get-tuple-element.24), channel_id=1, source_target_pairs={{0,1},{1,0},{2,3},{3,2},{4,5},{5,4},{6,7},{7,6},{8,9},{9,8},{10,11... | collective-permute-start | bytes 196616 | tf_op jit(solution)/shard_map/ppermute | solution.py:43
  48.3 4.8 %collective-permute-start.11 = (bf16[8,16,256]{2,1,0:T(8,128)(2,1)S(1)}, bf16[8,16,256]{2,1,0:T(8,128)(2,1)S(1)}, u32[]{:S(2)}, u32[]{:S(2)}) collective-permute-start(bf16[8,16,256]{2,1,0:T(8,128)(2,1)S(1)} %get-tuple-element.25), channel_id=1, source_target_pairs={{0,8},{1,9},{2,10},{3,11},{4,12},{5,13},{6,14},{7,15},{8,0},{9,1},... | collective-permute-start | bytes 196616 | tf_op jit(solution)/shard_map/ppermute | solution.py:43
  49.6 4.4 %collective-permute-start.12 = (bf16[8,16,256]{2,1,0:T(8,128)(2,1)S(1)}, bf16[8,16,256]{2,1,0:T(8,128)(2,1)S(1)}, u32[]{:S(2)}, u32[]{:S(2)}) collective-permute-start(bf16[8,16,256]{2,1,0:T(8,128)(2,1)S(1)} %get-tuple-element.26), channel_id=1, source_target_pairs={{0,9},{1,8},{2,11},{3,10},{4,13},{5,12},{6,15},{7,14},{8,1},{9,0},... | collective-permute-start | bytes 196616 | tf_op jit(solution)/shard_map/ppermute | solution.py:43
  54.1 6.6 %collective-permute-start.14 = (bf16[1,256,256]{2,1,0:T(8,128)(2,1)S(1)}, bf16[1,256,256]{2,1,0:T(8,128)(2,1)S(1)}, u32[]{:S(2)}, u32[]{:S(2)}) collective-permute-start(bf16[1,256,256]{2,1,0:T(8,128)(2,1)S(1)} %bitcast.1), channel_id=1, source_target_pairs={{0,192},{1,193},{2,194},{3,195},{4,196},{5,197},{6,198},{7,199},{8... | collective-permute-start | bytes 393224 | tf_op jit(solution)/shard_map/ppermute | solution.py:43
  55.7 10.4 %collective-permute-start.13 = (bf16[1,256,256]{2,1,0:T(8,128)(2,1)S(1)}, bf16[1,256,256]{2,1,0:T(8,128)(2,1)S(1)}, u32[]{:S(2)}, u32[]{:S(2)}) collective-permute-start(bf16[1,256,256]{2,1,0:T(8,128)(2,1)S(1)} %bitcast.2), channel_id=1, source_target_pairs={{0,64},{1,65},{2,66},{3,67},{4,68},{5,69},{6,70},{7,71},{8,72},{9,... | collective-permute-start | bytes 393224 | tf_op jit(solution)/shard_map/ppermute | solution.py:43
  66.1 12.0 %collective-permute-start.17 = (bf16[3,256,256]{2,1,0:T(8,128)(2,1)S(1)}, bf16[3,256,256]{2,1,0:T(8,128)(2,1)S(1)}, u32[]{:S(2)}, u32[]{:S(2)}) collective-permute-start(bf16[3,256,256]{2,1,0:T(8,128)(2,1)S(1)} %pad_maximum_fusion.n0), channel_id=1, source_target_pairs={{0,16},{1,17},{2,18},{3,19},{4,20},{5,21},{6,22},{7,23},{8,24},{9,... | collective-permute-start | bytes 1179656 | tf_op jit(solution)/shard_map/ppermute | solution.py:43
  66.2 16.2 %collective-permute-start.19 = (bf16[3,256,256]{2,1,0:T(8,128)(2,1)S(1)}, bf16[3,256,256]{2,1,0:T(8,128)(2,1)S(1)}, u32[]{:S(2)}, u32[]{:S(2)}) collective-permute-start(bf16[3,256,256]{2,1,0:T(8,128)(2,1)S(1)} %pad_maximum_fusion.n0), channel_id=1, source_target_pairs={{0,48},{1,49},{2,50},{3,51},{4,52},{5,53},{6,54},{7,55},{8,56},{9,... | collective-permute-start | bytes 1179656 | tf_op jit(solution)/shard_map/ppermute | solution.py:43
  69.5 8.8 %collective-permute-start.15 = (bf16[1,128,256]{2,1,0:T(8,128)(2,1)S(1)}, bf16[1,128,256]{2,1,0:T(8,128)(2,1)S(1)}, u32[]{:S(2)}, u32[]{:S(2)}) collective-permute-start(bf16[1,128,256]{2,1,0:T(8,128)(2,1)S(1)} %slice.16), channel_id=1, source_target_pairs={{0,64},{1,65},{2,66},{3,67},{4,68},{5,69},{6,70},{7,71},{8,72},{9,... | collective-permute-start | bytes 196616 | tf_op jit(solution)/shard_map/ppermute | solution.py:43
  69.6 8.7 %collective-permute-start.16 = (bf16[1,128,256]{2,1,0:T(8,128)(2,1)S(1)}, bf16[1,128,256]{2,1,0:T(8,128)(2,1)S(1)}, u32[]{:S(2)}, u32[]{:S(2)}) collective-permute-start(bf16[1,128,256]{2,1,0:T(8,128)(2,1)S(1)} %slice.17), channel_id=1, source_target_pairs={{0,192},{1,193},{2,194},{3,195},{4,196},{5,197},{6,198},{7,199},{8... | collective-permute-start | bytes 196616 | tf_op jit(solution)/shard_map/ppermute | solution.py:43
  78.1 13.9 %collective-permute-start.21 = (bf16[2,256,256]{2,1,0:T(8,128)(2,1)S(1)}, bf16[2,256,256]{2,1,0:T(8,128)(2,1)S(1)}, u32[]{:S(2)}, u32[]{:S(2)}) collective-permute-start(bf16[2,256,256]{2,1,0:T(8,128)(2,1)S(1)} %slice.18), channel_id=1, source_target_pairs={{0,16},{1,17},{2,18},{3,19},{4,20},{5,21},{6,22},{7,23},{8,24},{9,... | collective-permute-start | bytes 786440 | tf_op jit(solution)/shard_map/ppermute | solution.py:43
  78.3 10.3 %collective-permute-start.23 = (bf16[1,256,256]{2,1,0:T(8,128)(2,1)S(1)}, bf16[1,256,256]{2,1,0:T(8,128)(2,1)S(1)}, u32[]{:S(2)}, u32[]{:S(2)}) collective-permute-start(bf16[1,256,256]{2,1,0:T(8,128)(2,1)S(1)} %constant_dynamic-update-slice_fusion.n2), channel_id=1, source_target_pairs={{0,32},{1,33},{2,34},{3,35},{4,36},{5,37},{6,38},{7,39},{8,40},{9,... | collective-permute-start | bytes 393224 | tf_op jit(solution)/shard_map/ppermute | solution.py:43
  79.3 9.2 %collective-permute-start.20 = (bf16[1,256,256]{2,1,0:T(8,128)(2,1)S(1)}, bf16[1,256,256]{2,1,0:T(8,128)(2,1)S(1)}, u32[]{:S(2)}, u32[]{:S(2)}) collective-permute-start(bf16[1,256,256]{2,1,0:T(8,128)(2,1)S(1)} %constant_dynamic-update-slice_fusion.n2), channel_id=1, source_target_pairs={{0,48},{1,49},{2,50},{3,51},{4,52},{5,53},{6,54},{7,55},{8,56},{9,... | collective-permute-start | bytes 393224 | tf_op jit(solution)/shard_map/ppermute | solution.py:43
  81.7 10.4 %collective-permute-start.18 = (bf16[1,256,256]{2,1,0:T(8,128)(2,1)S(1)}, bf16[1,256,256]{2,1,0:T(8,128)(2,1)S(1)}, u32[]{:S(2)}, u32[]{:S(2)}) collective-permute-start(bf16[1,256,256]{2,1,0:T(8,128)(2,1)S(1)} %constant_dynamic-update-slice_fusion.n2), channel_id=1, source_target_pairs={{0,16},{1,17},{2,18},{3,19},{4,20},{5,21},{6,22},{7,23},{8,24},{9,... | collective-permute-start | bytes 393224 | tf_op jit(solution)/shard_map/ppermute | solution.py:43
  82.5 9.6 %collective-permute-start.22 = (bf16[1,256,256]{2,1,0:T(8,128)(2,1)S(1)}, bf16[1,256,256]{2,1,0:T(8,128)(2,1)S(1)}, u32[]{:S(2)}, u32[]{:S(2)}) collective-permute-start(bf16[1,256,256]{2,1,0:T(8,128)(2,1)S(1)} %slice.19), channel_id=1, source_target_pairs={{0,48},{1,49},{2,50},{3,51},{4,52},{5,53},{6,54},{7,55},{8,56},{9,... | collective-permute-start | bytes 393224 | tf_op jit(solution)/shard_map/ppermute | solution.py:43

commit v2 on v1

--- a/solution.py
+++ b/solution.py
@@ -208,7 +208,7 @@
                     second[q, pl.ds(where, 16), :] = value[source : source + 16]
         return carry
 
-    lax.fori_loop(0, 16, step, 0)
+    lax.fori_loop(0, 16, step, 0, unroll=True)
     for q in range(8):
         value = lax.dot_general(a_rel[...], second[q], NN, preferred_element_type=jnp.float32)
         keep_ref[q] = value[:64]
@@ -294,7 +294,7 @@
     )(keep, r01, r10, r11)
 
 
-def last_kernel(tau, n0, n2, l0, l2, r0, r2, fl, fr, f2, node_ref, side_ref, out_ref, sigma):
+def last_kernel(tau, n0, l0, r0, n1, l1, r1, n2, l2, r2, fl, fr, f2, node_ref, side_ref, out_hbm, sigma, out, sems):
     f32 = jnp.float32
     wide = lax.axis_index("wide")
     z_hi, x = wide // 4, lax.rem(wide, 4)
@@ -302,34 +302,34 @@
     column = lax.broadcasted_iota(jnp.int32, (256, 256), 1)
     eye = jnp.where(row == column, 1.0, 0.0).astype(jnp.bfloat16)
     pieces = []
-    for dx, near, far in ((0, n0, n2), (1, l0, l2), (3, r0, r2)):
-        pieces += [(dx, 0, near, 0), (dx, 1, near, 1), (dx, 3, near, 2), (dx, 2, far, 0)]
+    for dx, (own, near, far) in zip((0, 1, 3), ((n0, n1, n2), (l0, l1, l2), (r0, r1, r2))):
+        pieces += [(dx, 0, own, 0), (dx, 1, near, 0), (dx, 3, near, 1), (dx, 2, far, 0)]
     pieces += [(2, 0, fl, 0), (2, 1, fl, 1), (2, 3, fr, 0), (2, 2, f2, 0)]
-    for r in range(ROWS):
-        for dx, dz, ref, slot in pieces:
-            w = lax.rem(z_hi - dz + 4, 4) * 4 + lax.rem(x - dx + 4, 4)
-            place = pl.ds(pl.multiple_of(w * 16, 16), 16)
+    places = []
+    for dx, dz, _, _ in pieces:
+        w = lax.rem(z_hi - dz + 4, 4) * 4 + lax.rem(x - dx + 4, 4)
+        places.append(pl.ds(pl.multiple_of(w * 16, 16), 16))
+    for r in range(16):
+        for place, (_, _, ref, slot) in zip(places, pieces):
             sigma[r, place, :] = ref[slot, r * 16 : (r + 1) * 16]
-    for r in range(ROWS):
         turned = lax.dot_general(eye, sigma[r], NT, preferred_element_type=f32)
-        out_ref[r] = node_ref[r].astype(f32) + tau * (side_ref[r].astype(f32) - turned)
-
-
-ROWS = 4
+        out[r] = node_ref[r].astype(f32) + tau * (side_ref[r].astype(f32) - turned)
+        pltpu.make_async_copy(out.at[r], out_hbm.at[r], sems.at[r]).start()
+    for r in range(16):
+        pltpu.make_async_copy(out.at[r], out_hbm.at[r], sems.at[r]).wait()
 
 
 def last_of(tau, pieces, node, side):
-    def piece(n):
-        return pl.BlockSpec((n, ROWS * 16, 256), lambda r: (0, r, 0))
-
-    row = pl.BlockSpec((ROWS, 256, 256), lambda r: (r, 0, 0))
     return pl.pallas_call(
         functools.partial(last_kernel, tau),
         out_shape=jax.ShapeDtypeStruct((16, 256, 256), jnp.float32),
-        grid=(16 // ROWS,),
-        in_specs=[piece(p.shape[0]) for p in pieces] + [row, row],
-        out_specs=row,
-        scratch_shapes=[pltpu.VMEM((ROWS, 256, 256), jnp.bfloat16)],
+        in_specs=[pl.BlockSpec(memory_space=pltpu.VMEM)] * (len(pieces) + 2),
+        out_specs=pl.BlockSpec(memory_space=pltpu.HBM),
+        scratch_shapes=[
+            pltpu.VMEM((16, 256, 256), jnp.bfloat16),
+            pltpu.VMEM((16, 256, 256), jnp.float32),
+            pltpu.SemaphoreType.DMA((16,)),
+        ],
         compiler_params=grant(16),
         name="update",
     )(*pieces, node, side)
@@ -350,13 +350,16 @@
     piece = z_sum(keep, r01, r10, r11)
     piece = piece[None]
     z1, z3 = send(piece, dz_hi=1), send(piece, dz_hi=3)
-    near = jnp.concatenate([piece, z1, z3])
-    l0, r0 = send(near, dx=1), send(near, dx=3)
-    fa, fb = send(z1[:, :128], dz_hi=1), send(z3[:, 128:], dz_hi=3)
+    l0, r0 = send(piece, dx=1), send(piece, dx=3)
+    fa = send(z1[:, :128], dz_hi=1)
+    near = jnp.concatenate([z1, z3])
+    l1, r1 = send(near, dx=1), send(near, dx=3)
+    fb = send(z3[:, 128:], dz_hi=3)
     far = jnp.concatenate([fa, fb], axis=1)
     l2, r2, f2 = send(far, dx=1), send(far, dx=3), send(far, dx=2)
-    fl, fr = send(l0[:2], dx=1), send(r0[2:], dx=3)
-    return last_of(tau, (near, far, l0, l2, r0, r2, fl, fr, f2), node, right_side)
+    fl, fr = send(jnp.concatenate([l0, l1[:1]]), dx=1), send(r1[1:], dx=3)
+    pieces = (piece, l0, r0, near, l1, r1, far, l2, r2, fl, fr, f2)
+    return last_of(tau, pieces, node, right_side)
 
 
 def solution(mesh):

time: 95.7 us -> 91.8 us (0.959)
  the two profiles are of different devices: /device:TPU:32 before, /device:TPU:8 now
where the time goes in v2:
time: 91.8 us; the launch traced here: 91.7 us
  starting transfers between devices  41 us (45%)
  waiting for transfers between devices  35.4 us (39%)
  Pallas kernels  14.8 us (16%)
    ppermute x26, starting transfers between devices, send(): return lax.ppermute(value, ('wide', 'narrow'), pairs_of(move))  41 us
    ppermute x26, waiting for transfers between devices, send(): return lax.ppermute(value, ('wide', 'narrow'), pairs_of(move))  35.4 us
    pallas_call x1, Pallas kernels, main_of(): pl.pallas_call(main_kernel, out_shape=[jax.ShapeDtypeStruct((8, 64, 256),...  7.05 us
    pallas_call x1, Pallas kernels, prep(): pl.pallas_call(prep_kernel, out_shape=[jax.ShapeDtypeStruct((12, 2, 128,...  3.23 us
    pallas_call x1, Pallas kernels, last_of(): pl.pallas_call(functools.partial(last_kernel, tau), out_shape=jax.ShapeDt...  2.51 us
  transfers between devices with their start and end apart: 26, of which 14 were waited for; matrix products, arithmetic and copies ran while one was open for 0% of the time, Pallas kernels for 4%

profile of v2, /device:TPU:8, one launch (start us, length us, event | category | flops | bytes accessed | tf_op | source)
XLA Modules:
  0.0 91.7 jit_solution(6582933143641150839)
XLA Ops:
  0.7 3.1 %collective-permute-start.2 = (s32[16,128]{1,0:T(8,128)S(1)}, s32[16,128]{1,0:T(8,128)S(1)}, u32[]{:S(2)}, u32[]{:S(2)}) collective-permute-start(s32[16,128]{1,0:T(8,128)S(1)} %own_rows.1), channel_id=1, source_target_pairs={{0,32},{1,33},{2,34},{3,35},{4,36},{5,37},{6,38},{7,39},{8,40},{9,... | collective-permute-start | bytes 24584 | tf_op jit(solution)/shard_map/ppermute | solution.py:43
  3.8 1.1 %collective-permute-start.1 = (s32[16,128]{1,0:T(8,128)S(1)}, s32[16,128]{1,0:T(8,128)S(1)}, u32[]{:S(2)}, u32[]{:S(2)}) collective-permute-start(s32[16,128]{1,0:T(8,128)S(1)} %own_rows.1), channel_id=1, source_target_pairs={{0,48},{1,49},{2,50},{3,51},{4,52},{5,53},{6,54},{7,55},{8,56},{9,... | collective-permute-start | bytes 24584 | tf_op jit(solution)/shard_map/ppermute | solution.py:43
  6.0 1.5 %collective-permute-done.1 = s32[16,128]{1,0:T(8,128)S(1)} collective-permute-done((s32[16,128]{1,0:T(8,128)S(1)}, s32[16,128]{1,0:T(8,128)S(1)}, u32[]{:S(2)}, u32[]{:S(2)}) %collective-permute-start.1) | collective-permute-done | bytes 8224 | tf_op jit(solution)/shard_map/ppermute | solution.py:43
  7.5 2.4 %collective-permute-done = s32[16,128]{1,0:T(8,128)S(1)} collective-permute-done((s32[16,128]{1,0:T(8,128)S(1)}, s32[16,128]{1,0:T(8,128)S(1)}, u32[]{:S(2)}, u32[]{:S(2)}) %collective-permute-start) | collective-permute-done | bytes 8224 | tf_op jit(solution)/shard_map/ppermute | solution.py:43
  9.8 7.2 %collective-permute-start.5 = (s32[16,128]{1,0:T(8,128)S(1)}, s32[16,128]{1,0:T(8,128)S(1)}, u32[]{:S(2)}, u32[]{:S(2)}) collective-permute-start(s32[16,128]{1,0:T(8,128)S(1)} %add_add_fusion.1), channel_id=1, source_target_pairs={{0,128},{1,129},{2,130},{3,131},{4,132},{5,133},{6,134},{7,135},{8... | collective-permute-start | bytes 24584 | tf_op jit(solution)/shard_map/ppermute | solution.py:43
  17.0 2.9 %collective-permute-start.3 = (s32[16,128]{1,0:T(8,128)S(1)}, s32[16,128]{1,0:T(8,128)S(1)}, u32[]{:S(2)}, u32[]{:S(2)}) collective-permute-start(s32[16,128]{1,0:T(8,128)S(1)} %add_add_fusion.1), channel_id=1, source_target_pairs={{0,64},{1,65},{2,66},{3,67},{4,68},{5,69},{6,70},{7,71},{8,72},{9,... | collective-permute-start | bytes 24584 | tf_op jit(solution)/shard_map/ppermute | solution.py:43
  20.0 3.2 %prep.1 = (bf16[12,2,128,256]{3,2,1,0:T(8,128)(2,1)S(1)}, bf16[12,512,128]{2,1,0:T(8,128)(2,1)S(1)}, bf16[96,256]{1,0:T(8,128)(2,1)S(1)}) custom-call(bf16[16,256,256]{2,1,0:T(8,128)(2,1)} %node_ref.1, bf16[3,12,256,256]{3,2,1,0:T(8,128)(2,1)} %legs_hbm.3), custom_call_target="tpu_custom_call" | custom-call | flops 471859200 | bytes 6291456 | tf_op jit(solution)/shard_map/prep/pallas_call | solution.py:92
  23.2 1.1 %sibling.1.first_ref = bf16[12,2,128,256]{3,2,1,0:T(8,128)(2,1)S(1)} custom-call(bf16[16,256,256]{2,1,0:T(8,128)(2,1)S(1)} %collective-permute-done.6.node_ref, bf16[96,256]{1,0:T(8,128)(2,1)S(1)} %get-tuple-element.16.ops_ref, bf16[12,2,128,256]{3,2,1,0:T(8,128)(2,1)S(1)} %get-tuple-element.17.first_ref), custom_call_target="tpu_custom_call", output_to_operand_aliasing={{}: (2, {})} | custom-call | flops 201326592 | bytes 3145728 | tf_op jit(solution)/shard_map/sibling/pallas_call | solution.py:127
  24.4 7.1 %two_legs.1 = (f32[8,64,256]{2,1,0:T(8,128)S(1)}, bf16[8,64,256]{2,1,0:T(8,128)(2,1)S(1)}, bf16[8,64,256]{2,1,0:T(8,128)(2,1)S(1)}, bf16[8,64,256]{2,1,0:T(8,128)(2,1)S(1)}) custom-call(s32[16,128]{1,0:T(8,128)S(1)} %add_add_fusion.table, bf16[12,2,128,256]{3,2,1,0:T(8,128)(2,1)S(1)} %sibling.1.first_ref, bf16[3,12,256,256]{3,2,1,0:T(8,128)(2,1)} %legs_hbm.3, ...), custom_call_target="tpu_custom_call" | custom-call | flops 4294967296 | bytes 8388608 | tf_op jit(solution)/shard_map/two_legs/pallas_call | solution.py:222
  31.4 1.8 %collective-permute-start.7 = (bf16[8,64,256]{2,1,0:T(8,128)(2,1)S(1)}, bf16[8,64,256]{2,1,0:T(8,128)(2,1)S(1)}, u32[]{:S(2)}, u32[]{:S(2)}) collective-permute-start(bf16[8,64,256]{2,1,0:T(8,128)(2,1)S(1)} %get-tuple-element.20), channel_id=1, source_target_pairs={{0,2},{1,3},{2,4},{3,5},{4,6},{5,7},{6,0},{7,1},{8,10},{9,11},{10,... | collective-permute-start | bytes 786440 | tf_op jit(solution)/shard_map/ppermute | solution.py:43
  33.3 0.9 %collective-permute-start.8 = (bf16[8,64,256]{2,1,0:T(8,128)(2,1)S(1)}, bf16[8,64,256]{2,1,0:T(8,128)(2,1)S(1)}, u32[]{:S(2)}, u32[]{:S(2)}) collective-permute-start(bf16[8,64,256]{2,1,0:T(8,128)(2,1)S(1)} %get-tuple-element.21), channel_id=1, source_target_pairs={{0,4},{1,5},{2,6},{3,7},{4,0},{5,1},{6,2},{7,3},{8,12},{9,13},{10,... | collective-permute-start | bytes 786440 | tf_op jit(solution)/shard_map/ppermute | solution.py:43
  34.2 2.4 %collective-permute-start.9 = (bf16[8,64,256]{2,1,0:T(8,128)(2,1)S(1)}, bf16[8,64,256]{2,1,0:T(8,128)(2,1)S(1)}, u32[]{:S(2)}, u32[]{:S(2)}) collective-permute-start(bf16[8,64,256]{2,1,0:T(8,128)(2,1)S(1)} %get-tuple-element.22), channel_id=1, source_target_pairs={{0,6},{1,7},{2,0},{3,1},{4,2},{5,3},{6,4},{7,5},{8,14},{9,15},{10,... | collective-permute-start | bytes 786440 | tf_op jit(solution)/shard_map/ppermute | solution.py:43
  36.6 4.0 %collective-permute-done.7.r1_ref = bf16[8,64,256]{2,1,0:T(8,128)(2,1)S(1)} collective-permute-done((bf16[8,64,256]{2,1,0:T(8,128)(2,1)S(1)}, bf16[8,64,256]{2,1,0:T(8,128)(2,1)S(1)}, u32[]{:S(2)}, u32[]{:S(2)}) %collective-permute-start.7) | collective-permute-done | bytes 262176 | tf_op jit(solution)/shard_map/ppermute | solution.py:43
  40.7 2.8 %collective-permute-done.8.r2_ref = bf16[8,64,256]{2,1,0:T(8,128)(2,1)S(1)} collective-permute-done((bf16[8,64,256]{2,1,0:T(8,128)(2,1)S(1)}, bf16[8,64,256]{2,1,0:T(8,128)(2,1)S(1)}, u32[]{:S(2)}, u32[]{:S(2)}) %collective-permute-start.8) | collective-permute-done | bytes 262176 | tf_op jit(solution)/shard_map/ppermute | solution.py:43
  43.5 2.1 %collective-permute-done.9.r3_ref = bf16[8,64,256]{2,1,0:T(8,128)(2,1)S(1)} collective-permute-done((bf16[8,64,256]{2,1,0:T(8,128)(2,1)S(1)}, bf16[8,64,256]{2,1,0:T(8,128)(2,1)S(1)}, u32[]{:S(2)}, u32[]{:S(2)}) %collective-permute-start.9) | collective-permute-done | bytes 262176 | tf_op jit(solution)/shard_map/ppermute | solution.py:43
  45.8 1.1 %collective-permute-start.11 = (bf16[8,16,256]{2,1,0:T(8,128)(2,1)S(1)}, bf16[8,16,256]{2,1,0:T(8,128)(2,1)S(1)}, u32[]{:S(2)}, u32[]{:S(2)}) collective-permute-start(bf16[8,16,256]{2,1,0:T(8,128)(2,1)S(1)} %get-tuple-element.25), channel_id=1, source_target_pairs={{0,8},{1,9},{2,10},{3,11},{4,12},{5,13},{6,14},{7,15},{8,0},{9,1},... | collective-permute-start | bytes 196616 | tf_op jit(solution)/shard_map/ppermute | solution.py:43
  47.7 3.0 %collective-permute-done.11.r10_ref = bf16[8,16,256]{2,1,0:T(8,128)(2,1)S(1)} collective-permute-done((bf16[8,16,256]{2,1,0:T(8,128)(2,1)S(1)}, bf16[8,16,256]{2,1,0:T(8,128)(2,1)S(1)}, u32[]{:S(2)}, u32[]{:S(2)}) %collective-permute-start.11) | collective-permute-done | bytes 65568 | tf_op jit(solution)/shard_map/ppermute | solution.py:43
  51.5 2.8 %collective-permute-start.15 = (bf16[1,256,256]{2,1,0:T(8,128)(2,1)S(1)}, bf16[1,256,256]{2,1,0:T(8,128)(2,1)S(1)}, u32[]{:S(2)}, u32[]{:S(2)}) collective-permute-start(bf16[1,256,256]{2,1,0:T(8,128)(2,1)S(1)} %bitcast.1), channel_id=1, source_target_pairs={{0,64},{1,65},{2,66},{3,67},{4,68},{5,69},{6,70},{7,71},{8,72},{9,... | collective-permute-start | bytes 393224 | tf_op jit(solution)/shard_map/ppermute | solution.py:43
  54.2 1.5 %collective-permute-start.16 = (bf16[1,256,256]{2,1,0:T(8,128)(2,1)S(1)}, bf16[1,256,256]{2,1,0:T(8,128)(2,1)S(1)}, u32[]{:S(2)}, u32[]{:S(2)}) collective-permute-start(bf16[1,256,256]{2,1,0:T(8,128)(2,1)S(1)} %bitcast.2), channel_id=1, source_target_pairs={{0,192},{1,193},{2,194},{3,195},{4,196},{5,197},{6,198},{7,199},{8... | collective-permute-start | bytes 393224 | tf_op jit(solution)/shard_map/ppermute | solution.py:43
  55.7 3.7 %collective-permute-done.15 = bf16[1,256,256]{2,1,0:T(8,128)(2,1)S(1)} collective-permute-done((bf16[1,256,256]{2,1,0:T(8,128)(2,1)S(1)}, bf16[1,256,256]{2,1,0:T(8,128)(2,1)S(1)}, u32[]{:S(2)}, u32[]{:S(2)}) %collective-permute-start.15) | collective-permute-done | bytes 131104 | tf_op jit(solution)/shard_map/ppermute | solution.py:43
  59.4 3.9 %collective-permute-done.16 = bf16[1,256,256]{2,1,0:T(8,128)(2,1)S(1)} collective-permute-done((bf16[1,256,256]{2,1,0:T(8,128)(2,1)S(1)}, bf16[1,256,256]{2,1,0:T(8,128)(2,1)S(1)}, u32[]{:S(2)}, u32[]{:S(2)}) %collective-permute-start.16) | collective-permute-done | bytes 131104 | tf_op jit(solution)/shard_map/ppermute | solution.py:43
  63.8 2.9 %collective-permute-start.14 = (bf16[1,256,256]{2,1,0:T(8,128)(2,1)S(1)}, bf16[1,256,256]{2,1,0:T(8,128)(2,1)S(1)}, u32[]{:S(2)}, u32[]{:S(2)}) collective-permute-start(bf16[1,256,256]{2,1,0:T(8,128)(2,1)S(1)} %bitcast.4), channel_id=1, source_target_pairs={{0,48},{1,49},{2,50},{3,51},{4,52},{5,53},{6,54},{7,55},{8,56},{9,... | collective-permute-start | bytes 393224 | tf_op jit(solution)/shard_map/ppermute | solution.py:43
  66.7 1.9 %collective-permute-start.18 = (bf16[2,256,256]{2,1,0:T(8,128)(2,1)S(1)}, bf16[2,256,256]{2,1,0:T(8,128)(2,1)S(1)}, u32[]{:S(2)}, u32[]{:S(2)}) collective-permute-start(bf16[2,256,256]{2,1,0:T(8,128)(2,1)S(1)} %constant_dynamic-update-slice_fusion.n1), channel_id=1, source_target_pairs={{0,48},{1,49},{2,50},{3,51},{4,52},{5,53},{6,54},{7,55},{8,56},{9,... | collective-permute-start | bytes 786440 | tf_op jit(solution)/shard_map/ppermute | solution.py:43
  68.6 2.7 %collective-permute-start.20 = (bf16[1,128,256]{2,1,0:T(8,128)(2,1)S(1)}, bf16[1,128,256]{2,1,0:T(8,128)(2,1)S(1)}, u32[]{:S(2)}, u32[]{:S(2)}) collective-permute-start(bf16[1,128,256]{2,1,0:T(8,128)(2,1)S(1)} %slice.17), channel_id=1, source_target_pairs={{0,192},{1,193},{2,194},{3,195},{4,196},{5,197},{6,198},{7,199},{8... | collective-permute-start | bytes 196616 | tf_op jit(solution)/shard_map/ppermute | solution.py:43
  71.3 2.4 %collective-permute-done.17.l1 = bf16[2,256,256]{2,1,0:T(8,128)(2,1)S(1)} collective-permute-done((bf16[2,256,256]{2,1,0:T(8,128)(2,1)S(1)}, bf16[2,256,256]{2,1,0:T(8,128)(2,1)S(1)}, u32[]{:S(2)}, u32[]{:S(2)}) %collective-permute-start.17) | collective-permute-done | bytes 262176 | tf_op jit(solution)/shard_map/ppermute | solution.py:43
  73.8 1.5 %collective-permute-start.19 = (bf16[1,128,256]{2,1,0:T(8,128)(2,1)S(1)}, bf16[1,128,256]{2,1,0:T(8,128)(2,1)S(1)}, u32[]{:S(2)}, u32[]{:S(2)}) collective-permute-start(bf16[1,128,256]{2,1,0:T(8,128)(2,1)S(1)} %slice.16), channel_id=1, source_target_pairs={{0,64},{1,65},{2,66},{3,67},{4,68},{5,69},{6,70},{7,71},{8,72},{9,... | collective-permute-start | bytes 196616 | tf_op jit(solution)/shard_map/ppermute | solution.py:43
  75.4 4.8 %collective-permute-done.19 = bf16[1,128,256]{2,1,0:T(8,128)(2,1)S(1)} collective-permute-done((bf16[1,128,256]{2,1,0:T(8,128)(2,1)S(1)}, bf16[1,128,256]{2,1,0:T(8,128)(2,1)S(1)}, u32[]{:S(2)}, u32[]{:S(2)}) %collective-permute-start.19) | collective-permute-done | bytes 65568 | tf_op jit(solution)/shard_map/ppermute | solution.py:43
  80.3 1.5 %collective-permute-start.22 = (bf16[1,256,256]{2,1,0:T(8,128)(2,1)S(1)}, bf16[1,256,256]{2,1,0:T(8,128)(2,1)S(1)}, u32[]{:S(2)}, u32[]{:S(2)}) collective-permute-start(bf16[1,256,256]{2,1,0:T(8,128)(2,1)S(1)} %constant_dynamic-update-slice_fusion.2.n2), channel_id=1, source_target_pairs={{0,48},{1,49},{2,50},{3,51},{4,52},{5,53},{6,54},{7,55},{8,56},{9,... | collective-permute-start | bytes 393224 | tf_op jit(solution)/shard_map/ppermute | solution.py:43
  82.4 2.7 %collective-permute-start.24 = (bf16[1,256,256]{2,1,0:T(8,128)(2,1)S(1)}, bf16[1,256,256]{2,1,0:T(8,128)(2,1)S(1)}, u32[]{:S(2)}, u32[]{:S(2)}) collective-permute-start(bf16[1,256,256]{2,1,0:T(8,128)(2,1)S(1)} %slice.19), channel_id=1, source_target_pairs={{0,48},{1,49},{2,50},{3,51},{4,52},{5,53},{6,54},{7,55},{8,56},{9,... | collective-permute-start | bytes 393224 | tf_op jit(solution)/shard_map/ppermute | solution.py:43
  85.1 1.8 %collective-permute-done.25.f2 = bf16[1,256,256]{2,1,0:T(8,128)(2,1)S(1)} collective-permute-done((bf16[1,256,256]{2,1,0:T(8,128)(2,1)S(1)}, bf16[1,256,256]{2,1,0:T(8,128)(2,1)S(1)}, u32[]{:S(2)}, u32[]{:S(2)}) %collective-permute-start.25) | collective-permute-done | bytes 131104 | tf_op jit(solution)/shard_map/ppermute | solution.py:43
  86.8 2.2 %collective-permute-done.21.l2 = bf16[1,256,256]{2,1,0:T(8,128)(2,1)S(1)} collective-permute-done((bf16[1,256,256]{2,1,0:T(8,128)(2,1)S(1)}, bf16[1,256,256]{2,1,0:T(8,128)(2,1)S(1)}, u32[]{:S(2)}, u32[]{:S(2)}) %collective-permute-start.21) | collective-permute-done | bytes 131104 | tf_op jit(solution)/shard_map/ppermute | solution.py:43
  89.0 2.5 %update.1 = f32[16,256,256]{2,1,0:T(8,128)} custom-call(bf16[1,256,256]{2,1,0:T(8,128)(2,1)S(1)} %bitcast.5, bf16[1,256,256]{2,1,0:T(8,128)(2,1)S(1)} %collective-permute-done.13.l0, bf16[1,256,256]{2,1,0:T(8,128)(2,1)S(1)} %collective-permute-done.14.r0, bf16[2,256,256]{2,1,0:T(8,128)(2,1)S(1)} %constant_dynamic-update-slice_fusion.n1, ...), custom_call_target="tpu_custom_call" | custom-call | tf_op jit(solution)/shard_map/update/pallas_call | solution.py:323
  (42 shorter events, 4.9 us)
Async XLA Ops:
  0.0 23.2 %collective-permute-start.6 = (bf16[16,256,256]{2,1,0:T(8,128)(2,1)}, bf16[16,256,256]{2,1,0:T(8,128)(2,1)S(1)}, u32[]{:S(2)}, u32[]{:S(2)}) collective-permute-start(bf16[16,256,256]{2,1,0:T(8,128)(2,1)} %node_ref.1), channel_id=1, source_target_pairs={{0,1},{1,0},{2,3},{3,2},{4,5},{5,4},{6,7},{7,6},{8,9},{9,8},{10,11... | collective-permute-start | bytes 6291464 | tf_op jit(solution)/shard_map/ppermute | solution.py:43
  0.7 5.2 %collective-permute-start.2 = (s32[16,128]{1,0:T(8,128)S(1)}, s32[16,128]{1,0:T(8,128)S(1)}, u32[]{:S(2)}, u32[]{:S(2)}) collective-permute-start(s32[16,128]{1,0:T(8,128)S(1)} %own_rows.1), channel_id=1, source_target_pairs={{0,32},{1,33},{2,34},{3,35},{4,36},{5,37},{6,38},{7,39},{8,40},{9,... | collective-permute-start | bytes 24584 | tf_op jit(solution)/shard_map/ppermute | solution.py:43
  3.8 3.7 %collective-permute-start.1 = (s32[16,128]{1,0:T(8,128)S(1)}, s32[16,128]{1,0:T(8,128)S(1)}, u32[]{:S(2)}, u32[]{:S(2)}) collective-permute-start(s32[16,128]{1,0:T(8,128)S(1)} %own_rows.1), channel_id=1, source_target_pairs={{0,48},{1,49},{2,50},{3,51},{4,52},{5,53},{6,54},{7,55},{8,56},{9,... | collective-permute-start | bytes 24584 | tf_op jit(solution)/shard_map/ppermute | solution.py:43
  5.0 4.9 %collective-permute-start = (s32[16,128]{1,0:T(8,128)S(1)}, s32[16,128]{1,0:T(8,128)S(1)}, u32[]{:S(2)}, u32[]{:S(2)}) collective-permute-start(s32[16,128]{1,0:T(8,128)S(1)} %own_rows.1), channel_id=1, source_target_pairs={{0,16},{1,17},{2,18},{3,19},{4,20},{5,21},{6,22},{7,23},{8,24},{9,... | collective-permute-start | bytes 24584 | tf_op jit(solution)/shard_map/ppermute | solution.py:43
  9.8 13.4 %collective-permute-start.5 = (s32[16,128]{1,0:T(8,128)S(1)}, s32[16,128]{1,0:T(8,128)S(1)}, u32[]{:S(2)}, u32[]{:S(2)}) collective-permute-start(s32[16,128]{1,0:T(8,128)S(1)} %add_add_fusion.1), channel_id=1, source_target_pairs={{0,128},{1,129},{2,130},{3,131},{4,132},{5,133},{6,134},{7,135},{8... | collective-permute-start | bytes 24584 | tf_op jit(solution)/shard_map/ppermute | solution.py:43
  17.0 6.2 %collective-permute-start.4 = (s32[16,128]{1,0:T(8,128)S(1)}, s32[16,128]{1,0:T(8,128)S(1)}, u32[]{:S(2)}, u32[]{:S(2)}) collective-permute-start(s32[16,128]{1,0:T(8,128)S(1)} %add_add_fusion.1), channel_id=1, source_target_pairs={{0,192},{1,193},{2,194},{3,195},{4,196},{5,197},{6,198},{7,199},{8... | collective-permute-start | bytes 24584 | tf_op jit(solution)/shard_map/ppermute | solution.py:43
  17.0 6.2 %collective-permute-start.3 = (s32[16,128]{1,0:T(8,128)S(1)}, s32[16,128]{1,0:T(8,128)S(1)}, u32[]{:S(2)}, u32[]{:S(2)}) collective-permute-start(s32[16,128]{1,0:T(8,128)S(1)} %add_add_fusion.1), channel_id=1, source_target_pairs={{0,64},{1,65},{2,66},{3,67},{4,68},{5,69},{6,70},{7,71},{8,72},{9,... | collective-permute-start | bytes 24584 | tf_op jit(solution)/shard_map/ppermute | solution.py:43
  24.4 64.7 %copy-start.1 = (bf16[16,256,256]{2,1,0:T(8,128)(2,1)S(1)}, bf16[16,256,256]{2,1,0:T(8,128)(2,1)}, u32[]{:S(2)}) copy-start(bf16[16,256,256]{2,1,0:T(8,128)(2,1)} %side_ref.1) | copy-start | bytes 6291460
  31.4 57.6 %copy-start = (bf16[16,256,256]{2,1,0:T(8,128)(2,1)S(1)}, bf16[16,256,256]{2,1,0:T(8,128)(2,1)}, u32[]{:S(2)}) copy-start(bf16[16,256,256]{2,1,0:T(8,128)(2,1)} %node_ref.1) | copy-start | bytes 6291460
  31.4 9.2 %collective-permute-start.7 = (bf16[8,64,256]{2,1,0:T(8,128)(2,1)S(1)}, bf16[8,64,256]{2,1,0:T(8,128)(2,1)S(1)}, u32[]{:S(2)}, u32[]{:S(2)}) collective-permute-start(bf16[8,64,256]{2,1,0:T(8,128)(2,1)S(1)} %get-tuple-element.20), channel_id=1, source_target_pairs={{0,2},{1,3},{2,4},{3,5},{4,6},{5,7},{6,0},{7,1},{8,10},{9,11},{10,... | collective-permute-start | bytes 786440 | tf_op jit(solution)/shard_map/ppermute | solution.py:43
  33.3 10.2 %collective-permute-start.8 = (bf16[8,64,256]{2,1,0:T(8,128)(2,1)S(1)}, bf16[8,64,256]{2,1,0:T(8,128)(2,1)S(1)}, u32[]{:S(2)}, u32[]{:S(2)}) collective-permute-start(bf16[8,64,256]{2,1,0:T(8,128)(2,1)S(1)} %get-tuple-element.21), channel_id=1, source_target_pairs={{0,4},{1,5},{2,6},{3,7},{4,0},{5,1},{6,2},{7,3},{8,12},{9,13},{10,... | collective-permute-start | bytes 786440 | tf_op jit(solution)/shard_map/ppermute | solution.py:43
  34.2 11.4 %collective-permute-start.9 = (bf16[8,64,256]{2,1,0:T(8,128)(2,1)S(1)}, bf16[8,64,256]{2,1,0:T(8,128)(2,1)S(1)}, u32[]{:S(2)}, u32[]{:S(2)}) collective-permute-start(bf16[8,64,256]{2,1,0:T(8,128)(2,1)S(1)} %get-tuple-element.22), channel_id=1, source_target_pairs={{0,6},{1,7},{2,0},{3,1},{4,2},{5,3},{6,4},{7,5},{8,14},{9,15},{10,... | collective-permute-start | bytes 786440 | tf_op jit(solution)/shard_map/ppermute | solution.py:43
  45.7 2.0 %collective-permute-start.10 = (bf16[8,16,256]{2,1,0:T(8,128)(2,1)S(1)}, bf16[8,16,256]{2,1,0:T(8,128)(2,1)S(1)}, u32[]{:S(2)}, u32[]{:S(2)}) collective-permute-start(bf16[8,16,256]{2,1,0:T(8,128)(2,1)S(1)} %get-tuple-element.24), channel_id=1, source_target_pairs={{0,1},{1,0},{2,3},{3,2},{4,5},{5,4},{6,7},{7,6},{8,9},{9,8},{10,11... | collective-permute-start | bytes 196616 | tf_op jit(solution)/shard_map/ppermute | solution.py:43
  45.8 4.9 %collective-permute-start.11 = (bf16[8,16,256]{2,1,0:T(8,128)(2,1)S(1)}, bf16[8,16,256]{2,1,0:T(8,128)(2,1)S(1)}, u32[]{:S(2)}, u32[]{:S(2)}) collective-permute-start(bf16[8,16,256]{2,1,0:T(8,128)(2,1)S(1)} %get-tuple-element.25), channel_id=1, source_target_pairs={{0,8},{1,9},{2,10},{3,11},{4,12},{5,13},{6,14},{7,15},{8,0},{9,1},... | collective-permute-start | bytes 196616 | tf_op jit(solution)/shard_map/ppermute | solution.py:43
  46.9 4.4 %collective-permute-start.12 = (bf16[8,16,256]{2,1,0:T(8,128)(2,1)S(1)}, bf16[8,16,256]{2,1,0:T(8,128)(2,1)S(1)}, u32[]{:S(2)}, u32[]{:S(2)}) collective-permute-start(bf16[8,16,256]{2,1,0:T(8,128)(2,1)S(1)} %get-tuple-element.26), channel_id=1, source_target_pairs={{0,9},{1,8},{2,11},{3,10},{4,13},{5,12},{6,15},{7,14},{8,1},{9,0},... | collective-permute-start | bytes 196616 | tf_op jit(solution)/shard_map/ppermute | solution.py:43
  51.5 7.9 %collective-permute-start.15 = (bf16[1,256,256]{2,1,0:T(8,128)(2,1)S(1)}, bf16[1,256,256]{2,1,0:T(8,128)(2,1)S(1)}, u32[]{:S(2)}, u32[]{:S(2)}) collective-permute-start(bf16[1,256,256]{2,1,0:T(8,128)(2,1)S(1)} %bitcast.1), channel_id=1, source_target_pairs={{0,64},{1,65},{2,66},{3,67},{4,68},{5,69},{6,70},{7,71},{8,72},{9,... | collective-permute-start | bytes 393224 | tf_op jit(solution)/shard_map/ppermute | solution.py:43
  54.2 9.1 %collective-permute-start.16 = (bf16[1,256,256]{2,1,0:T(8,128)(2,1)S(1)}, bf16[1,256,256]{2,1,0:T(8,128)(2,1)S(1)}, u32[]{:S(2)}, u32[]{:S(2)}) collective-permute-start(bf16[1,256,256]{2,1,0:T(8,128)(2,1)S(1)} %bitcast.2), channel_id=1, source_target_pairs={{0,192},{1,193},{2,194},{3,195},{4,196},{5,197},{6,198},{7,199},{8... | collective-permute-start | bytes 393224 | tf_op jit(solution)/shard_map/ppermute | solution.py:43
  63.3 10.5 %collective-permute-start.17 = (bf16[2,256,256]{2,1,0:T(8,128)(2,1)S(1)}, bf16[2,256,256]{2,1,0:T(8,128)(2,1)S(1)}, u32[]{:S(2)}, u32[]{:S(2)}) collective-permute-start(bf16[2,256,256]{2,1,0:T(8,128)(2,1)S(1)} %constant_dynamic-update-slice_fusion.n1), channel_id=1, source_target_pairs={{0,16},{1,17},{2,18},{3,19},{4,20},{5,21},{6,22},{7,23},{8,24},{9,... | collective-permute-start | bytes 786440 | tf_op jit(solution)/shard_map/ppermute | solution.py:43
  63.4 11.9 %collective-permute-start.13 = (bf16[1,256,256]{2,1,0:T(8,128)(2,1)S(1)}, bf16[1,256,256]{2,1,0:T(8,128)(2,1)S(1)}, u32[]{:S(2)}, u32[]{:S(2)}) collective-permute-start(bf16[1,256,256]{2,1,0:T(8,128)(2,1)S(1)} %bitcast.3), channel_id=1, source_target_pairs={{0,16},{1,17},{2,18},{3,19},{4,20},{5,21},{6,22},{7,23},{8,24},{9,... | collective-permute-start | bytes 393224 | tf_op jit(solution)/shard_map/ppermute | solution.py:43
  63.8 18.6 %collective-permute-start.14 = (bf16[1,256,256]{2,1,0:T(8,128)(2,1)S(1)}, bf16[1,256,256]{2,1,0:T(8,128)(2,1)S(1)}, u32[]{:S(2)}, u32[]{:S(2)}) collective-permute-start(bf16[1,256,256]{2,1,0:T(8,128)(2,1)S(1)} %bitcast.4), channel_id=1, source_target_pairs={{0,48},{1,49},{2,50},{3,51},{4,52},{5,53},{6,54},{7,55},{8,56},{9,... | collective-permute-start | bytes 393224 | tf_op jit(solution)/shard_map/ppermute | solution.py:43
  66.7 15.0 %collective-permute-start.18 = (bf16[2,256,256]{2,1,0:T(8,128)(2,1)S(1)}, bf16[2,256,256]{2,1,0:T(8,128)(2,1)S(1)}, u32[]{:S(2)}, u32[]{:S(2)}) collective-permute-start(bf16[2,256,256]{2,1,0:T(8,128)(2,1)S(1)} %constant_dynamic-update-slice_fusion.n1), channel_id=1, source_target_pairs={{0,48},{1,49},{2,50},{3,51},{4,52},{5,53},{6,54},{7,55},{8,56},{9,... | collective-permute-start | bytes 786440 | tf_op jit(solution)/shard_map/ppermute | solution.py:43
  68.6 11.5 %collective-permute-start.20 = (bf16[1,128,256]{2,1,0:T(8,128)(2,1)S(1)}, bf16[1,128,256]{2,1,0:T(8,128)(2,1)S(1)}, u32[]{:S(2)}, u32[]{:S(2)}) collective-permute-start(bf16[1,128,256]{2,1,0:T(8,128)(2,1)S(1)} %slice.17), channel_id=1, source_target_pairs={{0,192},{1,193},{2,194},{3,195},{4,196},{5,197},{6,198},{7,199},{8... | collective-permute-start | bytes 196616 | tf_op jit(solution)/shard_map/ppermute | solution.py:43
  73.8 6.4 %collective-permute-start.19 = (bf16[1,128,256]{2,1,0:T(8,128)(2,1)S(1)}, bf16[1,128,256]{2,1,0:T(8,128)(2,1)S(1)}, u32[]{:S(2)}, u32[]{:S(2)}) collective-permute-start(bf16[1,128,256]{2,1,0:T(8,128)(2,1)S(1)} %slice.16), channel_id=1, source_target_pairs={{0,64},{1,65},{2,66},{3,67},{4,68},{5,69},{6,70},{7,71},{8,72},{9,... | collective-permute-start | bytes 196616 | tf_op jit(solution)/shard_map/ppermute | solution.py:43
  75.3 13.7 %collective-permute-start.23 = (bf16[2,256,256]{2,1,0:T(8,128)(2,1)S(1)}, bf16[2,256,256]{2,1,0:T(8,128)(2,1)S(1)}, u32[]{:S(2)}, u32[]{:S(2)}) collective-permute-start(bf16[2,256,256]{2,1,0:T(8,128)(2,1)S(1)} %pad_maximum_fusion), channel_id=1, source_target_pairs={{0,16},{1,17},{2,18},{3,19},{4,20},{5,21},{6,22},{7,23},{8,24},{9,... | collective-permute-start | bytes 786440 | tf_op jit(solution)/shard_map/ppermute | solution.py:43
  80.2 6.7 %collective-permute-start.25 = (bf16[1,256,256]{2,1,0:T(8,128)(2,1)S(1)}, bf16[1,256,256]{2,1,0:T(8,128)(2,1)S(1)}, u32[]{:S(2)}, u32[]{:S(2)}) collective-permute-start(bf16[1,256,256]{2,1,0:T(8,128)(2,1)S(1)} %constant_dynamic-update-slice_fusion.2.n2), channel_id=1, source_target_pairs={{0,32},{1,33},{2,34},{3,35},{4,36},{5,37},{6,38},{7,39},{8,40},{9,... | collective-permute-start | bytes 393224 | tf_op jit(solution)/shard_map/ppermute | solution.py:43
  80.3 6.6 %collective-permute-start.22 = (bf16[1,256,256]{2,1,0:T(8,128)(2,1)S(1)}, bf16[1,256,256]{2,1,0:T(8,128)(2,1)S(1)}, u32[]{:S(2)}, u32[]{:S(2)}) collective-permute-start(bf16[1,256,256]{2,1,0:T(8,128)(2,1)S(1)} %constant_dynamic-update-slice_fusion.2.n2), channel_id=1, source_target_pairs={{0,48},{1,49},{2,50},{3,51},{4,52},{5,53},{6,54},{7,55},{8,56},{9,... | collective-permute-start | bytes 393224 | tf_op jit(solution)/shard_map/ppermute | solution.py:43
  81.7 7.3 %collective-permute-start.21 = (bf16[1,256,256]{2,1,0:T(8,128)(2,1)S(1)}, bf16[1,256,256]{2,1,0:T(8,128)(2,1)S(1)}, u32[]{:S(2)}, u32[]{:S(2)}) collective-permute-start(bf16[1,256,256]{2,1,0:T(8,128)(2,1)S(1)} %constant_dynamic-update-slice_fusion.2.n2), channel_id=1, source_target_pairs={{0,16},{1,17},{2,18},{3,19},{4,20},{5,21},{6,22},{7,23},{8,24},{9,... | collective-permute-start | bytes 393224 | tf_op jit(solution)/shard_map/ppermute | solution.py:43
  82.4 6.6 %collective-permute-start.24 = (bf16[1,256,256]{2,1,0:T(8,128)(2,1)S(1)}, bf16[1,256,256]{2,1,0:T(8,128)(2,1)S(1)}, u32[]{:S(2)}, u32[]{:S(2)}) collective-permute-start(bf16[1,256,256]{2,1,0:T(8,128)(2,1)S(1)} %slice.19), channel_id=1, source_target_pairs={{0,48},{1,49},{2,50},{3,51},{4,52},{5,53},{6,54},{7,55},{8,56},{9,... | collective-permute-start | bytes 393224 | tf_op jit(solution)/shard_map/ppermute | solution.py:43

commit v3 on v2

--- a/solution.py
+++ b/solution.py
@@ -62,18 +62,23 @@
     wide, narrow = lax.axis_index("wide"), lax.axis_index("narrow")
     core = lax.rem(narrow, 2)
     columns = pl.ds(pl.multiple_of(wide * 16, 16), 16)
-    fetch_a = pltpu.make_async_copy(legs_hbm.at[0], leg_a, sems.at[0])
-    fetch_c = pltpu.make_async_copy(legs_hbm.at[2, :, columns, :], tiles, sems.at[1])
-    fetch_node = pltpu.make_async_copy(node_hbm, node_ref, sems.at[2])
-    fetch_a.start()
+    fetch_a = [
+        pltpu.make_async_copy(legs_hbm.at[0, pl.ds(3 * n, 3)], leg_a.at[pl.ds(3 * n, 3)], sems.at[2 + n])
+        for n in range(4)
+    ]
+    fetch_c = pltpu.make_async_copy(legs_hbm.at[2, :, columns, :], tiles, sems.at[0])
+    fetch_node = pltpu.make_async_copy(node_hbm, node_ref, sems.at[1])
+    for copy in fetch_a:
+        copy.start()
     fetch_c.start()
     fetch_node.start()
     lane = lax.broadcasted_iota(jnp.int32, (256, 128), 1) % 32
     source = (narrow - core) * 16 + jnp.where(lane < 16, core * 16 + lane, (1 - core) * 16 + lane - 16)
     row = lax.broadcasted_iota(jnp.int32, (256, 128), 0)
     pick = jnp.where(row == source, 1.0, 0.0).astype(jnp.bfloat16)
-    fetch_a.wait()
     for i in range(12):
+        if i % 3 == 0:
+            fetch_a[i // 3].wait()
         block = lax.dot_general(leg_a[i], pick, NN, preferred_element_type=jnp.float32)
         block = block.astype(jnp.bfloat16)
         cols_ref[i, :256] = block
@@ -109,7 +114,7 @@
             pltpu.VMEM((12, 16, 256), jnp.bfloat16),
             pltpu.VMEM((12, 16, 256), jnp.float32),
             pltpu.VMEM((2, 1536, 128), jnp.float32),
-            pltpu.SemaphoreType.DMA((3,)),
+            pltpu.SemaphoreType.DMA((6,)),
         ],
         compiler_params=grant(14),
         cost_estimate=pl.CostEstimate(flops=2 * 3072 * 256 * 300, bytes_accessed=6 << 20, transcendentals=0),
@@ -164,7 +169,7 @@
     )(in_hbm(op_index), in_hbm(offsets))
 
 
-def main_kernel(table, first_ref, legs_hbm, cols_ref, keep_ref, m1_ref, m2_ref, m3_ref, leg_b, second, a_abs, a_rel, sem):
+def main_kernel(table, first_ref, legs_hbm, cols_ref, second, a_own, m1_ref, m2_ref, m3_ref, leg_b, a_abs, a_rel, sem):
     fetch = pltpu.make_async_copy(legs_hbm.at[1], leg_b, sem)
     fetch.start()
     narrow = lax.axis_index("narrow")
@@ -191,7 +196,9 @@
         block = lax.rem(z_lo + dz, 2) * 8 + lax.rem(y + dy, 4) * 2 + lax.rem(core + dc, 2)
         source = pl.multiple_of(block * 16, 16)
         for g in range(16):
-            a_rel[16 * blk : 16 * blk + 16, g * 128 : (g + 1) * 128] = a_abs[g, pl.ds(source, 16), :]
+            rows = a_own if blk < 4 else a_rel
+            row = 16 * (blk % 4 if blk < 4 else blk - 4)
+            rows[row : row + 16, g * 128 : (g + 1) * 128] = a_abs[g, pl.ds(source, 16), :]
 
     fetch.wait()
 
@@ -211,17 +218,33 @@
     lax.fori_loop(0, 16, step, 0, unroll=True)
     for q in range(8):
         value = lax.dot_general(a_rel[...], second[q], NN, preferred_element_type=jnp.float32)
-        keep_ref[q] = value[:64]
-        m1_ref[q] = value[64:128].astype(jnp.bfloat16)
-        m2_ref[q] = value[128:192].astype(jnp.bfloat16)
-        m3_ref[q] = value[192:].astype(jnp.bfloat16)
+        m1_ref[q] = value[:64].astype(jnp.bfloat16)
+        m2_ref[q] = value[64:128].astype(jnp.bfloat16)
+        m3_ref[q] = value[128:].astype(jnp.bfloat16)
+
+
+def keep_kernel(second, a_own, keep_ref):
+    for q in range(8):
+        keep_ref[q] = lax.dot_general(a_own[...], second[q], NN, preferred_element_type=jnp.float32)
+
+
+def keep_of(second, a_own):
+    return pl.pallas_call(
+        keep_kernel,
+        out_shape=jax.ShapeDtypeStruct((8, 64, 256), jnp.float32),
+        in_specs=[pl.BlockSpec(memory_space=pltpu.VMEM)] * 2,
+        out_specs=pl.BlockSpec(memory_space=pltpu.VMEM),
+        compiler_params=grant(4),
+        cost_estimate=pl.CostEstimate(flops=2 * 64 * 2048 * 2048, bytes_accessed=9 << 20, transcendentals=0),
+        name="own_target",
+    )(second, a_own)
 
 
 def main_of(table, first, leg_ops, cols):
     whole3 = lambda g, s: (0, 0, 0)
     return pl.pallas_call(
         main_kernel,
-        out_shape=[jax.ShapeDtypeStruct((8, 64, 256), jnp.float32)]
+        out_shape=[jax.ShapeDtypeStruct((8, 2048, 256), jnp.bfloat16), jax.ShapeDtypeStruct((64, 2048), jnp.bfloat16)]
         + [jax.ShapeDtypeStruct((8, 64, 256), jnp.bfloat16)] * 3,
         grid_spec=pltpu.PrefetchScalarGridSpec(
             num_scalar_prefetch=1,
@@ -231,12 +254,11 @@
                 pl.BlockSpec(memory_space=pltpu.HBM),
                 pl.BlockSpec((12, 512, 128), whole3),
             ],
-            out_specs=[pl.BlockSpec((8, 64, 256), whole3)] * 4,
+            out_specs=[pl.BlockSpec(memory_space=pltpu.VMEM)] * 5,
             scratch_shapes=[
                 pltpu.VMEM((12, 256, 256), jnp.bfloat16),
-                pltpu.VMEM((8, 2048, 256), jnp.bfloat16),
                 pltpu.VMEM((16, 256, 128), jnp.bfloat16),
-                pltpu.VMEM((256, 2048), jnp.bfloat16),
+                pltpu.VMEM((192, 2048), jnp.bfloat16),
                 pltpu.SemaphoreType.DMA(()),
             ],
         ),
@@ -294,7 +316,7 @@
     )(keep, r01, r10, r11)
 
 
-def last_kernel(tau, n0, l0, r0, n1, l1, r1, n2, l2, r2, fl, fr, f2, node_ref, side_ref, out_hbm, sigma, out, sems):
+def last_kernel(tau, n0, l0, r0, n1, l1, r1, n2, f0, fl, fr, f2, node_ref, side_ref, out_hbm, sigma, out, sems):
     f32 = jnp.float32
     wide = lax.axis_index("wide")
     z_hi, x = wide // 4, lax.rem(wide, 4)
@@ -302,9 +324,9 @@
     column = lax.broadcasted_iota(jnp.int32, (256, 256), 1)
     eye = jnp.where(row == column, 1.0, 0.0).astype(jnp.bfloat16)
     pieces = []
-    for dx, (own, near, far) in zip((0, 1, 3), ((n0, n1, n2), (l0, l1, l2), (r0, r1, r2))):
-        pieces += [(dx, 0, own, 0), (dx, 1, near, 0), (dx, 3, near, 1), (dx, 2, far, 0)]
-    pieces += [(2, 0, fl, 0), (2, 1, fl, 1), (2, 3, fr, 0), (2, 2, f2, 0)]
+    for dx, own, near, (far, slot) in ((0, n0, n1, (n2, 0)), (1, l0, l1, (fl, 1)), (3, r0, r1, (fr, 1))):
+        pieces += [(dx, 0, own, 0), (dx, 1, near, 0), (dx, 3, near, 1), (dx, 2, far, slot)]
+    pieces += [(2, 0, f0, 0), (2, 1, fl, 0), (2, 3, fr, 0), (2, 2, f2, 0)]
     places = []
     for dx, dz, _, _ in pieces:
         w = lax.rem(z_hi - dz + 4, 4) * 4 + lax.rem(x - dx + 4, 4)
@@ -343,10 +365,12 @@
     sibling = send(node, dcore=1)
     first, cols, ops_c = prep(node, leg_ops)
     first = add_sibling(sibling, ops_c, first)
-    keep, m1, m2, m3 = main_of(table, first, leg_ops, cols)
+    second, a_own, m1, m2, m3 = main_of(table, first, leg_ops, cols)
     r1, r3, r2 = send(m1, dy=1), send(m3, dy=3), send(m2, dy=2)
+    keep = keep_of(second, a_own)
     keep, m01, m10, m11 = y_sum(keep, r1, r2, r3)
-    r10, r11, r01 = send(m10, dz_lo=1), send(m11, dz_lo=1, dcore=1), send(m01, dcore=1)
+    r10, r11 = send(m10, dz_lo=1), send(m11, dz_lo=1, dcore=1)
+    r01 = send(m01, dcore=1)
     piece = z_sum(keep, r01, r10, r11)
     piece = piece[None]
     z1, z3 = send(piece, dz_hi=1), send(piece, dz_hi=3)
@@ -355,10 +379,12 @@
     near = jnp.concatenate([z1, z3])
     l1, r1 = send(near, dx=1), send(near, dx=3)
     fb = send(z3[:, 128:], dz_hi=3)
+    f0 = send(l0, dx=1)
     far = jnp.concatenate([fa, fb], axis=1)
-    l2, r2, f2 = send(far, dx=1), send(far, dx=3), send(far, dx=2)
-    fl, fr = send(jnp.concatenate([l0, l1[:1]]), dx=1), send(r1[1:], dx=3)
-    pieces = (piece, l0, r0, near, l1, r1, far, l2, r2, fl, fr, f2)
+    fl = send(jnp.concatenate([l1[:1], far]), dx=1)
+    fr = send(jnp.concatenate([r1[1:], far]), dx=3)
+    f2 = send(far, dx=2)
+    pieces = (piece, l0, r0, near, l1, r1, far, f0, fl, fr, f2)
     return last_of(tau, pieces, node, right_side)
 
 

time: 91.8 us -> 89.3 us (0.973)
  starting transfers between devices: 41 us -> 36.1 us
  Pallas kernels: 14.8 us -> 15.9 us
    ppermute x26 -> x25, starting transfers between devices: 41 us -> 36.1 us  [send(): return lax.ppermute(value, ('wide', 'narrow'), pairs_of(move))]
    pallas_call x1 -> x2, Pallas kernels: 7.05 us -> 8.1 us  [the longest x1 6.55 us: main_of(): pl.pallas_call(main_kernel, out_shape=[jax.ShapeDtypeStruct((8, 2048, 256...]
    ppermute x26 -> x25, waiting for transfers between devices: 35.4 us -> 36.3 us  [send(): return lax.ppermute(value, ('wide', 'narrow'), pairs_of(move))]
  transfers between devices with their start and end apart: 26 -> 25, of which waited for: 14 -> 16; matrix products, arithmetic and copies ran while one was open for 0% -> 0% of each run, Pallas kernels for 4% -> 6%
where the time goes in v3:
time: 89.3 us; the launch traced here: 88.9 us
  waiting for transfers between devices  36.3 us (41%)
  starting transfers between devices  36.1 us (40%)
  Pallas kernels  15.9 us (18%)
    ppermute x25, waiting for transfers between devices, send(): return lax.ppermute(value, ('wide', 'narrow'), pairs_of(move))  36.3 us
    ppermute x25, starting transfers between devices, send(): return lax.ppermute(value, ('wide', 'narrow'), pairs_of(move))  36.1 us
    pallas_call x1, Pallas kernels, main_of(): pl.pallas_call(main_kernel, out_shape=[jax.ShapeDtypeStruct((8, 2048, 256...  6.55 us
    pallas_call x1, Pallas kernels, prep(): pl.pallas_call(prep_kernel, out_shape=[jax.ShapeDtypeStruct((12, 2, 128,...  3.29 us
    pallas_call x1, Pallas kernels, last_of(): pl.pallas_call(functools.partial(last_kernel, tau), out_shape=jax.ShapeDt...  2.5 us
  transfers between devices with their start and end apart: 25, of which 16 were waited for; matrix products, arithmetic and copies ran while one was open for 0% of the time, Pallas kernels for 6%

profile of v3, /device:TPU:8, one launch (start us, length us, event | category | flops | bytes accessed | tf_op | source)
XLA Modules:
  0.0 88.9 jit_solution(3208003158850226733)
XLA Ops:
  0.7 3.1 %collective-permute-start.2 = (s32[16,128]{1,0:T(8,128)S(1)}, s32[16,128]{1,0:T(8,128)S(1)}, u32[]{:S(2)}, u32[]{:S(2)}) collective-permute-start(s32[16,128]{1,0:T(8,128)S(1)} %own_rows.1), channel_id=1, source_target_pairs={{0,32},{1,33},{2,34},{3,35},{4,36},{5,37},{6,38},{7,39},{8,40},{9,... | collective-permute-start | bytes 24584 | tf_op jit(solution)/shard_map/ppermute | solution.py:43
  3.8 1.1 %collective-permute-start.1 = (s32[16,128]{1,0:T(8,128)S(1)}, s32[16,128]{1,0:T(8,128)S(1)}, u32[]{:S(2)}, u32[]{:S(2)}) collective-permute-start(s32[16,128]{1,0:T(8,128)S(1)} %own_rows.1), channel_id=1, source_target_pairs={{0,48},{1,49},{2,50},{3,51},{4,52},{5,53},{6,54},{7,55},{8,56},{9,... | collective-permute-start | bytes 24584 | tf_op jit(solution)/shard_map/ppermute | solution.py:43
  5.0 0.9 collective-permute-start
  6.0 1.5 %collective-permute-done.1 = s32[16,128]{1,0:T(8,128)S(1)} collective-permute-done((s32[16,128]{1,0:T(8,128)S(1)}, s32[16,128]{1,0:T(8,128)S(1)}, u32[]{:S(2)}, u32[]{:S(2)}) %collective-permute-start.1) | collective-permute-done | bytes 8224 | tf_op jit(solution)/shard_map/ppermute | solution.py:43
  7.5 2.4 %collective-permute-done = s32[16,128]{1,0:T(8,128)S(1)} collective-permute-done((s32[16,128]{1,0:T(8,128)S(1)}, s32[16,128]{1,0:T(8,128)S(1)}, u32[]{:S(2)}, u32[]{:S(2)}) %collective-permute-start) | collective-permute-done | bytes 8224 | tf_op jit(solution)/shard_map/ppermute | solution.py:43
  9.8 7.2 %collective-permute-start.5 = (s32[16,128]{1,0:T(8,128)S(1)}, s32[16,128]{1,0:T(8,128)S(1)}, u32[]{:S(2)}, u32[]{:S(2)}) collective-permute-start(s32[16,128]{1,0:T(8,128)S(1)} %add_add_fusion.1), channel_id=1, source_target_pairs={{0,128},{1,129},{2,130},{3,131},{4,132},{5,133},{6,134},{7,135},{8... | collective-permute-start | bytes 24584 | tf_op jit(solution)/shard_map/ppermute | solution.py:43
  17.0 2.9 %collective-permute-start.3 = (s32[16,128]{1,0:T(8,128)S(1)}, s32[16,128]{1,0:T(8,128)S(1)}, u32[]{:S(2)}, u32[]{:S(2)}) collective-permute-start(s32[16,128]{1,0:T(8,128)S(1)} %add_add_fusion.1), channel_id=1, source_target_pairs={{0,64},{1,65},{2,66},{3,67},{4,68},{5,69},{6,70},{7,71},{8,72},{9,... | collective-permute-start | bytes 24584 | tf_op jit(solution)/shard_map/ppermute | solution.py:43
  20.0 3.3 %prep.1 = (bf16[12,2,128,256]{3,2,1,0:T(8,128)(2,1)S(1)}, bf16[12,512,128]{2,1,0:T(8,128)(2,1)S(1)}, bf16[96,256]{1,0:T(8,128)(2,1)S(1)}) custom-call(bf16[16,256,256]{2,1,0:T(8,128)(2,1)} %node_ref.1, bf16[3,12,256,256]{3,2,1,0:T(8,128)(2,1)} %legs_hbm.3), custom_call_target="tpu_custom_call" | custom-call | flops 471859200 | bytes 6291456 | tf_op jit(solution)/shard_map/prep/pallas_call | solution.py:97
  23.3 1.1 %sibling.1.first_ref = bf16[12,2,128,256]{3,2,1,0:T(8,128)(2,1)S(1)} custom-call(bf16[16,256,256]{2,1,0:T(8,128)(2,1)S(1)} %collective-permute-done.6.node_ref, bf16[96,256]{1,0:T(8,128)(2,1)S(1)} %get-tuple-element.17.ops_ref, bf16[12,2,128,256]{3,2,1,0:T(8,128)(2,1)S(1)} %get-tuple-element.18.first_ref), custom_call_target="tpu_custom_call", output_to_operand_aliasing={{}: (2, {})} | custom-call | flops 201326592 | bytes 3145728 | tf_op jit(solution)/shard_map/sibling/pallas_call | solution.py:132
  24.4 6.6 %two_legs.1 = (bf16[8,2048,256]{2,1,0:T(8,128)(2,1)S(1)}, bf16[64,2048]{1,0:T(8,128)(2,1)S(1)}, bf16[8,64,256]{2,1,0:T(8,128)(2,1)S(1)}, bf16[8,64,256]{2,1,0:T(8,128)(2,1)S(1)}, bf16[8,64,256]{2,1,0:T(8,128)(2,1)S(1)}) custom-call(s32[16,128]{1,0:T(8,128)S(1)} %add_add_fusion.table, bf16[12,2,128,256]{3,2,1,0:T(8,128)(2,1)S(1)} %sibling.1.first_ref, ...), custom_call_target="tpu_custom_call" | custom-call | flops 4294967296 | bytes 8388608 | tf_op jit(solution)/shard_map/two_legs/pallas_call | solution.py:245
  31.0 1.7 %collective-permute-start.7 = (bf16[8,64,256]{2,1,0:T(8,128)(2,1)S(1)}, bf16[8,64,256]{2,1,0:T(8,128)(2,1)S(1)}, u32[]{:S(2)}, u32[]{:S(2)}) collective-permute-start(bf16[8,64,256]{2,1,0:T(8,128)(2,1)S(1)} %get-tuple-element.22), channel_id=1, source_target_pairs={{0,2},{1,3},{2,4},{3,5},{4,6},{5,7},{6,0},{7,1},{8,10},{9,11},{10,... | collective-permute-start | bytes 786440 | tf_op jit(solution)/shard_map/ppermute | solution.py:43
  32.6 1.0 %collective-permute-start.8 = (bf16[8,64,256]{2,1,0:T(8,128)(2,1)S(1)}, bf16[8,64,256]{2,1,0:T(8,128)(2,1)S(1)}, u32[]{:S(2)}, u32[]{:S(2)}) collective-permute-start(bf16[8,64,256]{2,1,0:T(8,128)(2,1)S(1)} %get-tuple-element.23), channel_id=1, source_target_pairs={{0,4},{1,5},{2,6},{3,7},{4,0},{5,1},{6,2},{7,3},{8,12},{9,13},{10,... | collective-permute-start | bytes 786440 | tf_op jit(solution)/shard_map/ppermute | solution.py:43
  33.6 2.4 %collective-permute-start.9 = (bf16[8,64,256]{2,1,0:T(8,128)(2,1)S(1)}, bf16[8,64,256]{2,1,0:T(8,128)(2,1)S(1)}, u32[]{:S(2)}, u32[]{:S(2)}) collective-permute-start(bf16[8,64,256]{2,1,0:T(8,128)(2,1)S(1)} %get-tuple-element.24), channel_id=1, source_target_pairs={{0,6},{1,7},{2,0},{3,1},{4,2},{5,3},{6,4},{7,5},{8,14},{9,15},{10,... | collective-permute-start | bytes 786440 | tf_op jit(solution)/shard_map/ppermute | solution.py:43
  36.0 1.6 %own_target.1.keep_ref = f32[8,64,256]{2,1,0:T(8,128)S(1)} custom-call(bf16[8,2048,256]{2,1,0:T(8,128)(2,1)S(1)} %get-tuple-element.20.second, bf16[64,2048]{1,0:T(8,128)(2,1)S(1)} %get-tuple-element.21.a_own), custom_call_target="tpu_custom_call" | custom-call | flops 536870912 | bytes 9437184 | tf_op jit(solution)/shard_map/own_target/pallas_call | solution.py:232
  37.6 2.5 %collective-permute-done.7.r1_ref = bf16[8,64,256]{2,1,0:T(8,128)(2,1)S(1)} collective-permute-done((bf16[8,64,256]{2,1,0:T(8,128)(2,1)S(1)}, bf16[8,64,256]{2,1,0:T(8,128)(2,1)S(1)}, u32[]{:S(2)}, u32[]{:S(2)}) %collective-permute-start.7) | collective-permute-done | bytes 262176 | tf_op jit(solution)/shard_map/ppermute | solution.py:43
  40.0 2.9 %collective-permute-done.8.r2_ref = bf16[8,64,256]{2,1,0:T(8,128)(2,1)S(1)} collective-permute-done((bf16[8,64,256]{2,1,0:T(8,128)(2,1)S(1)}, bf16[8,64,256]{2,1,0:T(8,128)(2,1)S(1)}, u32[]{:S(2)}, u32[]{:S(2)}) %collective-permute-start.8) | collective-permute-done | bytes 262176 | tf_op jit(solution)/shard_map/ppermute | solution.py:43
  42.9 2.3 %collective-permute-done.9.r3_ref = bf16[8,64,256]{2,1,0:T(8,128)(2,1)S(1)} collective-permute-done((bf16[8,64,256]{2,1,0:T(8,128)(2,1)S(1)}, bf16[8,64,256]{2,1,0:T(8,128)(2,1)S(1)}, u32[]{:S(2)}, u32[]{:S(2)}) %collective-permute-start.9) | collective-permute-done | bytes 262176 | tf_op jit(solution)/shard_map/ppermute | solution.py:43
  45.4 1.1 %collective-permute-start.11 = (bf16[8,16,256]{2,1,0:T(8,128)(2,1)S(1)}, bf16[8,16,256]{2,1,0:T(8,128)(2,1)S(1)}, u32[]{:S(2)}, u32[]{:S(2)}) collective-permute-start(bf16[8,16,256]{2,1,0:T(8,128)(2,1)S(1)} %get-tuple-element.27), channel_id=1, source_target_pairs={{0,8},{1,9},{2,10},{3,11},{4,12},{5,13},{6,14},{7,15},{8,0},{9,1},... | collective-permute-start | bytes 196616 | tf_op jit(solution)/shard_map/ppermute | solution.py:43
  47.2 3.0 %collective-permute-done.11.r10_ref = bf16[8,16,256]{2,1,0:T(8,128)(2,1)S(1)} collective-permute-done((bf16[8,16,256]{2,1,0:T(8,128)(2,1)S(1)}, bf16[8,16,256]{2,1,0:T(8,128)(2,1)S(1)}, u32[]{:S(2)}, u32[]{:S(2)}) %collective-permute-start.11) | collective-permute-done | bytes 65568 | tf_op jit(solution)/shard_map/ppermute | solution.py:43
  51.0 2.8 %collective-permute-start.15 = (bf16[1,256,256]{2,1,0:T(8,128)(2,1)S(1)}, bf16[1,256,256]{2,1,0:T(8,128)(2,1)S(1)}, u32[]{:S(2)}, u32[]{:S(2)}) collective-permute-start(bf16[1,256,256]{2,1,0:T(8,128)(2,1)S(1)} %bitcast.1), channel_id=1, source_target_pairs={{0,64},{1,65},{2,66},{3,67},{4,68},{5,69},{6,70},{7,71},{8,72},{9,... | collective-permute-start | bytes 393224 | tf_op jit(solution)/shard_map/ppermute | solution.py:43
  53.7 1.5 %collective-permute-start.16 = (bf16[1,256,256]{2,1,0:T(8,128)(2,1)S(1)}, bf16[1,256,256]{2,1,0:T(8,128)(2,1)S(1)}, u32[]{:S(2)}, u32[]{:S(2)}) collective-permute-start(bf16[1,256,256]{2,1,0:T(8,128)(2,1)S(1)} %bitcast.2), channel_id=1, source_target_pairs={{0,192},{1,193},{2,194},{3,195},{4,196},{5,197},{6,198},{7,199},{8... | collective-permute-start | bytes 393224 | tf_op jit(solution)/shard_map/ppermute | solution.py:43
  55.2 6.1 %collective-permute-done.15 = bf16[1,256,256]{2,1,0:T(8,128)(2,1)S(1)} collective-permute-done((bf16[1,256,256]{2,1,0:T(8,128)(2,1)S(1)}, bf16[1,256,256]{2,1,0:T(8,128)(2,1)S(1)}, u32[]{:S(2)}, u32[]{:S(2)}) %collective-permute-start.15) | collective-permute-done | bytes 131104 | tf_op jit(solution)/shard_map/ppermute | solution.py:43
  61.3 1.5 %collective-permute-done.16 = bf16[1,256,256]{2,1,0:T(8,128)(2,1)S(1)} collective-permute-done((bf16[1,256,256]{2,1,0:T(8,128)(2,1)S(1)}, bf16[1,256,256]{2,1,0:T(8,128)(2,1)S(1)}, u32[]{:S(2)}, u32[]{:S(2)}) %collective-permute-start.16) | collective-permute-done | bytes 131104 | tf_op jit(solution)/shard_map/ppermute | solution.py:43
  63.3 1.7 %collective-permute-start.17 = (bf16[2,256,256]{2,1,0:T(8,128)(2,1)S(1)}, bf16[2,256,256]{2,1,0:T(8,128)(2,1)S(1)}, u32[]{:S(2)}, u32[]{:S(2)}) collective-permute-start(bf16[2,256,256]{2,1,0:T(8,128)(2,1)S(1)} %constant_dynamic-update-slice_fusion.n1), channel_id=1, source_target_pairs={{0,16},{1,17},{2,18},{3,19},{4,20},{5,21},{6,22},{7,23},{8,24},{9,... | collective-permute-start | bytes 786440 | tf_op jit(solution)/shard_map/ppermute | solution.py:43
  65.0 2.7 %collective-permute-start.20 = (bf16[1,128,256]{2,1,0:T(8,128)(2,1)S(1)}, bf16[1,128,256]{2,1,0:T(8,128)(2,1)S(1)}, u32[]{:S(2)}, u32[]{:S(2)}) collective-permute-start(bf16[1,128,256]{2,1,0:T(8,128)(2,1)S(1)} %slice.17), channel_id=1, source_target_pairs={{0,192},{1,193},{2,194},{3,195},{4,196},{5,197},{6,198},{7,199},{8... | collective-permute-start | bytes 196616 | tf_op jit(solution)/shard_map/ppermute | solution.py:43
  68.0 2.1 %collective-permute-done.20 = bf16[1,128,256]{2,1,0:T(8,128)(2,1)S(1)} collective-permute-done((bf16[1,128,256]{2,1,0:T(8,128)(2,1)S(1)}, bf16[1,128,256]{2,1,0:T(8,128)(2,1)S(1)}, u32[]{:S(2)}, u32[]{:S(2)}) %collective-permute-start.20) | collective-permute-done | bytes 65568 | tf_op jit(solution)/shard_map/ppermute | solution.py:43
  70.7 2.7 %collective-permute-done.17.l1 = bf16[2,256,256]{2,1,0:T(8,128)(2,1)S(1)} collective-permute-done((bf16[2,256,256]{2,1,0:T(8,128)(2,1)S(1)}, bf16[2,256,256]{2,1,0:T(8,128)(2,1)S(1)}, u32[]{:S(2)}, u32[]{:S(2)}) %collective-permute-start.17) | collective-permute-done | bytes 262176 | tf_op jit(solution)/shard_map/ppermute | solution.py:43
  73.5 2.0 %collective-permute-start.22 = (bf16[2,256,256]{2,1,0:T(8,128)(2,1)S(1)}, bf16[2,256,256]{2,1,0:T(8,128)(2,1)S(1)}, u32[]{:S(2)}, u32[]{:S(2)}) collective-permute-start(bf16[2,256,256]{2,1,0:T(8,128)(2,1)S(1)} %get-tuple-element.30), channel_id=1, source_target_pairs={{0,16},{1,17},{2,18},{3,19},{4,20},{5,21},{6,22},{7,23},{8,24},{9,... | collective-permute-start | bytes 786440 | tf_op jit(solution)/shard_map/ppermute | solution.py:43
  75.6 1.3 %collective-permute-start.14 = (bf16[1,256,256]{2,1,0:T(8,128)(2,1)S(1)}, bf16[1,256,256]{2,1,0:T(8,128)(2,1)S(1)}, u32[]{:S(2)}, u32[]{:S(2)}) collective-permute-start(bf16[1,256,256]{2,1,0:T(8,128)(2,1)S(1)} %bitcast.4), channel_id=1, source_target_pairs={{0,48},{1,49},{2,50},{3,51},{4,52},{5,53},{6,54},{7,55},{8,56},{9,... | collective-permute-start | bytes 393224 | tf_op jit(solution)/shard_map/ppermute | solution.py:43
  78.3 4.6 %collective-permute-done.14.r0 = bf16[1,256,256]{2,1,0:T(8,128)(2,1)S(1)} collective-permute-done((bf16[1,256,256]{2,1,0:T(8,128)(2,1)S(1)}, bf16[1,256,256]{2,1,0:T(8,128)(2,1)S(1)}, u32[]{:S(2)}, u32[]{:S(2)}) %collective-permute-start.14) | collective-permute-done | bytes 131104 | tf_op jit(solution)/shard_map/ppermute | solution.py:43
  83.0 3.2 %collective-permute-done.21.f0 = bf16[1,256,256]{2,1,0:T(8,128)(2,1)S(1)} collective-permute-done((bf16[1,256,256]{2,1,0:T(8,128)(2,1)S(1)}, bf16[1,256,256]{2,1,0:T(8,128)(2,1)S(1)}, u32[]{:S(2)}, u32[]{:S(2)}) %collective-permute-start.21) | collective-permute-done | bytes 131104 | tf_op jit(solution)/shard_map/ppermute | solution.py:43
  86.2 2.5 %update.1 = f32[16,256,256]{2,1,0:T(8,128)} custom-call(bf16[1,256,256]{2,1,0:T(8,128)(2,1)S(1)} %bitcast.5, bf16[1,256,256]{2,1,0:T(8,128)(2,1)S(1)} %collective-permute-done.13.l0, bf16[1,256,256]{2,1,0:T(8,128)(2,1)S(1)} %collective-permute-done.14.r0, bf16[2,256,256]{2,1,0:T(8,128)(2,1)S(1)} %constant_dynamic-update-slice_fusion.n1, ...), custom_call_target="tpu_custom_call" | custom-call | tf_op jit(solution)/shard_map/update/pallas_call | solution.py:345
  (41 shorter events, 5.5 us)
Async XLA Ops:
  0.0 23.3 %collective-permute-start.6 = (bf16[16,256,256]{2,1,0:T(8,128)(2,1)}, bf16[16,256,256]{2,1,0:T(8,128)(2,1)S(1)}, u32[]{:S(2)}, u32[]{:S(2)}) collective-permute-start(bf16[16,256,256]{2,1,0:T(8,128)(2,1)} %node_ref.1), channel_id=1, source_target_pairs={{0,1},{1,0},{2,3},{3,2},{4,5},{5,4},{6,7},{7,6},{8,9},{9,8},{10,11... | collective-permute-start | bytes 6291464 | tf_op jit(solution)/shard_map/ppermute | solution.py:43
  0.7 5.2 %collective-permute-start.2 = (s32[16,128]{1,0:T(8,128)S(1)}, s32[16,128]{1,0:T(8,128)S(1)}, u32[]{:S(2)}, u32[]{:S(2)}) collective-permute-start(s32[16,128]{1,0:T(8,128)S(1)} %own_rows.1), channel_id=1, source_target_pairs={{0,32},{1,33},{2,34},{3,35},{4,36},{5,37},{6,38},{7,39},{8,40},{9,... | collective-permute-start | bytes 24584 | tf_op jit(solution)/shard_map/ppermute | solution.py:43
  3.8 3.7 %collective-permute-start.1 = (s32[16,128]{1,0:T(8,128)S(1)}, s32[16,128]{1,0:T(8,128)S(1)}, u32[]{:S(2)}, u32[]{:S(2)}) collective-permute-start(s32[16,128]{1,0:T(8,128)S(1)} %own_rows.1), channel_id=1, source_target_pairs={{0,48},{1,49},{2,50},{3,51},{4,52},{5,53},{6,54},{7,55},{8,56},{9,... | collective-permute-start | bytes 24584 | tf_op jit(solution)/shard_map/ppermute | solution.py:43
  5.0 4.9 %collective-permute-start = (s32[16,128]{1,0:T(8,128)S(1)}, s32[16,128]{1,0:T(8,128)S(1)}, u32[]{:S(2)}, u32[]{:S(2)}) collective-permute-start(s32[16,128]{1,0:T(8,128)S(1)} %own_rows.1), channel_id=1, source_target_pairs={{0,16},{1,17},{2,18},{3,19},{4,20},{5,21},{6,22},{7,23},{8,24},{9,... | collective-permute-start | bytes 24584 | tf_op jit(solution)/shard_map/ppermute | solution.py:43
  9.8 13.4 %collective-permute-start.5 = (s32[16,128]{1,0:T(8,128)S(1)}, s32[16,128]{1,0:T(8,128)S(1)}, u32[]{:S(2)}, u32[]{:S(2)}) collective-permute-start(s32[16,128]{1,0:T(8,128)S(1)} %add_add_fusion.1), channel_id=1, source_target_pairs={{0,128},{1,129},{2,130},{3,131},{4,132},{5,133},{6,134},{7,135},{8... | collective-permute-start | bytes 24584 | tf_op jit(solution)/shard_map/ppermute | solution.py:43
  17.0 6.2 %collective-permute-start.4 = (s32[16,128]{1,0:T(8,128)S(1)}, s32[16,128]{1,0:T(8,128)S(1)}, u32[]{:S(2)}, u32[]{:S(2)}) collective-permute-start(s32[16,128]{1,0:T(8,128)S(1)} %add_add_fusion.1), channel_id=1, source_target_pairs={{0,192},{1,193},{2,194},{3,195},{4,196},{5,197},{6,198},{7,199},{8... | collective-permute-start | bytes 24584 | tf_op jit(solution)/shard_map/ppermute | solution.py:43
  17.0 6.2 %collective-permute-start.3 = (s32[16,128]{1,0:T(8,128)S(1)}, s32[16,128]{1,0:T(8,128)S(1)}, u32[]{:S(2)}, u32[]{:S(2)}) collective-permute-start(s32[16,128]{1,0:T(8,128)S(1)} %add_add_fusion.1), channel_id=1, source_target_pairs={{0,64},{1,65},{2,66},{3,67},{4,68},{5,69},{6,70},{7,71},{8,72},{9,... | collective-permute-start | bytes 24584 | tf_op jit(solution)/shard_map/ppermute | solution.py:43
  31.0 9.1 %collective-permute-start.7 = (bf16[8,64,256]{2,1,0:T(8,128)(2,1)S(1)}, bf16[8,64,256]{2,1,0:T(8,128)(2,1)S(1)}, u32[]{:S(2)}, u32[]{:S(2)}) collective-permute-start(bf16[8,64,256]{2,1,0:T(8,128)(2,1)S(1)} %get-tuple-element.22), channel_id=1, source_target_pairs={{0,2},{1,3},{2,4},{3,5},{4,6},{5,7},{6,0},{7,1},{8,10},{9,11},{10,... | collective-permute-start | bytes 786440 | tf_op jit(solution)/shard_map/ppermute | solution.py:43
  32.6 10.3 %collective-permute-start.8 = (bf16[8,64,256]{2,1,0:T(8,128)(2,1)S(1)}, bf16[8,64,256]{2,1,0:T(8,128)(2,1)S(1)}, u32[]{:S(2)}, u32[]{:S(2)}) collective-permute-start(bf16[8,64,256]{2,1,0:T(8,128)(2,1)S(1)} %get-tuple-element.23), channel_id=1, source_target_pairs={{0,4},{1,5},{2,6},{3,7},{4,0},{5,1},{6,2},{7,3},{8,12},{9,13},{10,... | collective-permute-start | bytes 786440 | tf_op jit(solution)/shard_map/ppermute | solution.py:43
  33.6 11.5 %collective-permute-start.9 = (bf16[8,64,256]{2,1,0:T(8,128)(2,1)S(1)}, bf16[8,64,256]{2,1,0:T(8,128)(2,1)S(1)}, u32[]{:S(2)}, u32[]{:S(2)}) collective-permute-start(bf16[8,64,256]{2,1,0:T(8,128)(2,1)S(1)} %get-tuple-element.24), channel_id=1, source_target_pairs={{0,6},{1,7},{2,0},{3,1},{4,2},{5,3},{6,4},{7,5},{8,14},{9,15},{10,... | collective-permute-start | bytes 786440 | tf_op jit(solution)/shard_map/ppermute | solution.py:43
  37.6 48.6 %copy-start = (bf16[16,256,256]{2,1,0:T(8,128)(2,1)S(1)}, bf16[16,256,256]{2,1,0:T(8,128)(2,1)}, u32[]{:S(2)}) copy-start(bf16[16,256,256]{2,1,0:T(8,128)(2,1)} %node_ref.1) | copy-start | bytes 6291460
  37.6 48.6 %copy-start.1 = (bf16[16,256,256]{2,1,0:T(8,128)(2,1)S(1)}, bf16[16,256,256]{2,1,0:T(8,128)(2,1)}, u32[]{:S(2)}) copy-start(bf16[16,256,256]{2,1,0:T(8,128)(2,1)} %side_ref.1) | copy-start | bytes 6291460
  45.3 2.0 %collective-permute-start.10 = (bf16[8,16,256]{2,1,0:T(8,128)(2,1)S(1)}, bf16[8,16,256]{2,1,0:T(8,128)(2,1)S(1)}, u32[]{:S(2)}, u32[]{:S(2)}) collective-permute-start(bf16[8,16,256]{2,1,0:T(8,128)(2,1)S(1)} %get-tuple-element.26), channel_id=1, source_target_pairs={{0,1},{1,0},{2,3},{3,2},{4,5},{5,4},{6,7},{7,6},{8,9},{9,8},{10,11... | collective-permute-start | bytes 196616 | tf_op jit(solution)/shard_map/ppermute | solution.py:43
  45.4 4.9 %collective-permute-start.11 = (bf16[8,16,256]{2,1,0:T(8,128)(2,1)S(1)}, bf16[8,16,256]{2,1,0:T(8,128)(2,1)S(1)}, u32[]{:S(2)}, u32[]{:S(2)}) collective-permute-start(bf16[8,16,256]{2,1,0:T(8,128)(2,1)S(1)} %get-tuple-element.27), channel_id=1, source_target_pairs={{0,8},{1,9},{2,10},{3,11},{4,12},{5,13},{6,14},{7,15},{8,0},{9,1},... | collective-permute-start | bytes 196616 | tf_op jit(solution)/shard_map/ppermute | solution.py:43
  46.5 4.4 %collective-permute-start.12 = (bf16[8,16,256]{2,1,0:T(8,128)(2,1)S(1)}, bf16[8,16,256]{2,1,0:T(8,128)(2,1)S(1)}, u32[]{:S(2)}, u32[]{:S(2)}) collective-permute-start(bf16[8,16,256]{2,1,0:T(8,128)(2,1)S(1)} %get-tuple-element.28), channel_id=1, source_target_pairs={{0,9},{1,8},{2,11},{3,10},{4,13},{5,12},{6,15},{7,14},{8,1},{9,0},... | collective-permute-start | bytes 196616 | tf_op jit(solution)/shard_map/ppermute | solution.py:43
  51.0 10.3 %collective-permute-start.15 = (bf16[1,256,256]{2,1,0:T(8,128)(2,1)S(1)}, bf16[1,256,256]{2,1,0:T(8,128)(2,1)S(1)}, u32[]{:S(2)}, u32[]{:S(2)}) collective-permute-start(bf16[1,256,256]{2,1,0:T(8,128)(2,1)S(1)} %bitcast.1), channel_id=1, source_target_pairs={{0,64},{1,65},{2,66},{3,67},{4,68},{5,69},{6,70},{7,71},{8,72},{9,... | collective-permute-start | bytes 393224 | tf_op jit(solution)/shard_map/ppermute | solution.py:43
  53.7 9.1 %collective-permute-start.16 = (bf16[1,256,256]{2,1,0:T(8,128)(2,1)S(1)}, bf16[1,256,256]{2,1,0:T(8,128)(2,1)S(1)}, u32[]{:S(2)}, u32[]{:S(2)}) collective-permute-start(bf16[1,256,256]{2,1,0:T(8,128)(2,1)S(1)} %bitcast.2), channel_id=1, source_target_pairs={{0,192},{1,193},{2,194},{3,195},{4,196},{5,197},{6,198},{7,199},{8... | collective-permute-start | bytes 393224 | tf_op jit(solution)/shard_map/ppermute | solution.py:43
  61.3 6.8 %collective-permute-start.19 = (bf16[1,128,256]{2,1,0:T(8,128)(2,1)S(1)}, bf16[1,128,256]{2,1,0:T(8,128)(2,1)S(1)}, u32[]{:S(2)}, u32[]{:S(2)}) collective-permute-start(bf16[1,128,256]{2,1,0:T(8,128)(2,1)S(1)} %slice.16), channel_id=1, source_target_pairs={{0,64},{1,65},{2,66},{3,67},{4,68},{5,69},{6,70},{7,71},{8,72},{9,... | collective-permute-start | bytes 196616 | tf_op jit(solution)/shard_map/ppermute | solution.py:43
  62.8 7.9 %collective-permute-start.18 = (bf16[2,256,256]{2,1,0:T(8,128)(2,1)S(1)}, bf16[2,256,256]{2,1,0:T(8,128)(2,1)S(1)}, u32[]{:S(2)}, u32[]{:S(2)}) collective-permute-start(bf16[2,256,256]{2,1,0:T(8,128)(2,1)S(1)} %constant_dynamic-update-slice_fusion.n1), channel_id=1, source_target_pairs={{0,48},{1,49},{2,50},{3,51},{4,52},{5,53},{6,54},{7,55},{8,56},{9,... | collective-permute-start | bytes 786440 | tf_op jit(solution)/shard_map/ppermute | solution.py:43
  63.3 10.1 %collective-permute-start.17 = (bf16[2,256,256]{2,1,0:T(8,128)(2,1)S(1)}, bf16[2,256,256]{2,1,0:T(8,128)(2,1)S(1)}, u32[]{:S(2)}, u32[]{:S(2)}) collective-permute-start(bf16[2,256,256]{2,1,0:T(8,128)(2,1)S(1)} %constant_dynamic-update-slice_fusion.n1), channel_id=1, source_target_pairs={{0,16},{1,17},{2,18},{3,19},{4,20},{5,21},{6,22},{7,23},{8,24},{9,... | collective-permute-start | bytes 786440 | tf_op jit(solution)/shard_map/ppermute | solution.py:43
  64.9 11.9 %collective-permute-start.13 = (bf16[1,256,256]{2,1,0:T(8,128)(2,1)S(1)}, bf16[1,256,256]{2,1,0:T(8,128)(2,1)S(1)}, u32[]{:S(2)}, u32[]{:S(2)}) collective-permute-start(bf16[1,256,256]{2,1,0:T(8,128)(2,1)S(1)} %bitcast.3), channel_id=1, source_target_pairs={{0,16},{1,17},{2,18},{3,19},{4,20},{5,21},{6,22},{7,23},{8,24},{9,... | collective-permute-start | bytes 393224 | tf_op jit(solution)/shard_map/ppermute | solution.py:43
  65.0 5.2 %collective-permute-start.20 = (bf16[1,128,256]{2,1,0:T(8,128)(2,1)S(1)}, bf16[1,128,256]{2,1,0:T(8,128)(2,1)S(1)}, u32[]{:S(2)}, u32[]{:S(2)}) collective-permute-start(bf16[1,128,256]{2,1,0:T(8,128)(2,1)S(1)} %slice.17), channel_id=1, source_target_pairs={{0,192},{1,193},{2,194},{3,195},{4,196},{5,197},{6,198},{7,199},{8... | collective-permute-start | bytes 196616 | tf_op jit(solution)/shard_map/ppermute | solution.py:43
  73.4 12.7 %collective-permute-start.23 = (bf16[2,256,256]{2,1,0:T(8,128)(2,1)S(1)}, bf16[2,256,256]{2,1,0:T(8,128)(2,1)S(1)}, u32[]{:S(2)}, u32[]{:S(2)}) collective-permute-start(bf16[2,256,256]{2,1,0:T(8,128)(2,1)S(1)} %get-tuple-element.29), channel_id=1, source_target_pairs={{0,48},{1,49},{2,50},{3,51},{4,52},{5,53},{6,54},{7,55},{8,56},{9,... | collective-permute-start | bytes 786440 | tf_op jit(solution)/shard_map/ppermute | solution.py:43
  73.5 12.6 %collective-permute-start.22 = (bf16[2,256,256]{2,1,0:T(8,128)(2,1)S(1)}, bf16[2,256,256]{2,1,0:T(8,128)(2,1)S(1)}, u32[]{:S(2)}, u32[]{:S(2)}) collective-permute-start(bf16[2,256,256]{2,1,0:T(8,128)(2,1)S(1)} %get-tuple-element.30), channel_id=1, source_target_pairs={{0,16},{1,17},{2,18},{3,19},{4,20},{5,21},{6,22},{7,23},{8,24},{9,... | collective-permute-start | bytes 786440 | tf_op jit(solution)/shard_map/ppermute | solution.py:43
  75.6 7.4 %collective-permute-start.14 = (bf16[1,256,256]{2,1,0:T(8,128)(2,1)S(1)}, bf16[1,256,256]{2,1,0:T(8,128)(2,1)S(1)}, u32[]{:S(2)}, u32[]{:S(2)}) collective-permute-start(bf16[1,256,256]{2,1,0:T(8,128)(2,1)S(1)} %bitcast.4), channel_id=1, source_target_pairs={{0,48},{1,49},{2,50},{3,51},{4,52},{5,53},{6,54},{7,55},{8,56},{9,... | collective-permute-start | bytes 393224 | tf_op jit(solution)/shard_map/ppermute | solution.py:43
  76.9 9.3 %collective-permute-start.21 = (bf16[1,256,256]{2,1,0:T(8,128)(2,1)S(1)}, bf16[1,256,256]{2,1,0:T(8,128)(2,1)S(1)}, u32[]{:S(2)}, u32[]{:S(2)}) collective-permute-start(bf16[1,256,256]{2,1,0:T(8,128)(2,1)S(1)} %collective-permute-done.13.l0), channel_id=1, source_target_pairs={{0,16},{1,17},{2,18},{3,19},{4,20},{5,21},{6,22},{7,23},{8,24},{9,... | collective-permute-start | bytes 393224 | tf_op jit(solution)/shard_map/ppermute | solution.py:43
  77.6 8.6 %collective-permute-start.24 = (bf16[1,256,256]{2,1,0:T(8,128)(2,1)S(1)}, bf16[1,256,256]{2,1,0:T(8,128)(2,1)S(1)}, u32[]{:S(2)}, u32[]{:S(2)}) collective-permute-start(bf16[1,256,256]{2,1,0:T(8,128)(2,1)S(1)} %constant_dynamic-update-slice_fusion.2.n2), channel_id=1, source_target_pairs={{0,32},{1,33},{2,34},{3,35},{4,36},{5,37},{6,38},{7,39},{8,40},{9,... | collective-permute-start | bytes 393224 | tf_op jit(solution)/shard_map/ppermute | solution.py:43

commit v4 on v3

--- a/solution.py
+++ b/solution.py
@@ -51,11 +51,11 @@
             scratch[c, pl.ds(a, rows, stride=16), :] = block[:, c * 128 : (c + 1) * 128]
 
 
-def put_first(scratch, out_ref):
+def put_first(scratch, out_ref, half):
     for k in range(12):
         for c in range(2):
             value = scratch[c, k * 128 : (k + 1) * 128].astype(jnp.bfloat16)
-            out_ref[k, 0, :, c * 128 : (c + 1) * 128] = value
+            out_ref[k, half, :, c * 128 : (c + 1) * 128] = value
 
 
 def prep_kernel(node_hbm, legs_hbm, first_ref, cols_ref, ops_ref, node_ref, leg_a, tiles, wide_tiles, scratch, sems):
@@ -90,7 +90,7 @@
     ops_ref[...] = ops
     fetch_node.wait()
     leg_c(node_ref, ops, scratch)
-    put_first(scratch, first_ref)
+    put_first(scratch, first_ref, 0)
 
 
 def prep(node, leg_ops):
@@ -103,11 +103,7 @@
         ],
         grid=(1,),
         in_specs=[pl.BlockSpec(memory_space=pltpu.HBM)] * 2,
-        out_specs=[
-            pl.BlockSpec((12, 1, 128, 256), lambda g: (0, 0, 0, 0)),
-            pl.BlockSpec((12, 512, 128), lambda g: (0, 0, 0)),
-            pl.BlockSpec((96, 256), lambda g: (0, 0)),
-        ],
+        out_specs=[pl.BlockSpec(memory_space=pltpu.VMEM)] * 3,
         scratch_shapes=[
             pltpu.VMEM((16, 256, 256), jnp.bfloat16),
             pltpu.VMEM((12, 256, 256), jnp.bfloat16),
@@ -125,7 +121,7 @@
 def sibling_kernel(node_ref, ops_ref, first_ref, out_ref, scratch):
     del first_ref
     leg_c(node_ref, ops_ref[...], scratch)
-    put_first(scratch, out_ref)
+    put_first(scratch, out_ref, 1)
 
 
 def add_sibling(node, ops, first):
@@ -133,12 +129,8 @@
         sibling_kernel,
         out_shape=jax.ShapeDtypeStruct((12, 2, 128, 256), jnp.bfloat16),
         grid=(1,),
-        in_specs=[
-            pl.BlockSpec((16, 256, 256), lambda g: (0, 0, 0)),
-            pl.BlockSpec((96, 256), lambda g: (0, 0)),
-            pl.BlockSpec(memory_space=pl.ANY),
-        ],
-        out_specs=pl.BlockSpec((12, 1, 128, 256), lambda g: (0, 1, 0, 0)),
+        in_specs=[pl.BlockSpec(memory_space=pltpu.VMEM)] * 3,
+        out_specs=pl.BlockSpec(memory_space=pltpu.VMEM),
         scratch_shapes=[pltpu.VMEM((2, 1536, 128), jnp.float32)],
         input_output_aliases={2: 0},
         compiler_params=grant(10),
@@ -241,7 +233,6 @@
 
 
 def main_of(table, first, leg_ops, cols):
-    whole3 = lambda g, s: (0, 0, 0)
     return pl.pallas_call(
         main_kernel,
         out_shape=[jax.ShapeDtypeStruct((8, 2048, 256), jnp.bfloat16), jax.ShapeDtypeStruct((64, 2048), jnp.bfloat16)]
@@ -250,9 +241,9 @@
             num_scalar_prefetch=1,
             grid=(1,),
             in_specs=[
-                pl.BlockSpec((12, 2, 128, 256), lambda g, s: (0, 0, 0, 0)),
+                pl.BlockSpec(memory_space=pltpu.VMEM),
                 pl.BlockSpec(memory_space=pltpu.HBM),
-                pl.BlockSpec((12, 512, 128), whole3),
+                pl.BlockSpec(memory_space=pltpu.VMEM),
             ],
             out_specs=[pl.BlockSpec(memory_space=pltpu.VMEM)] * 5,
             scratch_shapes=[

time: 89.3 us -> 89.1 us (level)
  starting transfers between devices: 36.1 us -> 38.2 us
  waiting for transfers between devices: 36.3 us -> 34.2 us
    ppermute x25, waiting for transfers between devices: 36.3 us -> 34.2 us  [send(): return lax.ppermute(value, ('wide', 'narrow'), pairs_of(move))]
    ppermute x25, starting transfers between devices: 36.1 us -> 38.2 us  [send(): return lax.ppermute(value, ('wide', 'narrow'), pairs_of(move))]
  transfers between devices with their start and end apart: 25 -> 25, of which waited for: 16 -> 15; matrix products, arithmetic and copies ran while one was open for 0% -> 0% of each run, Pallas kernels for 6% -> 6%
where the time goes in v4:
time: 89.1 us; the launch traced here: 88.6 us
  starting transfers between devices  38.2 us (43%)
  waiting for transfers between devices  34.2 us (38%)
  Pallas kernels  15.8 us (18%)
    ppermute x25, starting transfers between devices, send(): return lax.ppermute(value, ('wide', 'narrow'), pairs_of(move))  38.2 us
    ppermute x25, waiting for transfers between devices, send(): return lax.ppermute(value, ('wide', 'narrow'), pairs_of(move))  34.2 us
    pallas_call x1, Pallas kernels, main_of(): pl.pallas_call(main_kernel, out_shape=[jax.ShapeDtypeStruct((8, 2048, 256...  6.55 us
    pallas_call x1, Pallas kernels, prep(): pl.pallas_call(prep_kernel, out_shape=[jax.ShapeDtypeStruct((12, 2, 128,...  3.2 us
    pallas_call x1, Pallas kernels, last_of(): pl.pallas_call(functools.partial(last_kernel, tau), out_shape=jax.ShapeDt...  2.5 us
  transfers between devices with their start and end apart: 25, of which 15 were waited for; matrix products, arithmetic and copies ran while one was open for 0% of the time, Pallas kernels for 6%

profile of v4, /device:TPU:8, one launch (start us, length us, event | category | flops | bytes accessed | tf_op | source)
XLA Modules:
  0.0 88.6 jit_solution(15489514287463879423)
XLA Ops:
  0.7 3.1 %collective-permute-start.2 = (s32[16,128]{1,0:T(8,128)S(1)}, s32[16,128]{1,0:T(8,128)S(1)}, u32[]{:S(2)}, u32[]{:S(2)}) collective-permute-start(s32[16,128]{1,0:T(8,128)S(1)} %own_rows.1), channel_id=1, source_target_pairs={{0,32},{1,33},{2,34},{3,35},{4,36},{5,37},{6,38},{7,39},{8,40},{9,... | collective-permute-start | bytes 24584 | tf_op jit(solution)/shard_map/ppermute | solution.py:43
  3.8 1.1 %collective-permute-start.1 = (s32[16,128]{1,0:T(8,128)S(1)}, s32[16,128]{1,0:T(8,128)S(1)}, u32[]{:S(2)}, u32[]{:S(2)}) collective-permute-start(s32[16,128]{1,0:T(8,128)S(1)} %own_rows.1), channel_id=1, source_target_pairs={{0,48},{1,49},{2,50},{3,51},{4,52},{5,53},{6,54},{7,55},{8,56},{9,... | collective-permute-start | bytes 24584 | tf_op jit(solution)/shard_map/ppermute | solution.py:43
  6.0 1.5 %collective-permute-done.1 = s32[16,128]{1,0:T(8,128)S(1)} collective-permute-done((s32[16,128]{1,0:T(8,128)S(1)}, s32[16,128]{1,0:T(8,128)S(1)}, u32[]{:S(2)}, u32[]{:S(2)}) %collective-permute-start.1) | collective-permute-done | bytes 8224 | tf_op jit(solution)/shard_map/ppermute | solution.py:43
  7.5 2.4 %collective-permute-done = s32[16,128]{1,0:T(8,128)S(1)} collective-permute-done((s32[16,128]{1,0:T(8,128)S(1)}, s32[16,128]{1,0:T(8,128)S(1)}, u32[]{:S(2)}, u32[]{:S(2)}) %collective-permute-start) | collective-permute-done | bytes 8224 | tf_op jit(solution)/shard_map/ppermute | solution.py:43
  9.8 7.2 %collective-permute-start.5 = (s32[16,128]{1,0:T(8,128)S(1)}, s32[16,128]{1,0:T(8,128)S(1)}, u32[]{:S(2)}, u32[]{:S(2)}) collective-permute-start(s32[16,128]{1,0:T(8,128)S(1)} %add_add_fusion.1), channel_id=1, source_target_pairs={{0,128},{1,129},{2,130},{3,131},{4,132},{5,133},{6,134},{7,135},{8... | collective-permute-start | bytes 24584 | tf_op jit(solution)/shard_map/ppermute | solution.py:43
  17.0 2.9 %collective-permute-start.3 = (s32[16,128]{1,0:T(8,128)S(1)}, s32[16,128]{1,0:T(8,128)S(1)}, u32[]{:S(2)}, u32[]{:S(2)}) collective-permute-start(s32[16,128]{1,0:T(8,128)S(1)} %add_add_fusion.1), channel_id=1, source_target_pairs={{0,64},{1,65},{2,66},{3,67},{4,68},{5,69},{6,70},{7,71},{8,72},{9,... | collective-permute-start | bytes 24584 | tf_op jit(solution)/shard_map/ppermute | solution.py:43
  20.0 3.2 %prep.1 = (bf16[12,2,128,256]{3,2,1,0:T(8,128)(2,1)S(1)}, bf16[12,512,128]{2,1,0:T(8,128)(2,1)S(1)}, bf16[96,256]{1,0:T(8,128)(2,1)S(1)}) custom-call(bf16[16,256,256]{2,1,0:T(8,128)(2,1)} %node_ref.1, bf16[3,12,256,256]{3,2,1,0:T(8,128)(2,1)} %legs_hbm.3), custom_call_target="tpu_custom_call" | custom-call | flops 471859200 | bytes 6291456 | tf_op jit(solution)/shard_map/prep/pallas_call | solution.py:97
  23.2 1.0 %sibling.1.first_ref = bf16[12,2,128,256]{3,2,1,0:T(8,128)(2,1)S(1)} custom-call(bf16[16,256,256]{2,1,0:T(8,128)(2,1)S(1)} %collective-permute-done.6.node_ref, bf16[96,256]{1,0:T(8,128)(2,1)S(1)} %get-tuple-element.17.ops_ref, bf16[12,2,128,256]{3,2,1,0:T(8,128)(2,1)S(1)} %get-tuple-element.18.first_ref), custom_call_target="tpu_custom_call", output_to_operand_aliasing={{}: (2, {})} | custom-call | flops 201326592 | bytes 3145728 | tf_op jit(solution)/shard_map/sibling/pallas_call | solution.py:128
  24.2 6.6 %two_legs.1 = (bf16[8,2048,256]{2,1,0:T(8,128)(2,1)S(1)}, bf16[64,2048]{1,0:T(8,128)(2,1)S(1)}, bf16[8,64,256]{2,1,0:T(8,128)(2,1)S(1)}, bf16[8,64,256]{2,1,0:T(8,128)(2,1)S(1)}, bf16[8,64,256]{2,1,0:T(8,128)(2,1)S(1)}) custom-call(s32[16,128]{1,0:T(8,128)S(1)} %add_add_fusion.table, bf16[12,2,128,256]{3,2,1,0:T(8,128)(2,1)S(1)} %sibling.1.first_ref, ...), custom_call_target="tpu_custom_call" | custom-call | flops 4294967296 | bytes 8388608 | tf_op jit(solution)/shard_map/two_legs/pallas_call | solution.py:236
  30.8 1.7 %collective-permute-start.7 = (bf16[8,64,256]{2,1,0:T(8,128)(2,1)S(1)}, bf16[8,64,256]{2,1,0:T(8,128)(2,1)S(1)}, u32[]{:S(2)}, u32[]{:S(2)}) collective-permute-start(bf16[8,64,256]{2,1,0:T(8,128)(2,1)S(1)} %get-tuple-element.22), channel_id=1, source_target_pairs={{0,2},{1,3},{2,4},{3,5},{4,6},{5,7},{6,0},{7,1},{8,10},{9,11},{10,... | collective-permute-start | bytes 786440 | tf_op jit(solution)/shard_map/ppermute | solution.py:43
  32.5 1.0 %collective-permute-start.8 = (bf16[8,64,256]{2,1,0:T(8,128)(2,1)S(1)}, bf16[8,64,256]{2,1,0:T(8,128)(2,1)S(1)}, u32[]{:S(2)}, u32[]{:S(2)}) collective-permute-start(bf16[8,64,256]{2,1,0:T(8,128)(2,1)S(1)} %get-tuple-element.23), channel_id=1, source_target_pairs={{0,4},{1,5},{2,6},{3,7},{4,0},{5,1},{6,2},{7,3},{8,12},{9,13},{10,... | collective-permute-start | bytes 786440 | tf_op jit(solution)/shard_map/ppermute | solution.py:43
  33.5 2.4 %collective-permute-start.9 = (bf16[8,64,256]{2,1,0:T(8,128)(2,1)S(1)}, bf16[8,64,256]{2,1,0:T(8,128)(2,1)S(1)}, u32[]{:S(2)}, u32[]{:S(2)}) collective-permute-start(bf16[8,64,256]{2,1,0:T(8,128)(2,1)S(1)} %get-tuple-element.24), channel_id=1, source_target_pairs={{0,6},{1,7},{2,0},{3,1},{4,2},{5,3},{6,4},{7,5},{8,14},{9,15},{10,... | collective-permute-start | bytes 786440 | tf_op jit(solution)/shard_map/ppermute | solution.py:43
  35.8 1.6 %own_target.1.keep_ref = f32[8,64,256]{2,1,0:T(8,128)S(1)} custom-call(bf16[8,2048,256]{2,1,0:T(8,128)(2,1)S(1)} %get-tuple-element.20.second, bf16[64,2048]{1,0:T(8,128)(2,1)S(1)} %get-tuple-element.21.a_own), custom_call_target="tpu_custom_call" | custom-call | flops 536870912 | bytes 9437184 | tf_op jit(solution)/shard_map/own_target/pallas_call | solution.py:224
  37.4 2.5 %collective-permute-done.7.r1_ref = bf16[8,64,256]{2,1,0:T(8,128)(2,1)S(1)} collective-permute-done((bf16[8,64,256]{2,1,0:T(8,128)(2,1)S(1)}, bf16[8,64,256]{2,1,0:T(8,128)(2,1)S(1)}, u32[]{:S(2)}, u32[]{:S(2)}) %collective-permute-start.7) | collective-permute-done | bytes 262176 | tf_op jit(solution)/shard_map/ppermute | solution.py:43
  39.9 2.9 %collective-permute-done.8.r2_ref = bf16[8,64,256]{2,1,0:T(8,128)(2,1)S(1)} collective-permute-done((bf16[8,64,256]{2,1,0:T(8,128)(2,1)S(1)}, bf16[8,64,256]{2,1,0:T(8,128)(2,1)S(1)}, u32[]{:S(2)}, u32[]{:S(2)}) %collective-permute-start.8) | collective-permute-done | bytes 262176 | tf_op jit(solution)/shard_map/ppermute | solution.py:43
  42.7 2.3 %collective-permute-done.9.r3_ref = bf16[8,64,256]{2,1,0:T(8,128)(2,1)S(1)} collective-permute-done((bf16[8,64,256]{2,1,0:T(8,128)(2,1)S(1)}, bf16[8,64,256]{2,1,0:T(8,128)(2,1)S(1)}, u32[]{:S(2)}, u32[]{:S(2)}) %collective-permute-start.9) | collective-permute-done | bytes 262176 | tf_op jit(solution)/shard_map/ppermute | solution.py:43
  45.2 1.1 %collective-permute-start.11 = (bf16[8,16,256]{2,1,0:T(8,128)(2,1)S(1)}, bf16[8,16,256]{2,1,0:T(8,128)(2,1)S(1)}, u32[]{:S(2)}, u32[]{:S(2)}) collective-permute-start(bf16[8,16,256]{2,1,0:T(8,128)(2,1)S(1)} %get-tuple-element.27), channel_id=1, source_target_pairs={{0,8},{1,9},{2,10},{3,11},{4,12},{5,13},{6,14},{7,15},{8,0},{9,1},... | collective-permute-start | bytes 196616 | tf_op jit(solution)/shard_map/ppermute | solution.py:43
  47.0 3.0 %collective-permute-done.11.r10_ref = bf16[8,16,256]{2,1,0:T(8,128)(2,1)S(1)} collective-permute-done((bf16[8,16,256]{2,1,0:T(8,128)(2,1)S(1)}, bf16[8,16,256]{2,1,0:T(8,128)(2,1)S(1)}, u32[]{:S(2)}, u32[]{:S(2)}) %collective-permute-start.11) | collective-permute-done | bytes 65568 | tf_op jit(solution)/shard_map/ppermute | solution.py:43
  50.8 2.8 %collective-permute-start.15 = (bf16[1,256,256]{2,1,0:T(8,128)(2,1)S(1)}, bf16[1,256,256]{2,1,0:T(8,128)(2,1)S(1)}, u32[]{:S(2)}, u32[]{:S(2)}) collective-permute-start(bf16[1,256,256]{2,1,0:T(8,128)(2,1)S(1)} %bitcast.1), channel_id=1, source_target_pairs={{0,64},{1,65},{2,66},{3,67},{4,68},{5,69},{6,70},{7,71},{8,72},{9,... | collective-permute-start | bytes 393224 | tf_op jit(solution)/shard_map/ppermute | solution.py:43
  53.6 1.5 %collective-permute-start.16 = (bf16[1,256,256]{2,1,0:T(8,128)(2,1)S(1)}, bf16[1,256,256]{2,1,0:T(8,128)(2,1)S(1)}, u32[]{:S(2)}, u32[]{:S(2)}) collective-permute-start(bf16[1,256,256]{2,1,0:T(8,128)(2,1)S(1)} %bitcast.2), channel_id=1, source_target_pairs={{0,192},{1,193},{2,194},{3,195},{4,196},{5,197},{6,198},{7,199},{8... | collective-permute-start | bytes 393224 | tf_op jit(solution)/shard_map/ppermute | solution.py:43
  55.0 3.7 %collective-permute-done.15 = bf16[1,256,256]{2,1,0:T(8,128)(2,1)S(1)} collective-permute-done((bf16[1,256,256]{2,1,0:T(8,128)(2,1)S(1)}, bf16[1,256,256]{2,1,0:T(8,128)(2,1)S(1)}, u32[]{:S(2)}, u32[]{:S(2)}) %collective-permute-start.15) | collective-permute-done | bytes 131104 | tf_op jit(solution)/shard_map/ppermute | solution.py:43
  58.7 2.0 %collective-permute-start.19 = (bf16[1,128,256]{2,1,0:T(8,128)(2,1)S(1)}, bf16[1,128,256]{2,1,0:T(8,128)(2,1)S(1)}, u32[]{:S(2)}, u32[]{:S(2)}) collective-permute-start(bf16[1,128,256]{2,1,0:T(8,128)(2,1)S(1)} %slice.16), channel_id=1, source_target_pairs={{0,64},{1,65},{2,66},{3,67},{4,68},{5,69},{6,70},{7,71},{8,72},{9,... | collective-permute-start | bytes 196616 | tf_op jit(solution)/shard_map/ppermute | solution.py:43
  60.8 1.8 %collective-permute-done.16 = bf16[1,256,256]{2,1,0:T(8,128)(2,1)S(1)} collective-permute-done((bf16[1,256,256]{2,1,0:T(8,128)(2,1)S(1)}, bf16[1,256,256]{2,1,0:T(8,128)(2,1)S(1)}, u32[]{:S(2)}, u32[]{:S(2)}) %collective-permute-start.16) | collective-permute-done | bytes 131104 | tf_op jit(solution)/shard_map/ppermute | solution.py:43
  63.1 1.7 %collective-permute-start.17 = (bf16[2,256,256]{2,1,0:T(8,128)(2,1)S(1)}, bf16[2,256,256]{2,1,0:T(8,128)(2,1)S(1)}, u32[]{:S(2)}, u32[]{:S(2)}) collective-permute-start(bf16[2,256,256]{2,1,0:T(8,128)(2,1)S(1)} %constant_dynamic-update-slice_fusion.n1), channel_id=1, source_target_pairs={{0,16},{1,17},{2,18},{3,19},{4,20},{5,21},{6,22},{7,23},{8,24},{9,... | collective-permute-start | bytes 786440 | tf_op jit(solution)/shard_map/ppermute | solution.py:43
  64.8 2.7 %collective-permute-start.20 = (bf16[1,128,256]{2,1,0:T(8,128)(2,1)S(1)}, bf16[1,128,256]{2,1,0:T(8,128)(2,1)S(1)}, u32[]{:S(2)}, u32[]{:S(2)}) collective-permute-start(bf16[1,128,256]{2,1,0:T(8,128)(2,1)S(1)} %slice.17), channel_id=1, source_target_pairs={{0,192},{1,193},{2,194},{3,195},{4,196},{5,197},{6,198},{7,199},{8... | collective-permute-start | bytes 196616 | tf_op jit(solution)/shard_map/ppermute | solution.py:43
  67.5 2.5 %collective-permute-done.20 = bf16[1,128,256]{2,1,0:T(8,128)(2,1)S(1)} collective-permute-done((bf16[1,128,256]{2,1,0:T(8,128)(2,1)S(1)}, bf16[1,128,256]{2,1,0:T(8,128)(2,1)S(1)}, u32[]{:S(2)}, u32[]{:S(2)}) %collective-permute-start.20) | collective-permute-done | bytes 65568 | tf_op jit(solution)/shard_map/ppermute | solution.py:43
  70.5 2.7 %collective-permute-done.17.l1 = bf16[2,256,256]{2,1,0:T(8,128)(2,1)S(1)} collective-permute-done((bf16[2,256,256]{2,1,0:T(8,128)(2,1)S(1)}, bf16[2,256,256]{2,1,0:T(8,128)(2,1)S(1)}, u32[]{:S(2)}, u32[]{:S(2)}) %collective-permute-start.17) | collective-permute-done | bytes 262176 | tf_op jit(solution)/shard_map/ppermute | solution.py:43
  73.3 2.0 %collective-permute-start.22 = (bf16[2,256,256]{2,1,0:T(8,128)(2,1)S(1)}, bf16[2,256,256]{2,1,0:T(8,128)(2,1)S(1)}, u32[]{:S(2)}, u32[]{:S(2)}) collective-permute-start(bf16[2,256,256]{2,1,0:T(8,128)(2,1)S(1)} %get-tuple-element.30), channel_id=1, source_target_pairs={{0,16},{1,17},{2,18},{3,19},{4,20},{5,21},{6,22},{7,23},{8,24},{9,... | collective-permute-start | bytes 786440 | tf_op jit(solution)/shard_map/ppermute | solution.py:43
  75.4 1.3 %collective-permute-start.14 = (bf16[1,256,256]{2,1,0:T(8,128)(2,1)S(1)}, bf16[1,256,256]{2,1,0:T(8,128)(2,1)S(1)}, u32[]{:S(2)}, u32[]{:S(2)}) collective-permute-start(bf16[1,256,256]{2,1,0:T(8,128)(2,1)S(1)} %bitcast.4), channel_id=1, source_target_pairs={{0,48},{1,49},{2,50},{3,51},{4,52},{5,53},{6,54},{7,55},{8,56},{9,... | collective-permute-start | bytes 393224 | tf_op jit(solution)/shard_map/ppermute | solution.py:43
  78.2 4.6 %collective-permute-done.14.r0 = bf16[1,256,256]{2,1,0:T(8,128)(2,1)S(1)} collective-permute-done((bf16[1,256,256]{2,1,0:T(8,128)(2,1)S(1)}, bf16[1,256,256]{2,1,0:T(8,128)(2,1)S(1)}, u32[]{:S(2)}, u32[]{:S(2)}) %collective-permute-start.14) | collective-permute-done | bytes 131104 | tf_op jit(solution)/shard_map/ppermute | solution.py:43
  82.8 3.2 %collective-permute-done.21.f0 = bf16[1,256,256]{2,1,0:T(8,128)(2,1)S(1)} collective-permute-done((bf16[1,256,256]{2,1,0:T(8,128)(2,1)S(1)}, bf16[1,256,256]{2,1,0:T(8,128)(2,1)S(1)}, u32[]{:S(2)}, u32[]{:S(2)}) %collective-permute-start.21) | collective-permute-done | bytes 131104 | tf_op jit(solution)/shard_map/ppermute | solution.py:43
  86.0 2.5 %update.1 = f32[16,256,256]{2,1,0:T(8,128)} custom-call(bf16[1,256,256]{2,1,0:T(8,128)(2,1)S(1)} %bitcast.5, bf16[1,256,256]{2,1,0:T(8,128)(2,1)S(1)} %collective-permute-done.13.l0, bf16[1,256,256]{2,1,0:T(8,128)(2,1)S(1)} %collective-permute-done.14.r0, bf16[2,256,256]{2,1,0:T(8,128)(2,1)S(1)} %constant_dynamic-update-slice_fusion.n1, ...), custom_call_target="tpu_custom_call" | custom-call | tf_op jit(solution)/shard_map/update/pallas_call | solution.py:336
  (41 shorter events, 6.1 us)
Async XLA Ops:
  0.0 23.2 %collective-permute-start.6 = (bf16[16,256,256]{2,1,0:T(8,128)(2,1)}, bf16[16,256,256]{2,1,0:T(8,128)(2,1)S(1)}, u32[]{:S(2)}, u32[]{:S(2)}) collective-permute-start(bf16[16,256,256]{2,1,0:T(8,128)(2,1)} %node_ref.1), channel_id=1, source_target_pairs={{0,1},{1,0},{2,3},{3,2},{4,5},{5,4},{6,7},{7,6},{8,9},{9,8},{10,11... | collective-permute-start | bytes 6291464 | tf_op jit(solution)/shard_map/ppermute | solution.py:43
  0.7 5.2 %collective-permute-start.2 = (s32[16,128]{1,0:T(8,128)S(1)}, s32[16,128]{1,0:T(8,128)S(1)}, u32[]{:S(2)}, u32[]{:S(2)}) collective-permute-start(s32[16,128]{1,0:T(8,128)S(1)} %own_rows.1), channel_id=1, source_target_pairs={{0,32},{1,33},{2,34},{3,35},{4,36},{5,37},{6,38},{7,39},{8,40},{9,... | collective-permute-start | bytes 24584 | tf_op jit(solution)/shard_map/ppermute | solution.py:43
  3.8 3.7 %collective-permute-start.1 = (s32[16,128]{1,0:T(8,128)S(1)}, s32[16,128]{1,0:T(8,128)S(1)}, u32[]{:S(2)}, u32[]{:S(2)}) collective-permute-start(s32[16,128]{1,0:T(8,128)S(1)} %own_rows.1), channel_id=1, source_target_pairs={{0,48},{1,49},{2,50},{3,51},{4,52},{5,53},{6,54},{7,55},{8,56},{9,... | collective-permute-start | bytes 24584 | tf_op jit(solution)/shard_map/ppermute | solution.py:43
  5.0 4.9 %collective-permute-start = (s32[16,128]{1,0:T(8,128)S(1)}, s32[16,128]{1,0:T(8,128)S(1)}, u32[]{:S(2)}, u32[]{:S(2)}) collective-permute-start(s32[16,128]{1,0:T(8,128)S(1)} %own_rows.1), channel_id=1, source_target_pairs={{0,16},{1,17},{2,18},{3,19},{4,20},{5,21},{6,22},{7,23},{8,24},{9,... | collective-permute-start | bytes 24584 | tf_op jit(solution)/shard_map/ppermute | solution.py:43
  9.8 13.3 %collective-permute-start.5 = (s32[16,128]{1,0:T(8,128)S(1)}, s32[16,128]{1,0:T(8,128)S(1)}, u32[]{:S(2)}, u32[]{:S(2)}) collective-permute-start(s32[16,128]{1,0:T(8,128)S(1)} %add_add_fusion.1), channel_id=1, source_target_pairs={{0,128},{1,129},{2,130},{3,131},{4,132},{5,133},{6,134},{7,135},{8... | collective-permute-start | bytes 24584 | tf_op jit(solution)/shard_map/ppermute | solution.py:43
  17.0 6.1 %collective-permute-start.4 = (s32[16,128]{1,0:T(8,128)S(1)}, s32[16,128]{1,0:T(8,128)S(1)}, u32[]{:S(2)}, u32[]{:S(2)}) collective-permute-start(s32[16,128]{1,0:T(8,128)S(1)} %add_add_fusion.1), channel_id=1, source_target_pairs={{0,192},{1,193},{2,194},{3,195},{4,196},{5,197},{6,198},{7,199},{8... | collective-permute-start | bytes 24584 | tf_op jit(solution)/shard_map/ppermute | solution.py:43
  17.0 6.1 %collective-permute-start.3 = (s32[16,128]{1,0:T(8,128)S(1)}, s32[16,128]{1,0:T(8,128)S(1)}, u32[]{:S(2)}, u32[]{:S(2)}) collective-permute-start(s32[16,128]{1,0:T(8,128)S(1)} %add_add_fusion.1), channel_id=1, source_target_pairs={{0,64},{1,65},{2,66},{3,67},{4,68},{5,69},{6,70},{7,71},{8,72},{9,... | collective-permute-start | bytes 24584 | tf_op jit(solution)/shard_map/ppermute | solution.py:43
  30.8 9.1 %collective-permute-start.7 = (bf16[8,64,256]{2,1,0:T(8,128)(2,1)S(1)}, bf16[8,64,256]{2,1,0:T(8,128)(2,1)S(1)}, u32[]{:S(2)}, u32[]{:S(2)}) collective-permute-start(bf16[8,64,256]{2,1,0:T(8,128)(2,1)S(1)} %get-tuple-element.22), channel_id=1, source_target_pairs={{0,2},{1,3},{2,4},{3,5},{4,6},{5,7},{6,0},{7,1},{8,10},{9,11},{10,... | collective-permute-start | bytes 786440 | tf_op jit(solution)/shard_map/ppermute | solution.py:43
  32.5 10.3 %collective-permute-start.8 = (bf16[8,64,256]{2,1,0:T(8,128)(2,1)S(1)}, bf16[8,64,256]{2,1,0:T(8,128)(2,1)S(1)}, u32[]{:S(2)}, u32[]{:S(2)}) collective-permute-start(bf16[8,64,256]{2,1,0:T(8,128)(2,1)S(1)} %get-tuple-element.23), channel_id=1, source_target_pairs={{0,4},{1,5},{2,6},{3,7},{4,0},{5,1},{6,2},{7,3},{8,12},{9,13},{10,... | collective-permute-start | bytes 786440 | tf_op jit(solution)/shard_map/ppermute | solution.py:43
  33.5 11.5 %collective-permute-start.9 = (bf16[8,64,256]{2,1,0:T(8,128)(2,1)S(1)}, bf16[8,64,256]{2,1,0:T(8,128)(2,1)S(1)}, u32[]{:S(2)}, u32[]{:S(2)}) collective-permute-start(bf16[8,64,256]{2,1,0:T(8,128)(2,1)S(1)} %get-tuple-element.24), channel_id=1, source_target_pairs={{0,6},{1,7},{2,0},{3,1},{4,2},{5,3},{6,4},{7,5},{8,14},{9,15},{10,... | collective-permute-start | bytes 786440 | tf_op jit(solution)/shard_map/ppermute | solution.py:43
  37.4 48.6 %copy-start = (bf16[16,256,256]{2,1,0:T(8,128)(2,1)S(1)}, bf16[16,256,256]{2,1,0:T(8,128)(2,1)}, u32[]{:S(2)}) copy-start(bf16[16,256,256]{2,1,0:T(8,128)(2,1)} %node_ref.1) | copy-start | bytes 6291460
  37.4 48.6 %copy-start.1 = (bf16[16,256,256]{2,1,0:T(8,128)(2,1)S(1)}, bf16[16,256,256]{2,1,0:T(8,128)(2,1)}, u32[]{:S(2)}) copy-start(bf16[16,256,256]{2,1,0:T(8,128)(2,1)} %side_ref.1) | copy-start | bytes 6291460
  45.1 2.0 %collective-permute-start.10 = (bf16[8,16,256]{2,1,0:T(8,128)(2,1)S(1)}, bf16[8,16,256]{2,1,0:T(8,128)(2,1)S(1)}, u32[]{:S(2)}, u32[]{:S(2)}) collective-permute-start(bf16[8,16,256]{2,1,0:T(8,128)(2,1)S(1)} %get-tuple-element.26), channel_id=1, source_target_pairs={{0,1},{1,0},{2,3},{3,2},{4,5},{5,4},{6,7},{7,6},{8,9},{9,8},{10,11... | collective-permute-start | bytes 196616 | tf_op jit(solution)/shard_map/ppermute | solution.py:43
  45.2 4.9 %collective-permute-start.11 = (bf16[8,16,256]{2,1,0:T(8,128)(2,1)S(1)}, bf16[8,16,256]{2,1,0:T(8,128)(2,1)S(1)}, u32[]{:S(2)}, u32[]{:S(2)}) collective-permute-start(bf16[8,16,256]{2,1,0:T(8,128)(2,1)S(1)} %get-tuple-element.27), channel_id=1, source_target_pairs={{0,8},{1,9},{2,10},{3,11},{4,12},{5,13},{6,14},{7,15},{8,0},{9,1},... | collective-permute-start | bytes 196616 | tf_op jit(solution)/shard_map/ppermute | solution.py:43
  46.3 4.4 %collective-permute-start.12 = (bf16[8,16,256]{2,1,0:T(8,128)(2,1)S(1)}, bf16[8,16,256]{2,1,0:T(8,128)(2,1)S(1)}, u32[]{:S(2)}, u32[]{:S(2)}) collective-permute-start(bf16[8,16,256]{2,1,0:T(8,128)(2,1)S(1)} %get-tuple-element.28), channel_id=1, source_target_pairs={{0,9},{1,8},{2,11},{3,10},{4,13},{5,12},{6,15},{7,14},{8,1},{9,0},... | collective-permute-start | bytes 196616 | tf_op jit(solution)/shard_map/ppermute | solution.py:43
  50.8 7.9 %collective-permute-start.15 = (bf16[1,256,256]{2,1,0:T(8,128)(2,1)S(1)}, bf16[1,256,256]{2,1,0:T(8,128)(2,1)S(1)}, u32[]{:S(2)}, u32[]{:S(2)}) collective-permute-start(bf16[1,256,256]{2,1,0:T(8,128)(2,1)S(1)} %bitcast.1), channel_id=1, source_target_pairs={{0,64},{1,65},{2,66},{3,67},{4,68},{5,69},{6,70},{7,71},{8,72},{9,... | collective-permute-start | bytes 393224 | tf_op jit(solution)/shard_map/ppermute | solution.py:43
  53.6 9.1 %collective-permute-start.16 = (bf16[1,256,256]{2,1,0:T(8,128)(2,1)S(1)}, bf16[1,256,256]{2,1,0:T(8,128)(2,1)S(1)}, u32[]{:S(2)}, u32[]{:S(2)}) collective-permute-start(bf16[1,256,256]{2,1,0:T(8,128)(2,1)S(1)} %bitcast.2), channel_id=1, source_target_pairs={{0,192},{1,193},{2,194},{3,195},{4,196},{5,197},{6,198},{7,199},{8... | collective-permute-start | bytes 393224 | tf_op jit(solution)/shard_map/ppermute | solution.py:43
  58.7 8.7 %collective-permute-start.19 = (bf16[1,128,256]{2,1,0:T(8,128)(2,1)S(1)}, bf16[1,128,256]{2,1,0:T(8,128)(2,1)S(1)}, u32[]{:S(2)}, u32[]{:S(2)}) collective-permute-start(bf16[1,128,256]{2,1,0:T(8,128)(2,1)S(1)} %slice.16), channel_id=1, source_target_pairs={{0,64},{1,65},{2,66},{3,67},{4,68},{5,69},{6,70},{7,71},{8,72},{9,... | collective-permute-start | bytes 196616 | tf_op jit(solution)/shard_map/ppermute | solution.py:43
  62.6 7.8 %collective-permute-start.18 = (bf16[2,256,256]{2,1,0:T(8,128)(2,1)S(1)}, bf16[2,256,256]{2,1,0:T(8,128)(2,1)S(1)}, u32[]{:S(2)}, u32[]{:S(2)}) collective-permute-start(bf16[2,256,256]{2,1,0:T(8,128)(2,1)S(1)} %constant_dynamic-update-slice_fusion.n1), channel_id=1, source_target_pairs={{0,48},{1,49},{2,50},{3,51},{4,52},{5,53},{6,54},{7,55},{8,56},{9,... | collective-permute-start | bytes 786440 | tf_op jit(solution)/shard_map/ppermute | solution.py:43
  63.1 10.1 %collective-permute-start.17 = (bf16[2,256,256]{2,1,0:T(8,128)(2,1)S(1)}, bf16[2,256,256]{2,1,0:T(8,128)(2,1)S(1)}, u32[]{:S(2)}, u32[]{:S(2)}) collective-permute-start(bf16[2,256,256]{2,1,0:T(8,128)(2,1)S(1)} %constant_dynamic-update-slice_fusion.n1), channel_id=1, source_target_pairs={{0,16},{1,17},{2,18},{3,19},{4,20},{5,21},{6,22},{7,23},{8,24},{9,... | collective-permute-start | bytes 786440 | tf_op jit(solution)/shard_map/ppermute | solution.py:43
  64.7 11.9 %collective-permute-start.13 = (bf16[1,256,256]{2,1,0:T(8,128)(2,1)S(1)}, bf16[1,256,256]{2,1,0:T(8,128)(2,1)S(1)}, u32[]{:S(2)}, u32[]{:S(2)}) collective-permute-start(bf16[1,256,256]{2,1,0:T(8,128)(2,1)S(1)} %bitcast.3), channel_id=1, source_target_pairs={{0,16},{1,17},{2,18},{3,19},{4,20},{5,21},{6,22},{7,23},{8,24},{9,... | collective-permute-start | bytes 393224 | tf_op jit(solution)/shard_map/ppermute | solution.py:43
  64.8 5.2 %collective-permute-start.20 = (bf16[1,128,256]{2,1,0:T(8,128)(2,1)S(1)}, bf16[1,128,256]{2,1,0:T(8,128)(2,1)S(1)}, u32[]{:S(2)}, u32[]{:S(2)}) collective-permute-start(bf16[1,128,256]{2,1,0:T(8,128)(2,1)S(1)} %slice.17), channel_id=1, source_target_pairs={{0,192},{1,193},{2,194},{3,195},{4,196},{5,197},{6,198},{7,199},{8... | collective-permute-start | bytes 196616 | tf_op jit(solution)/shard_map/ppermute | solution.py:43
  73.2 12.7 %collective-permute-start.23 = (bf16[2,256,256]{2,1,0:T(8,128)(2,1)S(1)}, bf16[2,256,256]{2,1,0:T(8,128)(2,1)S(1)}, u32[]{:S(2)}, u32[]{:S(2)}) collective-permute-start(bf16[2,256,256]{2,1,0:T(8,128)(2,1)S(1)} %get-tuple-element.29), channel_id=1, source_target_pairs={{0,48},{1,49},{2,50},{3,51},{4,52},{5,53},{6,54},{7,55},{8,56},{9,... | collective-permute-start | bytes 786440 | tf_op jit(solution)/shard_map/ppermute | solution.py:43
  73.3 12.6 %collective-permute-start.22 = (bf16[2,256,256]{2,1,0:T(8,128)(2,1)S(1)}, bf16[2,256,256]{2,1,0:T(8,128)(2,1)S(1)}, u32[]{:S(2)}, u32[]{:S(2)}) collective-permute-start(bf16[2,256,256]{2,1,0:T(8,128)(2,1)S(1)} %get-tuple-element.30), channel_id=1, source_target_pairs={{0,16},{1,17},{2,18},{3,19},{4,20},{5,21},{6,22},{7,23},{8,24},{9,... | collective-permute-start | bytes 786440 | tf_op jit(solution)/shard_map/ppermute | solution.py:43
  75.4 7.4 %collective-permute-start.14 = (bf16[1,256,256]{2,1,0:T(8,128)(2,1)S(1)}, bf16[1,256,256]{2,1,0:T(8,128)(2,1)S(1)}, u32[]{:S(2)}, u32[]{:S(2)}) collective-permute-start(bf16[1,256,256]{2,1,0:T(8,128)(2,1)S(1)} %bitcast.4), channel_id=1, source_target_pairs={{0,48},{1,49},{2,50},{3,51},{4,52},{5,53},{6,54},{7,55},{8,56},{9,... | collective-permute-start | bytes 393224 | tf_op jit(solution)/shard_map/ppermute | solution.py:43
  76.7 9.3 %collective-permute-start.21 = (bf16[1,256,256]{2,1,0:T(8,128)(2,1)S(1)}, bf16[1,256,256]{2,1,0:T(8,128)(2,1)S(1)}, u32[]{:S(2)}, u32[]{:S(2)}) collective-permute-start(bf16[1,256,256]{2,1,0:T(8,128)(2,1)S(1)} %collective-permute-done.13.l0), channel_id=1, source_target_pairs={{0,16},{1,17},{2,18},{3,19},{4,20},{5,21},{6,22},{7,23},{8,24},{9,... | collective-permute-start | bytes 393224 | tf_op jit(solution)/shard_map/ppermute | solution.py:43
  77.4 8.6 %collective-permute-start.24 = (bf16[1,256,256]{2,1,0:T(8,128)(2,1)S(1)}, bf16[1,256,256]{2,1,0:T(8,128)(2,1)S(1)}, u32[]{:S(2)}, u32[]{:S(2)}) collective-permute-start(bf16[1,256,256]{2,1,0:T(8,128)(2,1)S(1)} %constant_dynamic-update-slice_fusion.2.n2), channel_id=1, source_target_pairs={{0,32},{1,33},{2,34},{3,35},{4,36},{5,37},{6,38},{7,39},{8,40},{9,... | collective-permute-start | bytes 393224 | tf_op jit(solution)/shard_map/ppermute | solution.py:43
